TPU v7x, 32 devices: a whole 2x2x4 slice. The times are simulated.
32 devices in a mesh: dp: 8 (over y, x, core), fsdp: 4 (over z).
Axes of the slice: x: 2, y: 2, z: 4, core: 2. Of those that a mesh axis runs over, the one named last changes fastest.
Arguments:
- rows_in: bfloat16 [256, 32, 1024], P(None, ('dp', 'fsdp')), may hold values from -6 to 6
- cotangent: bfloat16 [256, 32, 1024], P(None, ('dp', 'fsdp')), may hold values from -6 to 6
- lengths: int32 [64], replicated, may hold values from 65 to 191, as said below
- deal_order: int32 [64], replicated, may hold values from 0 to 63, as said below
- w_qkv: bfloat16 [1024, 3072], P(('dp', 'fsdp')), may hold values from -0.25 to 0.25
- b_query: bfloat16 [1024], P(('dp', 'fsdp')), may hold values from -3 to 3
- b_value: bfloat16 [1024], P(('dp', 'fsdp')), may hold values from -3 to 3
- w_out: bfloat16 [1024, 1024], P(('dp', 'fsdp')), may hold values from -0.5 to 0.5
- b_out: bfloat16 [1024], P(('dp', 'fsdp')), may hold values from -3 to 3
- gain_one: bfloat16 [1024], P(('dp', 'fsdp')), may hold values from 0.5 to 1.5
- shift_one: bfloat16 [1024], P(('dp', 'fsdp')), may hold values from -2 to 2
- w_up: bfloat16 [1024, 4096], P(('dp', 'fsdp')), may hold values from -0.1875 to 0.1875
- b_up: bfloat16 [4096], P(('dp', 'fsdp')), may hold values from -3 to 3
- w_down: bfloat16 [4096, 1024], P(('dp', 'fsdp')), may hold values from -0.125 to 0.125
- b_down: bfloat16 [1024], P(('dp', 'fsdp')), may hold values from -3 to 3
- gain_two: bfloat16 [1024], P(('dp', 'fsdp')), may hold values from 0.5 to 1.5
- shift_two: bfloat16 [1024], P(('dp', 'fsdp')), may hold values from -2 to 2
Outputs:
- rows_out: bfloat16 [256, 32, 1024], P(None, ('dp', 'fsdp'))
- grad_rows: bfloat16 [256, 32, 1024], P(None, ('dp', 'fsdp'))
- grad_w_qkv: float32 [1024, 3072], P(('dp', 'fsdp'))
- grad_b_query: float32 [1024], P(('dp', 'fsdp'))
- grad_b_value: float32 [1024], P(('dp', 'fsdp'))
- grad_w_out: float32 [1024, 1024], P(('dp', 'fsdp'))
- grad_b_out: float32 [1024], P(('dp', 'fsdp'))
- grad_gain_one: float32 [1024], P(('dp', 'fsdp'))
- grad_shift_one: float32 [1024], P(('dp', 'fsdp'))
- grad_w_up: float32 [1024, 4096], P(('dp', 'fsdp'))
- grad_b_up: float32 [4096], P(('dp', 'fsdp'))
- grad_w_down: float32 [4096, 1024], P(('dp', 'fsdp'))
- grad_b_down: float32 [1024], P(('dp', 'fsdp'))
- grad_gain_two: float32 [1024], P(('dp', 'fsdp'))
- grad_shift_two: float32 [1024], P(('dp', 'fsdp'))
Inputs may be any that keep to these rules, and one draw needn't show every extreme that they name: `lengths`: they sum to 8192; sequences deal_order[2 i] and deal_order[2 i + 1] hold 256 tokens together for every i, so at most 9 rows of one device belong to the two sequences of another. `deal_order`: A permutation of the sequences.
All inputs are finite; a program needn't handle non-finite values.
Results may differ from a plain program's by a relative error of at most 0.014.
Values may be sent and summed in bfloat16 or wider, within the bound.
No kernel may reach another device: no remote copies, remote signals or barrier semaphores. Data moves between devices by JAX's collectives and lax.ppermute only.
A program may use at most 192 MiB of HBM per device.

v0:
```python
import jax
import jax.numpy as jnp
from jax import lax
from jax.experimental import pallas as pl
from jax.experimental.pallas import tpu as pltpu
from jax.sharding import PartitionSpec as P

HEADS = 16
HEAD_DIM = 64
EPSILON = 1e-05
AXES = ("dp", "fsdp")
BF16 = jnp.bfloat16
F32 = jnp.float32


class Grid:
    def __init__(self, n_dp, n_z):
        self.n_dp, self.n_z = n_dp, n_z
        side = 1
        while side * side * 2 < n_dp:
            side *= 2
        self.nx, self.ny = side, n_dp // (2 * side)
        self.x_masks = [2 * k for k in range(1, self.nx)]
        self.y_masks = [2 * side * k for k in range(1, self.ny)]
        self.z_masks = list(range(1, n_z))
        self.square = self.nx == self.ny == 2 and n_z == 4

    def bind(self):
        self.my_dp = lax.axis_index("dp").astype(jnp.int32)
        self.my_z = lax.axis_index("fsdp").astype(jnp.int32)
        self.me = lax.axis_index(AXES).astype(jnp.int32)

    def over_dp(self, value, mask):
        return lax.ppermute(value, "dp", [(i, i ^ mask) for i in range(self.n_dp)])

    def crossed(self, value, even_mask, odd_mask):
        pairs = [(i, i ^ (odd_mask if i % 2 else even_mask)) for i in range(self.n_dp)]
        return lax.ppermute(value, "dp", pairs)

    def over_z(self, value, mask):
        return lax.ppermute(value, "fsdp", [(i, i ^ mask) for i in range(self.n_z)])


class Clock:
    def __init__(self):
        self.last = ()

    def gate(self, *values):
        held = lax.optimization_barrier(tuple(values) + self.last)[: len(values)]
        return held if len(values) > 1 else held[0]

    def tick(self, *values):
        self.last = values


class Lines:
    def __init__(self, grid, clock, shards):
        self.grid, self.clock = grid, clock
        self.block = shards[0].shape[0]
        self.parts, blocks = [], []
        at = 0
        for shard in shards:
            height, cols = shard.shape
            count = height // self.block
            blocks += [shard[k * self.block : (k + 1) * self.block] for k in range(count)]
            self.parts.append((at, count, cols))
            at += count * cols
        self.shard = jnp.concatenate(blocks, axis=1) if len(blocks) > 1 else blocks[0]

    def step0(self):
        self.held = self.clock.gate(self.shard)
        self.far = [m for m in self.grid.z_masks if m % 2 == 0]
        self.coming = [self.grid.over_z(self.held, m) for m in self.far]

    def step1(self):
        *got, held = self.clock.gate(*self.coming, self.held)
        self.held = jnp.concatenate([held, *got], 0)
        self.clock.tick(self.held)
        self.coming = self.grid.over_z(self.held, 1)

    def step2(self):
        got, held = self.clock.gate(self.coming, self.held)
        z_marks = [0] + self.far
        z_marks += [m ^ 1 for m in z_marks]
        joined = []
        for at, count, cols in self.parts:
            cut = slice(at, at + count * cols)
            joined.append(jnp.concatenate([held[:, cut], got[:, cut]], 0))
        self.clock.tick(*joined)
        return [
            Gather(self.grid, self.clock, rows, z_marks, self.block, count, cols)
            for rows, (_, count, cols) in zip(joined, self.parts)
        ]


class Gather:
    def __init__(self, grid, clock, rows, z_marks, block, count, cols):
        self.grid, self.clock, self.rows = grid, clock, rows
        self.z_marks, self.block, self.count, self.cols = z_marks, block, count, cols
        self.pieces = []

    def take(self, rows, even_mask, odd_mask):
        self.pieces.append((rows, even_mask, odd_mask))
        self.crossing = (self.grid.over_dp(rows, 1), odd_mask ^ 1, even_mask ^ 1)

    def land(self, coming):
        rows, crossed = self.clock.gate(coming, self.crossing[0])
        self.pieces.append((crossed, *self.crossing[1:]))
        self.clock.tick(rows)
        return rows

    def step0(self):
        grid = self.grid
        (x,), (y,) = grid.x_masks, grid.y_masks
        rows = self.clock.gate(self.rows)
        self.first = grid.crossed(rows, x, y)
        self.second = grid.crossed(rows, y, x)
        self.take(rows, 0, 0)

    def step1(self):
        grid = self.grid
        (x,), (y,) = grid.x_masks, grid.y_masks
        first = self.land(self.first)
        self.third = grid.crossed(first, y, x)
        self.take(first, x, y)

    def step2(self):
        (x,), (y,) = self.grid.x_masks, self.grid.y_masks
        self.take(self.land(self.second), y, x)

    def step3(self):
        (x,), (y,) = self.grid.x_masks, self.grid.y_masks
        self.take(self.land(self.third), x ^ y, x ^ y)
        self.pieces.append(self.crossing)

    def done(self, cuts=()):
        grid, block, count = self.grid, self.block, self.count
        pieces, z_marks = self.pieces, self.z_marks
        owners = grid.n_dp * grid.n_z
        edges = [0, *cuts, self.cols]
        spans = list(zip(edges[:-1], edges[1:]))
        copies = owners * count * len(spans)

        def kernel(me_ref, *refs):
            sources = refs[: len(pieces)]
            results = refs[len(pieces) : len(pieces) + len(spans)]
            sems = refs[-1]
            me = me_ref[0]
            odd = (me // grid.n_z) % 2 == 1
            started = []
            for source, (_, even_mask, odd_mask) in zip(sources, pieces):
                mask = jnp.where(odd, jnp.int32(odd_mask), jnp.int32(even_mask))
                for at, z in enumerate(z_marks):
                    owner = lax.bitwise_xor(me, mask * grid.n_z + z)
                    for k in range(count):
                        to = pl.multiple_of((owner * count + k) * block, block)
                        for result, (lo, hi) in zip(results, spans):
                            copy = pltpu.make_async_copy(
                                source.at[
                                    pl.ds(at * block, block), pl.ds(k * self.cols + lo, hi - lo)
                                ],
                                result.at[pl.ds(to, block)],
                                sems.at[len(started)],
                            )
                            copy.start()
                            started.append(copy)
            for copy in started:
                copy.wait()

        arrays = self.clock.gate(*[v for v, _, _ in pieces])
        rows = owners * count * block
        full = pl.pallas_call(
            kernel,
            out_shape=[jax.ShapeDtypeStruct((rows, hi - lo), BF16) for lo, hi in spans],
            grid_spec=pltpu.PrefetchScalarGridSpec(
                num_scalar_prefetch=1,
                grid=(),
                in_specs=[pl.BlockSpec(memory_space=pl.ANY)] * len(pieces),
                out_specs=[pl.BlockSpec(memory_space=pltpu.VMEM)] * len(spans),
                scratch_shapes=[pltpu.SemaphoreType.DMA((copies,))],
            ),
            compiler_params=pltpu.CompilerParams(vmem_limit_bytes=10 << 20),
            cost_estimate=pl.CostEstimate(flops=0, bytes_accessed=0, transcendentals=0),
            name="assemble",
        )(grid.me.reshape(1), *arrays)
        self.clock.tick(*full)
        return full


class PlainLines:
    def __init__(self, grid, clock, shards):
        self.shards = shards

    def step0(self):
        pass

    step1 = step0

    def step2(self):
        return [PlainGather(v) for v in self.shards]


class PlainGather:
    def __init__(self, shard):
        self.full = lax.all_gather(shard, AXES, axis=0, tiled=True)

    def step0(self):
        pass

    step1 = step2 = step3 = step0

    def done(self, cuts=()):
        edges = [0, *cuts, self.full.shape[1]]
        return [self.full[:, lo:hi] for lo, hi in zip(edges[:-1], edges[1:])]


def make_lines(grid, clock, *shards):
    plain = shards[0].shape[0] % 16 or not grid.square
    kind = PlainLines if plain else Lines
    return kind(grid, clock, shards)


def contract_rows(left, right):
    return lax.dot_general(left, right, (((0,), (0,)), ((), ())), preferred_element_type=F32)


def back_dot(grad_rows, weight):
    return lax.dot_general(grad_rows, weight, (((1,), (1,)), ((), ())), preferred_element_type=F32)


def pick(array, index):
    return lax.dynamic_index_in_dim(array, index, 0, keepdims=False)


def total_of(base, parts):
    for part in parts:
        base = base + part.astype(F32)
    return base


class Scatter:
    places = 4

    def __init__(self, grid, clock, lefts, rights):
        self.grid, self.clock, self.lefts, self.rights = grid, clock, lefts, rights
        self.chunk = lefts[0].shape[1] // grid.n_dp
        self.cols = sum(right.shape[1] for right in rights)
        once = pl.Buffered(1)
        self.whole = pl.BlockSpec(
            (self.chunk, self.cols), lambda j, dp: (0, 0), pipeline_mode=once
        )
        self.rows = [
            pl.BlockSpec(right.shape, lambda j, dp: (0, 0), pipeline_mode=once) for right in rights
        ]

    def shape(self, dtype):
        return jax.ShapeDtypeStruct((self.chunk, self.cols), dtype)

    def call(self, kernel, other, ins, shapes, specs):
        tokens, count = self.lefts[0].shape[0], len(self.lefts)

        def place(j, dp):
            a, b = j // 2, j % 2
            odd = (dp[0] + other) % 2
            mask = jnp.where(odd == 1, 2 * a + 4 * b, 4 * a + 2 * b)
            return 0, lax.bitwise_xor(dp[0], mask + other)

        def whole_kernel(dp_ref, *refs):
            lefts, rights, rest = refs[:count], refs[count : 2 * count], refs[2 * count :]
            terms = [contract_rows(a[...], b[...]) for a, b in zip(lefts, rights)]
            kernel(jnp.concatenate(terms, axis=1) if count > 1 else terms[0], *rest)

        ins = self.clock.gate(*self.lefts, *self.rights, *ins)
        return pl.pallas_call(
            whole_kernel,
            out_shape=shapes,
            grid_spec=pltpu.PrefetchScalarGridSpec(
                num_scalar_prefetch=1,
                grid=(self.places,),
                in_specs=[
                    *[pl.BlockSpec((tokens, self.chunk), place) for _ in self.lefts],
                    *self.rows,
                    *[self.whole for _ in ins[2 * count :]],
                ],
                out_specs=specs,
            ),
            compiler_params=pltpu.CompilerParams(vmem_limit_bytes=18 << 20),
            cost_estimate=pl.CostEstimate(flops=0, bytes_accessed=0, transcendentals=0),
            name="outer",
        )(self.grid.my_dp.reshape(1), *ins)

    def across(self):
        def kernel(term, *outs):
            term = term.astype(BF16)
            for k, out in enumerate(outs):

                @pl.when(pl.program_id(0) == k)
                def _(out=out):
                    out[...] = term

        shapes = [self.shape(BF16)] * self.places
        sends = self.call(kernel, 1, (), shapes, [self.whole] * self.places)
        self.clock.tick(*sends)
        self.got = [self.grid.over_dp(v, 1) for v in sends]

    def first(self):
        grid, places = self.grid, self.places
        (x,), (y,) = grid.x_masks, grid.y_masks

        def kernel(term, *refs):
            got, (keep, pass_on, far) = refs[:places], refs[places:]
            outs = (keep, pass_on, far.at[0], far.at[1])
            for k in range(places):

                @pl.when(pl.program_id(0) == k)
                def _(k=k):
                    outs[k][...] = (term + got[k][...].astype(F32)).astype(outs[k].dtype)

        wide = self.shape(F32)
        pair = jax.ShapeDtypeStruct((2, *wide.shape), BF16)
        pair_spec = pl.BlockSpec(
            pair.shape, lambda j, dp: (0, 0, 0), pipeline_mode=pl.Buffered(1)
        )
        keep, pass_on, far = self.call(
            kernel, 0, self.got, [wide, wide, pair], [self.whole, self.whole, pair_spec]
        )
        self.clock.tick(far)
        self.keep, self.pass_on = keep, pass_on
        self.got = grid.crossed(far, y, x)

    def second(self):
        (x,), (y,) = self.grid.x_masks, self.grid.y_masks
        got, pass_on = self.clock.gate(self.got, self.pass_on)
        send = (pass_on + got[1].astype(F32)).astype(BF16)
        self.clock.tick(send)
        self.aside = got[0]
        self.got = self.grid.crossed(send, x, y)

    def land(self):
        self.got = self.clock.gate(self.got)
        self.clock.tick(self.got)

    def third(self):
        grid = self.grid
        got, keep = self.clock.gate(self.got, self.keep)
        lines = total_of(keep, [got, self.aside]).reshape(2, 2, -1, self.cols)
        odd = grid.my_z % 2
        send = lax.dynamic_index_in_dim(lines, 1 - odd, 1, keepdims=False).astype(BF16)
        self.keep = lax.dynamic_index_in_dim(lines, odd, 1, keepdims=False)
        self.clock.tick(send)
        self.got = grid.over_z(send, 1)

    def fourth(self):
        grid = self.grid
        got, keep = self.clock.gate(self.got, self.keep)
        held = keep + got.astype(F32)
        pair = grid.my_z // 2
        send = pick(held, 1 - pair).astype(BF16)
        self.keep = pick(held, pair)
        self.clock.tick(send)
        self.got = grid.over_z(send, 2)

    def done(self):
        got, keep = self.clock.gate(self.got, self.keep)
        outs, at = [], 0
        for right in self.rights:
            cut = slice(at, at + right.shape[1])
            outs.append(keep[:, cut] + got[:, cut].astype(F32))
            at += right.shape[1]
        self.clock.tick(*outs)
        return outs


class PlainScatter:
    def __init__(self, lefts, rights):
        self.terms = [contract_rows(a, b) for a, b in zip(lefts, rights)]

    def across(self):
        pass

    first = second = land = third = fourth = across

    def done(self):
        return [lax.psum_scatter(t, AXES, scatter_dimension=0, tiled=True) for t in self.terms]


def make_scatter(grid, clock, *pairs):
    lefts, rights = [a for a, _ in pairs], [b for _, b in pairs]
    if (lefts[0].shape[1] // grid.n_dp) % 128 or not grid.square:
        return PlainScatter(lefts, rights)
    return Scatter(grid, clock, lefts, rights)


def lookup(small_table, index_rows):
    matches = index_rows[:, None] == jnp.arange(small_table.shape[0], dtype=jnp.int32)[None, :]
    return jnp.sum(jnp.where(matches, small_table[None, :], 0), axis=1)


def rank_among(group_label, order_key):
    earlier = (group_label[None, :] == group_label[:, None]) & (
        order_key[None, :] < order_key[:, None]
    )
    return jnp.sum(earlier.astype(jnp.int32), axis=1)


def routing(lengths, deal_order, devices, row_count, device):
    slot_count = deal_order.shape[0]
    slot_ids = jnp.arange(slot_count, dtype=jnp.int32)
    starts = jnp.cumsum(lengths) - lengths
    slot_of = jnp.sum(
        jnp.where(deal_order[None, :] == slot_ids[:, None], slot_ids[None, :], 0), axis=1
    )
    slot_lengths = lookup(lengths, deal_order)
    local_rows = jnp.arange(row_count, dtype=jnp.int32)
    token_index = local_rows * devices + device
    sequence = jnp.sum((starts[None, :] <= token_index[:, None]).astype(jnp.int32), axis=1) - 1
    slot_index = lookup(slot_of, sequence)
    target = slot_index // 2
    send_rank = rank_among(target, local_rows)
    first_len = lax.dynamic_index_in_dim(slot_lengths, 2 * device, 0, False)
    second = local_rows >= first_len
    first_seq = lax.dynamic_index_in_dim(deal_order, 2 * device, 0, False)
    second_seq = lax.dynamic_index_in_dim(deal_order, 2 * device + 1, 0, False)
    sequence_here = jnp.where(second, second_seq, first_seq)
    position = local_rows - jnp.where(second, first_len, 0)
    source_token = lookup(starts, sequence_here) + position
    source = source_token % devices
    take_rank = rank_among(source, source_token)
    return target, send_rank, source, take_rank, first_len.reshape(1)


HEADS_AT_ONCE = 4
LANES = HEADS_AT_ONCE * HEAD_DIM


def head_probs(query, key, first_len):
    scores = back_dot(query, key)
    q_at = lax.broadcasted_iota(jnp.int32, scores.shape, 0)
    k_at = lax.broadcasted_iota(jnp.int32, scores.shape, 1)
    allowed = (k_at <= q_at) & ((q_at < first_len) | (k_at >= first_len))
    masked = jnp.where(allowed, scores, -1000000000.0)
    exps = jnp.exp(masked - jnp.max(masked, axis=-1, keepdims=True))
    return exps * (1.0 / jnp.sum(exps, axis=-1, keepdims=True))


def of_heads(rows, parts):
    head = lax.broadcasted_iota(jnp.int32, (rows, LANES), 1) // HEAD_DIM
    whole = parts[0]
    for k in range(1, len(parts)):
        whole = jnp.where(head == k, parts[k], whole)
    return whole


def one_head(values, k):
    head = lax.broadcasted_iota(jnp.int32, values.shape, 1) // HEAD_DIM
    return jnp.where(head == k, values, jnp.zeros((), BF16))


def attend(first_len, mixed_b):
    rows, width = mixed_b.shape[0], mixed_b.shape[1] // 3
    steps = width // LANES

    def kernel(first_ref, query, key, value, out):
        scaled = query[...] * jnp.asarray(HEAD_DIM**-0.5, BF16)
        probs = [
            head_probs(one_head(scaled, k), key[...], first_ref[0]).astype(BF16)
            for k in range(HEADS_AT_ONCE)
        ]
        found = [jnp.dot(p, value[...], preferred_element_type=F32) for p in probs]
        out[...] = of_heads(rows, found).astype(BF16)

    def part(k):
        return pl.BlockSpec((rows, LANES), lambda h, first: (0, k * steps + h))

    return pl.pallas_call(
        kernel,
        out_shape=jax.ShapeDtypeStruct((rows, width), BF16),
        grid_spec=pltpu.PrefetchScalarGridSpec(
            num_scalar_prefetch=1,
            grid=(steps,),
            in_specs=[part(0), part(1), part(2)],
            out_specs=part(0),
        ),
        compiler_params=pltpu.CompilerParams(vmem_limit_bytes=10 << 20),
        cost_estimate=pl.CostEstimate(flops=0, bytes_accessed=0, transcendentals=0),
        name="attend",
    )(first_len, mixed_b, mixed_b, mixed_b)


def attend_back(first_len, mixed_b, grad_att_b):
    rows, width = grad_att_b.shape
    steps = width // LANES

    def kernel(first_ref, query, key, value, grad, out, sums):
        h = pl.program_id(0)
        scaled = query[...] * jnp.asarray(HEAD_DIM**-0.5, BF16)
        to_query, to_key, to_value = [], [], []
        for k in range(HEADS_AT_ONCE):
            q, g = one_head(scaled, k), one_head(grad[...], k)
            probs = head_probs(q, key[...], first_ref[0])
            grad_probs = back_dot(g, value[...])
            dots = jnp.sum(probs * grad_probs, axis=-1, keepdims=True)
            grad_scores = (probs * (grad_probs - dots)).astype(BF16)
            to_query.append(jnp.dot(grad_scores, key[...], preferred_element_type=F32))
            to_key.append(contract_rows(grad_scores, q))
            to_value.append(contract_rows(probs.astype(BF16), g))
        results = (of_heads(rows, to_query) * HEAD_DIM**-0.5, sum(to_key), sum(to_value))
        for k, block in enumerate(results):
            block = block.astype(BF16)
            at = pl.multiple_of(k * width + h * LANES, LANES)
            out[:, pl.ds(at, LANES)] = block
            sums[:, pl.ds(at, LANES)] = jnp.sum(block.astype(F32), axis=0, keepdims=True)

    def part(k):
        return pl.BlockSpec((rows, LANES), lambda h, first: (0, k * steps + h))

    return pl.pallas_call(
        kernel,
        out_shape=[
            jax.ShapeDtypeStruct((rows, 3 * width), BF16),
            jax.ShapeDtypeStruct((1, 3 * width), F32),
        ],
        grid_spec=pltpu.PrefetchScalarGridSpec(
            num_scalar_prefetch=1,
            grid=(steps,),
            in_specs=[part(0), part(1), part(2), part(0)],
            out_specs=[
                pl.BlockSpec((rows, 3 * width), lambda h, first: (0, 0)),
                pl.BlockSpec((1, 3 * width), lambda h, first: (0, 0)),
            ],
        ),
        compiler_params=pltpu.CompilerParams(vmem_limit_bytes=16 << 20),
        cost_estimate=pl.CostEstimate(flops=0, bytes_accessed=0, transcendentals=0),
        name="attend_back",
    )(first_len, mixed_b, mixed_b, mixed_b, grad_att_b)


def gelu_back(grad_b, weight, slope):
    rows, width = grad_b.shape
    hidden = weight.shape[0]
    tile = min(1024, hidden)

    def kernel(grad, weight, slope, out, sums):
        block = (back_dot(grad[...], weight[...]) * slope[...]).astype(BF16)
        out[...] = block
        sums[...] = jnp.sum(block.astype(F32), axis=0, keepdims=True)

    return pl.pallas_call(
        kernel,
        out_shape=[
            jax.ShapeDtypeStruct((rows, hidden), BF16),
            jax.ShapeDtypeStruct((1, hidden), F32),
        ],
        grid=(hidden // tile,),
        in_specs=[
            pl.BlockSpec((rows, width), lambda j: (0, 0)),
            pl.BlockSpec((tile, width), lambda j: (j, 0)),
            pl.BlockSpec((rows, tile), lambda j: (0, j)),
        ],
        out_specs=[
            pl.BlockSpec((rows, tile), lambda j: (0, j)),
            pl.BlockSpec((1, tile), lambda j: (0, j)),
        ],
        compiler_params=pltpu.CompilerParams(vmem_limit_bytes=14 << 20),
        cost_estimate=pl.CostEstimate(flops=0, bytes_accessed=0, transcendentals=0),
        name="gelu_back",
    )(grad_b, weight, slope)


def norm_back(grad_b, weight, unit, gain, scale, passed, keep_wide):
    rows, depth = grad_b.shape
    width = weight.shape[0]
    tile = 1024
    steps = depth // tile

    def kernel(grad, weight, unit, gain, scale, passed, *refs):
        outs, total = refs[:-1], refs[-1]
        step = pl.program_id(0)
        part = back_dot(grad[...], weight[...])

        @pl.when(step == 0)
        def _():
            total[...] = part

        @pl.when(step > 0)
        def _():
            total[...] += part

        @pl.when(step == steps - 1)
        def _():
            whole, u = total[...], unit[...]
            normed = whole * gain[...]
            out = passed[...].astype(F32) + standardize_back(normed, u, scale[...])
            out_b = out.astype(BF16)
            outs[0][...] = out_b
            outs[1][0:1] = jnp.sum(whole * u, axis=0, keepdims=True)
            outs[1][1:2] = jnp.sum(whole, axis=0, keepdims=True)
            outs[1][2:3] = jnp.sum(out_b.astype(F32), axis=0, keepdims=True)
            if keep_wide:
                outs[2][...] = out

    def once(shape):
        return pl.BlockSpec(shape, lambda j: (0, 0), pipeline_mode=pl.Buffered(1))

    shapes = [((rows, width), BF16), ((8, width), F32)]
    shapes += [((rows, width), F32)] if keep_wide else []
    return pl.pallas_call(
        kernel,
        out_shape=[jax.ShapeDtypeStruct(*s) for s in shapes],
        grid=(steps,),
        in_specs=[
            pl.BlockSpec((rows, tile), lambda j: (0, j)),
            pl.BlockSpec((width, tile), lambda j: (0, j)),
            once((rows, width)),
            once((1, width)),
            once((rows, 1)),
            once((rows, width)),
        ],
        out_specs=[once(shape) for shape, _ in shapes],
        scratch_shapes=[pltpu.VMEM((rows, width), F32)],
        compiler_params=pltpu.CompilerParams(vmem_limit_bytes=16 << 20),
        cost_estimate=pl.CostEstimate(flops=0, bytes_accessed=0, transcendentals=0),
        name="norm_back",
    )(grad_b, pltpu.with_memory_space_constraint(weight, pltpu.HBM), unit, gain, scale, passed)


def standardize(values):
    centered = values - jnp.mean(values, axis=-1, keepdims=True)
    scale = lax.rsqrt(jnp.mean(centered * centered, axis=-1, keepdims=True) + EPSILON)
    return centered * scale, scale


def standardize_back(grad, unit, scale):
    return scale * (
        grad
        - jnp.mean(grad, axis=-1, keepdims=True)
        - unit * jnp.mean(grad * unit, axis=-1, keepdims=True)
    )


def col_sum(values):
    return jnp.sum(values.astype(F32), axis=0)


def on_device(
    n_dp,
    n_z,
    rows_in,
    cotangent,
    lengths,
    deal_order,
    w_qkv,
    b_query,
    b_value,
    w_out,
    b_out,
    gain_one,
    shift_one,
    w_up,
    b_up,
    w_down,
    b_down,
    gain_two,
    shift_two,
):
    grid = Grid(n_dp, n_z)
    grid.bind()
    clock = Clock()
    devices = n_dp * n_z
    row_count, _, width = rows_in.shape
    hidden = w_up.shape[1]
    share = width // devices

    early = make_lines(grid, clock, jnp.concatenate([w_qkv, w_out], axis=1))
    middle = make_lines(grid, clock, w_up)
    late = make_lines(grid, clock, w_down)
    early.step0()

    target, send_rank, source, take_rank, first_len = routing(
        lengths, deal_order, devices, row_count, grid.me
    )
    slot_rows = row_count // devices + 1
    in_rows = slot_rows
    out_rows = 2 * slot_rows

    def selector(owner, rank, block_rows):
        at = (owner * block_rows + rank)[:, None]
        slot_ids = jnp.arange(devices * block_rows, dtype=jnp.int32)[None, :]
        return (at == slot_ids).astype(BF16)

    to_slots = selector(target, send_rank, in_rows)
    from_slots = selector(source, take_rank, in_rows)

    def both_of(owner, rank):
        at = owner * out_rows + rank
        return jnp.concatenate([at, at + slot_rows])

    out_slot_ids = jnp.arange(devices * out_rows, dtype=jnp.int32)
    take_both = (both_of(target, send_rank)[:, None] == out_slot_ids[None, :]).astype(BF16)
    send_both = (out_slot_ids[:, None] == both_of(source, take_rank)[None, :]).astype(BF16)

    def swap(block, lines=None):
        block = block.reshape(devices, -1, 128)
        if lines is not None:
            block = jnp.concatenate([block, lines], axis=1)
        block = lax.all_to_all(block, AXES, split_axis=0, concat_axis=0, tiled=True)
        if lines is None:
            return block.reshape(-1, width)
        height = block.shape[1] - lines.shape[1]
        return block[:, :height].reshape(-1, width), block[:, height:]

    vectors = jnp.stack(
        [b_query, b_value, b_out, gain_one, shift_one, b_down, gain_two, shift_two]
    )
    groups = 128 // share
    spot = grid.me % groups
    at_spot = lax.broadcasted_iota(jnp.int32, (8, 128), 1) // share == spot
    vectors = jnp.where(at_spot, jnp.tile(vectors, (1, groups)), jnp.zeros((), BF16))
    bias_groups = max(1, 128 * devices // hidden)
    bias = jnp.tile(b_up[None, :], (1, bias_groups))
    at_bias = lax.broadcasted_iota(jnp.int32, (1, 128), 1) // b_up.shape[0]
    bias = jnp.where(at_bias == grid.me % bias_groups, bias, jnp.zeros((), BF16))
    bias = jnp.pad(bias, ((0, 7), (0, 0)))
    small = jnp.concatenate([vectors, bias], axis=0)
    early.step1()
    middle.step0()
    to_slots, own_rows = clock.gate(to_slots, rows_in)
    block = contract_rows(to_slots, own_rows.reshape(row_count, width))
    block = block.astype(BF16)
    clock.tick(block)
    (attn,) = early.step2()
    attn.step0()
    middle.step1()
    late.step0()
    small = jnp.broadcast_to(small[None], (devices, *small.shape))
    arrived, small_all = swap(clock.gate(block), small)
    attn.step1()
    attn.step2()
    (up,) = middle.step2()
    up.step0()
    late.step1()
    attn.step3()
    arrived, small_all = clock.gate(arrived, small_all)
    inputs = jnp.dot(from_slots, arrived, preferred_element_type=F32)
    lines = jnp.sum(small_all[:, :8].astype(F32).reshape(-1, groups, 8, 128), axis=1)
    bq, bv, bo, g1, s1, bd, g2, s2 = [
        v[None, :] for v in jnp.swapaxes(lines, 0, 1).reshape(8, width)
    ]
    lines = jnp.sum(small_all[:, 8].astype(F32).reshape(-1, bias_groups, 128), axis=1)
    bu = lines.reshape(1, hidden)
    unit_one, scale_one = standardize(inputs)
    normed_one_b = (unit_one * g1 + s1).astype(BF16)
    clock.tick(normed_one_b)
    take_both, send_both = clock.gate(take_both, send_both)
    clock.tick(take_both, send_both)
    (down,) = late.step2()
    up.step1()
    up.step2()
    down.step0()
    full_qkv, full_out = attn.done((3 * width,))
    mixed = jnp.dot(clock.gate(normed_one_b), full_qkv, preferred_element_type=F32)
    mixed_b = (mixed + jnp.concatenate([bq, jnp.zeros_like(bq), bv], axis=1)).astype(BF16)
    attended_b = attend(first_len, mixed_b)
    clock.tick(attended_b)
    up.step3()
    attended_b, cot_rows = clock.gate(attended_b, cotangent)
    cot_block = contract_rows(to_slots, cot_rows.reshape(row_count, width)).astype(BF16)
    clock.tick(cot_block)
    arrived_cot = swap(cot_block)
    hidden_one = inputs + jnp.dot(attended_b, full_out, preferred_element_type=F32) + bo
    unit_two, scale_two = standardize(hidden_one)
    normed_two_b = (unit_two * g2 + s2).astype(BF16)
    clock.tick(normed_two_b)

    (full_up,) = up.done()
    down.step1()
    down.step2()
    pre_act = jnp.dot(clock.gate(normed_two_b), full_up, preferred_element_type=F32) + bu
    half_cdf = 0.5 * (1.0 + lax.erf(pre_act * (0.5**0.5)))
    activation_b = (pre_act * half_cdf).astype(BF16)
    density = jnp.exp(-0.5 * pre_act * pre_act) * ((2.0 * jnp.pi) ** -0.5)
    slope = half_cdf + pre_act * density
    clock.tick(activation_b, slope)

    arrived_cot = clock.gate(arrived_cot)
    grad_m_b = jnp.dot(from_slots, arrived_cot, preferred_element_type=F32)
    grad_m_b = grad_m_b.astype(BF16)
    clock.tick(grad_m_b)
    term_b_down = col_sum(grad_m_b)[None, :]
    for_down = make_scatter(grid, clock, (activation_b, grad_m_b))
    for_down.across()
    down.step3()
    (full_down,) = down.done()
    grad_pre_b, term_b_up = gelu_back(clock.gate(grad_m_b), full_down, slope)
    clock.tick(grad_pre_b)
    for_down.first()
    for_up = make_scatter(grid, clock, (normed_two_b, grad_pre_b))
    for_up.across()

    grad_branch_b, sums_two, grad_hidden = norm_back(
        clock.gate(grad_pre_b), full_up, unit_two, g2, scale_two, grad_m_b, True
    )
    clock.tick(grad_branch_b)
    for_up.first()
    for_down.second()
    grad_att_b = back_dot(clock.gate(grad_branch_b), full_out).astype(BF16)
    clock.tick(grad_att_b)
    grad_mixed_b, term_mixed = attend_back(first_len, mixed_b, clock.gate(grad_att_b))
    clock.tick(grad_mixed_b)
    for_attn = make_scatter(
        grid, clock, (normed_one_b, grad_mixed_b), (attended_b, grad_branch_b)
    )
    for_attn.across()

    grad_inputs_b, sums_one = norm_back(
        clock.gate(grad_mixed_b), full_qkv, unit_one, g1, scale_one, grad_hidden, False
    )
    clock.tick(grad_inputs_b)
    for_attn.first()
    for_up.second()
    for_down.third()
    result = jnp.dot(clock.gate(activation_b), full_down, preferred_element_type=F32)
    result_b = (hidden_one + result + bd).astype(BF16)
    term_mixed, sums_one, sums_two, term_b_down, term_b_up, result_b = clock.gate(
        term_mixed, sums_one, sums_two, term_b_down, term_b_up, result_b
    )
    terms = [term_mixed[:, :width], term_mixed[:, 2 * width :], sums_two[2:3], sums_one[:2]]
    terms = jnp.concatenate([*terms, term_b_down, sums_two[:2]], axis=0).astype(BF16)
    lines = jnp.swapaxes(terms.reshape(8, -1, 128), 0, 1)
    lines = jnp.repeat(lines, groups, axis=0)
    bias = jnp.repeat(term_b_up.astype(BF16).reshape(-1, 1, 128), bias_groups, axis=0)
    lines = jnp.concatenate([lines, jnp.pad(bias, ((0, 0), (0, 7), (0, 0)))], axis=1)
    both = jnp.concatenate([result_b, grad_inputs_b], axis=0)
    block = jnp.dot(send_both, both, preferred_element_type=F32)
    block = block.astype(BF16)
    clock.tick(block)
    returned, small_back = swap(block, lines)

    for_up.third()
    for_attn.second()
    for_down.fourth()
    returned, small_back = clock.gate(returned, small_back)
    clock.tick(returned)
    for_attn.third()
    for_up.fourth()
    for_attn.fourth()
    returned = clock.gate(returned)
    placed = jnp.dot(take_both, returned, preferred_element_type=F32)
    placed = placed.astype(BF16)
    rows_out, grad_rows = placed[:row_count], placed[row_count:]
    sums = jnp.sum(small_back.astype(F32), axis=0)
    clock.tick(placed)
    (grad_w_down,) = for_down.done()
    (grad_w_up,) = for_up.done()
    grad_w_qkv, grad_w_out = for_attn.done()

    mine = lax.dynamic_slice_in_dim(sums[:8], spot * share, share, axis=1)
    grad_bq, grad_bv, grad_bo, grad_g1, grad_s1, grad_bd, grad_g2, grad_s2 = mine
    bias_width = hidden // devices
    grad_bu = lax.dynamic_slice_in_dim(
        sums[8], (grid.me % bias_groups) * bias_width, bias_width, axis=0
    )
    return (
        rows_out.reshape(row_count, 1, width),
        grad_rows.reshape(row_count, 1, width),
        grad_w_qkv,
        grad_bq,
        grad_bv,
        grad_w_out,
        grad_bo,
        grad_g1,
        grad_s1,
        grad_w_up,
        grad_bu,
        grad_w_down,
        grad_bd,
        grad_g2,
        grad_s2,
    )


def solution(mesh):
    n_dp, n_z = mesh.shape["dp"], mesh.shape["fsdp"]
    rows, vec, mat = P(None, AXES, None), P(AXES), P(AXES, None)

    def run(*args):
        return on_device(n_dp, n_z, *args)

    return jax.shard_map(
        run,
        mesh=mesh,
        in_specs=(rows, rows, P(), P())
        + (mat, vec, vec, mat, vec, vec, vec, mat, vec, mat, vec, vec, vec),
        out_specs=(rows, rows, mat, vec, vec, mat, vec, vec, vec, mat, vec, mat, vec, vec, vec),
        check_vma=False,
    )
```

profile of v0, /device:TPU:0, one launch (start us, length us, event | category | flops | bytes accessed | tf_op | source)
XLA Modules:
  0.0 354.6 jit_solution(7767125353256784300)
XLA Ops:
  1.7 4.1 %collective-permute-start = (bf16[32,4096]{1,0:T(8,128)(2,1)S(1)}, bf16[32,4096]{1,0:T(8,128)(2,1)S(1)}, u32[]{:S(2)}, u32[]{:S(2)}) collective-permute-start(bf16[32,4096]{1,0:T(8,128)(2,1)S(1)} %pad_maximum_fusion.1), channel_id=1, source_target_pairs={{0,2},{1,3},{2,0},{3,1},{4,6},{5,7},{6,4},{7,5},{8,10},{9,11},{10,... | collective-permute-start | bytes 786440 | tf_op jit(solution)/shard_map/ppermute | solution.py:41
  22.5 14.1 %collective-permute-done.2 = bf16[64,4096]{1,0:T(8,128)(2,1)S(1)} collective-permute-done((bf16[64,4096]{1,0:T(8,128)(2,1)S(1)}, bf16[64,4096]{1,0:T(8,128)(2,1)S(1)}, u32[]{:S(2)}, u32[]{:S(2)}) %collective-permute-start.2) | collective-permute-done | bytes 524320 | tf_op jit(solution)/shard_map/ppermute | solution.py:41
  41.1 5.9 %all-to-all-start = ((bf16[32,88,128]{2,1,0:T(8,128)(2,1)}), bf16[32,88,128]{2,1,0:T(8,128)(2,1)S(1)}, u32[]{:S(2)}, u32[]{:S(2)}) async-start(bf16[32,88,128]{2,1,0:T(8,128)(2,1)} %pad_maximum_fusion), calls=%async_computation | async-start | bytes 1441792 | tf_op jit(solution)/shard_map/all_to_all | solution.py:706
  48.9 7.2 %collective-permute-done.3.refs_2_ = bf16[128,4096]{1,0:T(8,128)(2,1)S(1)} collective-permute-done((bf16[128,4096]{1,0:T(8,128)(2,1)S(1)}, bf16[128,4096]{1,0:T(8,128)(2,1)S(1)}, u32[]{:S(2)}, u32[]{:S(2)}) %collective-permute-start.3) | collective-permute-done | bytes 1048608 | tf_op jit(solution)/shard_map/ppermute | solution.py:38
  59.1 7.2 %collective-permute-start.9 = (bf16[128,1024]{1,0:T(8,128)(2,1)}, bf16[128,1024]{1,0:T(8,128)(2,1)}, u32[]{:S(2)}, u32[]{:S(2)}) collective-permute-start(bf16[128,1024]{1,0:T(8,128)(2,1)} %param.30), channel_id=1, source_target_pairs={{0,2},{1,3},{2,0},{3,1},{4,6},{5,7},{6,4},{7,5},{8,10},{9,11},{10,... | collective-permute-start | bytes 786440 | tf_op jit(solution)/shard_map/ppermute | solution.py:41
  71.8 8.3 %collective-permute-done.10 = bf16[64,4096]{1,0:T(8,128)(2,1)} collective-permute-done((bf16[64,4096]{1,0:T(8,128)(2,1)S(1)}, bf16[64,4096]{1,0:T(8,128)(2,1)}, u32[]{:S(2)}, u32[]{:S(2)}) %collective-permute-start.10) | collective-permute-done | bytes 524320 | tf_op jit(solution)/shard_map/ppermute | solution.py:41
  88.1 10.9 %collective-permute-done.15 = bf16[256,1024]{1,0:T(8,128)(2,1)S(1)} collective-permute-done((bf16[256,1024]{1,0:T(8,128)(2,1)S(1)}, bf16[256,1024]{1,0:T(8,128)(2,1)S(1)}, u32[]{:S(2)}, u32[]{:S(2)}) %collective-permute-start.15) | collective-permute-done | bytes 524320 | tf_op jit(solution)/shard_map/ppermute | solution.py:41
  100.7 6.2 %collective-permute-done.13.refs_2_ = bf16[128,4096]{1,0:T(8,128)(2,1)S(1)} collective-permute-done((bf16[128,4096]{1,0:T(8,128)(2,1)S(1)}, bf16[128,4096]{1,0:T(8,128)(2,1)S(1)}, u32[]{:S(2)}, u32[]{:S(2)}) %collective-permute-start.13) | collective-permute-done | bytes 1048608 | tf_op jit(solution)/shard_map/ppermute | solution.py:38
  134.3 8.0 %all-to-all-start.1 = ((bf16[32,72,128]{2,1,0:T(8,128)(2,1)}), bf16[32,72,128]{2,1,0:T(8,128)(2,1)}, u32[]{:S(2)}, u32[]{:S(2)}) async-start(bf16[32,72,128]{2,1,0:T(8,128)(2,1)} %reshape.379), calls=%async_computation.1 | async-start | bytes 1179648 | tf_op jit(solution)/shard_map/all_to_all | solution.py:706
  160.6 6.3 %fusion.3 = (f32[256,4096]{1,0:T(8,128)S(1)}, bf16[256,4096]{1,0:T(8,128)(2,1)S(1)}) fusion(f32[4096]{0:T(1024)S(1)} %bitcast.179, bf16[256,1024]{1,0:T(8,128)(2,1)S(1)} %get-tuple-element.281.refs_0_, bf16[1024,4096]{1,0:T(8,128)(2,1)} %copy-done.3), kind=kOutput, calls=%fused_computation.5 | convolution fusion | flops 2159017984 | bytes 15220736 | tf_op jit(solution)/shard_map/dot_general | solution.py:778
  180.4 4.1 %outer.7 = (f32[512,1024]{1,0:T(8,128)S(1)}, f32[512,1024]{1,0:T(8,128)S(1)}, bf16[2,512,1024]{2,1,0:T(8,128)(2,1)}) custom-call(s32[1]{0:T(128)} %bitcast.27.dp_ref, bf16[256,4096]{1,0:T(8,128)(2,1)S(1)} %get-tuple-element.322.refs_0_, bf16[256,1024]{1,0:T(8,128)(2,1)S(1)} %get-tuple-element.266.refs_1_.grad.passed, ...), custom_call_target="tpu_custom_call" | custom-call | tf_op jit(solution)/shard_map/outer/pallas_call | solution.py:274
  187.3 4.5 %outer.8 = (bf16[128,4096]{1,0:T(8,128)(2,1)}, bf16[128,4096]{1,0:T(8,128)(2,1)}, bf16[128,4096]{1,0:T(8,128)(2,1)}, bf16[128,4096]{1,0:T(8,128)(2,1)}) custom-call(s32[1]{0:T(128)} %bitcast.27.dp_ref, bf16[256,1024]{1,0:T(8,128)(2,1)S(1)} %copy-done.16, bf16[256,4096]{1,0:T(8,128)(2,1)S(1)} %get-tuple-element.282.refs_1_.grad), custom_call_target="tpu_custom_call" | custom-call | tf_op jit(solution)/shard_map/outer/pallas_call | solution.py:274
  195.8 6.8 %norm_back.2 = (bf16[256,1024]{1,0:T(8,128)(2,1)S(1)}, f32[8,1024]{1,0:T(8,128)S(1)}, f32[256,1024]{1,0:T(8,128)S(1)}) custom-call(bf16[256,4096]{1,0:T(8,128)(2,1)S(1)} %copy-done.5, bf16[1024,4096]{1,0:T(8,128)(2,1)} %copy-done.3, f32[256,1024]{1,0:T(8,128)S(1)} %copy-done.18, f32[1,1024]{1,0:T(1,128)S(1)} %get-tuple-element.375.gain, ...), custom_call_target="tpu_custom_call" | custom-call | tf_op jit(solution)/shard_map/norm_back/pallas_call | solution.py:607
  203.7 6.6 %outer.9 = (f32[128,4096]{1,0:T(8,128)S(1)}, f32[128,4096]{1,0:T(8,128)S(1)}, bf16[2,128,4096]{2,1,0:T(8,128)(2,1)}) custom-call(s32[1]{0:T(128)} %bitcast.27.dp_ref, bf16[256,1024]{1,0:T(8,128)(2,1)S(1)} %copy-done.16, bf16[256,4096]{1,0:T(8,128)(2,1)S(1)} %copy-done.6, bf16[128,4096]{1,0:T(8,128)(2,1)} %collective-permute-done.32.refs_2_, ...), custom_call_target="tpu_custom_call" | custom-call | tf_op jit(solution)/shard_map/outer/pallas_call | solution.py:274
  216.2 9.8 %attend_back.1 = (bf16[256,3072]{1,0:T(8,128)(2,1)S(1)}, f32[1,3072]{1,0:T(1,128)S(1)}) custom-call(s32[1]{0:T(128)} %dynamic_slice.54.first_ref, bf16[256,3072]{1,0:T(8,128)(2,1)S(1)} %fusion.4.query.key.value, bf16[256,3072]{1,0:T(8,128)(2,1)S(1)} %fusion.4.query.key.value, bf16[256,3072]{1,0:T(8,128)(2,1)S(1)} %fusion.4.query.key.value, ...), custom_call_target="tpu_custom_call" | custom-call | tf_op jit(solution)/shard_map/attend_back/pallas_call | solution.py:517
  226.1 4.5 %outer.10 = (bf16[128,4096]{1,0:T(8,128)(2,1)S(1)}, bf16[128,4096]{1,0:T(8,128)(2,1)}, bf16[128,4096]{1,0:T(8,128)(2,1)}, bf16[128,4096]{1,0:T(8,128)(2,1)}) custom-call(s32[1]{0:T(128)} %bitcast.27.dp_ref, bf16[256,1024]{1,0:T(8,128)(2,1)S(1)} %copy-done.14, bf16[256,1024]{1,0:T(8,128)(2,1)S(1)} %attend.1.refs_1_, ...), custom_call_target="tpu_custom_call" | custom-call | tf_op jit(solution)/shard_map/outer/pallas_call | solution.py:274
  240.6 6.0 %norm_back.3 = (bf16[256,1024]{1,0:T(8,128)(2,1)S(1)}, f32[8,1024]{1,0:T(8,128)S(1)}) custom-call(bf16[256,3072]{1,0:T(8,128)(2,1)S(1)} %copy-done.8, bf16[1024,3072]{1,0:T(8,128)(2,1)} %copy-done.12, f32[256,1024]{1,0:T(8,128)S(1)} %copy-done.17, f32[1,1024]{1,0:T(1,128)S(1)} %get-tuple-element.374.gain, f32[256,1]{1,0:T(8,128)S(1)} %copy.56.scale, ...), custom_call_target="tpu_custom_call" | custom-call | tf_op jit(solution)/shard_map/norm_back/pallas_call | solution.py:607
  246.7 6.3 %outer.11 = (f32[128,4096]{1,0:T(8,128)S(1)}, f32[128,4096]{1,0:T(8,128)S(1)}, bf16[2,128,4096]{2,1,0:T(8,128)(2,1)}) custom-call(s32[1]{0:T(128)} %bitcast.27.dp_ref, bf16[256,1024]{1,0:T(8,128)(2,1)S(1)} %copy-done.14, bf16[256,1024]{1,0:T(8,128)(2,1)S(1)} %attend.1.refs_1_, bf16[256,3072]{1,0:T(8,128)(2,1)S(1)} %copy-done.9, ...), custom_call_target="tpu_custom_call" | custom-call | tf_op jit(solution)/shard_map/outer/pallas_call | solution.py:274
  271.8 4.2 %all-to-all-start.2 = ((bf16[32,160,128]{2,1,0:T(8,128)(2,1)}), bf16[32,160,128]{2,1,0:T(8,128)(2,1)}, u32[]{:S(2)}, u32[]{:S(2)}) async-start(bf16[32,160,128]{2,1,0:T(8,128)(2,1)} %fusion.10), calls=%async_computation.2 | async-start | bytes 2621440 | tf_op jit(solution)/shard_map/all_to_all | solution.py:706
  277.2 13.1 %collective-permute-done.44 = bf16[128,4096]{1,0:T(8,128)(2,1)} collective-permute-done((bf16[128,4096]{1,0:T(8,128)(2,1)}, bf16[128,4096]{1,0:T(8,128)(2,1)}, u32[]{:S(2)}, u32[]{:S(2)}) %collective-permute-start.44) | collective-permute-done | bytes 1048608 | tf_op jit(solution)/shard_map/ppermute | solution.py:38
  294.9 9.2 %collective-permute-done.43 = bf16[2,128,4096]{2,1,0:T(8,128)(2,1)} collective-permute-done((bf16[2,128,4096]{2,1,0:T(8,128)(2,1)}, bf16[2,128,4096]{2,1,0:T(8,128)(2,1)}, u32[]{:S(2)}, u32[]{:S(2)}) %collective-permute-start.43) | collective-permute-done | bytes 2097184 | tf_op jit(solution)/shard_map/ppermute | solution.py:38
  316.6 5.1 %collective-permute-done.45 = bf16[128,4096]{1,0:T(8,128)(2,1)} collective-permute-done((bf16[128,4096]{1,0:T(8,128)(2,1)}, bf16[128,4096]{1,0:T(8,128)(2,1)}, u32[]{:S(2)}, u32[]{:S(2)}) %collective-permute-start.45) | collective-permute-done | bytes 1048608 | tf_op jit(solution)/shard_map/ppermute | solution.py:38
  329.7 10.5 %collective-permute-done.46 = bf16[2,32,4096]{2,1,0:T(8,128)(2,1)S(1)} collective-permute-done((bf16[2,32,4096]{2,1,0:T(8,128)(2,1)S(1)}, bf16[2,32,4096]{2,1,0:T(8,128)(2,1)S(1)}, u32[]{:S(2)}, u32[]{:S(2)}) %collective-permute-start.46) | collective-permute-done | bytes 524320 | tf_op jit(solution)/shard_map/ppermute | solution.py:41
  345.5 7.6 %collective-permute-done.48 = bf16[32,4096]{1,0:T(8,128)(2,1)S(1)} collective-permute-done((bf16[32,4096]{1,0:T(8,128)(2,1)S(1)}, bf16[32,4096]{1,0:T(8,128)(2,1)S(1)}, u32[]{:S(2)}, u32[]{:S(2)}) %collective-permute-start.48) | collective-permute-done | bytes 262176 | tf_op jit(solution)/shard_map/ppermute | solution.py:41
  (364 shorter events, 176.1 us)
Async XLA Ops:
  18.7 19.3 %collective-permute-start.1 = (bf16[32,4096]{1,0:T(8,128)(2,1)}, bf16[32,4096]{1,0:T(8,128)(2,1)S(1)}, u32[]{:S(2)}, u32[]{:S(2)}) collective-permute-start(bf16[32,4096]{1,0:T(8,128)(2,1)} %param.28), channel_id=1, source_target_pairs={{0,2},{1,3},{2,0},{3,1},{4,6},{5,7},{6,4},{7,5},{8,10},{9,11},{10,... | collective-permute-start | bytes 786440 | tf_op jit(solution)/shard_map/ppermute | solution.py:41
  36.7 19.4 %collective-permute-start.3 = (bf16[128,4096]{1,0:T(8,128)(2,1)S(1)}, bf16[128,4096]{1,0:T(8,128)(2,1)S(1)}, u32[]{:S(2)}, u32[]{:S(2)}) collective-permute-start(bf16[128,4096]{1,0:T(8,128)(2,1)S(1)} %constant_dynamic-update-slice_fusion.2.refs_0_), channel_id=1, source_target_pairs={{0,8},{4,20},{8,0},{12,28},{16,24},{20,4},{24,16},{28,12},{1,9},{5... | collective-permute-start | bytes 3145736 | tf_op jit(solution)/shard_map/ppermute | solution.py:38
  41.1 26.7 %all-to-all-start = ((bf16[32,88,128]{2,1,0:T(8,128)(2,1)}), bf16[32,88,128]{2,1,0:T(8,128)(2,1)S(1)}, u32[]{:S(2)}, u32[]{:S(2)}) async-start(bf16[32,88,128]{2,1,0:T(8,128)(2,1)} %pad_maximum_fusion), calls=%async_computation | async-start | bytes 1441792 | tf_op jit(solution)/shard_map/all_to_all | solution.py:706
  47.1 23.8 %collective-permute-start.6 = (bf16[128,4096]{1,0:T(8,128)(2,1)S(1)}, bf16[128,4096]{1,0:T(8,128)(2,1)}, u32[]{:S(2)}, u32[]{:S(2)}) collective-permute-start(bf16[128,4096]{1,0:T(8,128)(2,1)S(1)} %constant_dynamic-update-slice_fusion.2.refs_0_), channel_id=1, source_target_pairs={{0,16},{4,12},{8,24},{12,4},{16,0},{20,28},{24,8},{28,20},{1,17},{... | collective-permute-start | bytes 3145736 | tf_op jit(solution)/shard_map/ppermute | solution.py:38
  57.0 23.2 %collective-permute-start.10 = (bf16[64,4096]{1,0:T(8,128)(2,1)S(1)}, bf16[64,4096]{1,0:T(8,128)(2,1)}, u32[]{:S(2)}, u32[]{:S(2)}) collective-permute-start(bf16[64,4096]{1,0:T(8,128)(2,1)S(1)} %constant_dynamic-update-slice_fusion.4), channel_id=1, source_target_pairs={{0,1},{1,0},{2,3},{3,2},{4,5},{5,4},{6,7},{7,6},{8,9},{9,8},{10,11... | collective-permute-start | bytes 1572872 | tf_op jit(solution)/shard_map/ppermute | solution.py:41
  59.1 24.3 %collective-permute-start.9 = (bf16[128,1024]{1,0:T(8,128)(2,1)}, bf16[128,1024]{1,0:T(8,128)(2,1)}, u32[]{:S(2)}, u32[]{:S(2)}) collective-permute-start(bf16[128,1024]{1,0:T(8,128)(2,1)} %param.30), channel_id=1, source_target_pairs={{0,2},{1,3},{2,0},{3,1},{4,6},{5,7},{6,4},{7,5},{8,10},{9,11},{10,... | collective-permute-start | bytes 786440 | tf_op jit(solution)/shard_map/ppermute | solution.py:41
  66.3 19.5 %collective-permute-start.5 = (bf16[128,4096]{1,0:T(8,128)(2,1)S(1)}, bf16[128,4096]{1,0:T(8,128)(2,1)}, u32[]{:S(2)}, u32[]{:S(2)}) collective-permute-start(bf16[128,4096]{1,0:T(8,128)(2,1)S(1)} %collective-permute-done.3.refs_2_), channel_id=1, source_target_pairs={{0,16},{4,12},{8,24},{12,4},{16,0},{20,28},{24,8},{28,20},{1,17},{... | collective-permute-start | bytes 3145736 | tf_op jit(solution)/shard_map/ppermute | solution.py:38
  81.3 25.5 %collective-permute-start.13 = (bf16[128,4096]{1,0:T(8,128)(2,1)S(1)}, bf16[128,4096]{1,0:T(8,128)(2,1)S(1)}, u32[]{:S(2)}, u32[]{:S(2)}) collective-permute-start(bf16[128,4096]{1,0:T(8,128)(2,1)S(1)} %constant_dynamic-update-slice_fusion.6.refs_0_), channel_id=1, source_target_pairs={{0,8},{4,20},{8,0},{12,28},{16,24},{20,4},{24,16},{28,12},{1,9},{5... | collective-permute-start | bytes 3145736 | tf_op jit(solution)/shard_map/ppermute | solution.py:38
  83.3 23.5 %collective-permute-start.14 = (bf16[128,4096]{1,0:T(8,128)(2,1)S(1)}, bf16[128,4096]{1,0:T(8,128)(2,1)S(1)}, u32[]{:S(2)}, u32[]{:S(2)}) collective-permute-start(bf16[128,4096]{1,0:T(8,128)(2,1)S(1)} %constant_dynamic-update-slice_fusion.6.refs_0_), channel_id=1, source_target_pairs={{0,4},{4,0},{8,12},{12,8},{16,20},{20,16},{24,28},{28,24},{1,5},{5... | collective-permute-start | bytes 3145736 | tf_op jit(solution)/shard_map/ppermute | solution.py:34
  83.3 26.4 %collective-permute-start.12 = (bf16[128,4096]{1,0:T(8,128)(2,1)S(1)}, bf16[128,4096]{1,0:T(8,128)(2,1)S(1)}, u32[]{:S(2)}, u32[]{:S(2)}) collective-permute-start(bf16[128,4096]{1,0:T(8,128)(2,1)S(1)} %constant_dynamic-update-slice_fusion.6.refs_0_), channel_id=1, source_target_pairs={{0,16},{4,12},{8,24},{12,4},{16,0},{20,28},{24,8},{28,20},{1,17},{... | collective-permute-start | bytes 3145736 | tf_op jit(solution)/shard_map/ppermute | solution.py:38
  108.4 21.6 %collective-permute-start.17 = (bf16[128,4096]{1,0:T(8,128)(2,1)S(1)}, bf16[128,4096]{1,0:T(8,128)(2,1)}, u32[]{:S(2)}, u32[]{:S(2)}) collective-permute-start(bf16[128,4096]{1,0:T(8,128)(2,1)S(1)} %collective-permute-done.13.refs_2_), channel_id=1, source_target_pairs={{0,16},{4,12},{8,24},{12,4},{16,0},{20,28},{24,8},{28,20},{1,17},{... | collective-permute-start | bytes 3145736 | tf_op jit(solution)/shard_map/ppermute | solution.py:38
  113.1 40.2 %collective-permute-start.20 = (bf16[512,1024]{1,0:T(8,128)(2,1)}, bf16[512,1024]{1,0:T(8,128)(2,1)}, u32[]{:S(2)}, u32[]{:S(2)}) collective-permute-start(bf16[512,1024]{1,0:T(8,128)(2,1)} %constant_dynamic-update-slice_fusion.10.refs_0_), channel_id=1, source_target_pairs={{0,8},{4,20},{8,0},{12,28},{16,24},{20,4},{24,16},{28,12},{1,9},{5... | collective-permute-start | bytes 3145736 | tf_op jit(solution)/shard_map/ppermute | solution.py:38
  115.7 37.6 %collective-permute-start.21 = (bf16[512,1024]{1,0:T(8,128)(2,1)}, bf16[512,1024]{1,0:T(8,128)(2,1)}, u32[]{:S(2)}, u32[]{:S(2)}) collective-permute-start(bf16[512,1024]{1,0:T(8,128)(2,1)} %constant_dynamic-update-slice_fusion.10.refs_0_), channel_id=1, source_target_pairs={{0,4},{4,0},{8,12},{12,8},{16,20},{20,16},{24,28},{28,24},{1,5},{5... | collective-permute-start | bytes 3145736 | tf_op jit(solution)/shard_map/ppermute | solution.py:34
  115.7 43.4 %collective-permute-start.19 = (bf16[512,1024]{1,0:T(8,128)(2,1)}, bf16[512,1024]{1,0:T(8,128)(2,1)}, u32[]{:S(2)}, u32[]{:S(2)}) collective-permute-start(bf16[512,1024]{1,0:T(8,128)(2,1)} %constant_dynamic-update-slice_fusion.10.refs_0_), channel_id=1, source_target_pairs={{0,16},{4,12},{8,24},{12,4},{16,0},{20,28},{24,8},{28,20},{1,17},{... | collective-permute-start | bytes 3145736 | tf_op jit(solution)/shard_map/ppermute | solution.py:38
  134.3 23.4 %all-to-all-start.1 = ((bf16[32,72,128]{2,1,0:T(8,128)(2,1)}), bf16[32,72,128]{2,1,0:T(8,128)(2,1)}, u32[]{:S(2)}, u32[]{:S(2)}) async-start(bf16[32,72,128]{2,1,0:T(8,128)(2,1)} %reshape.379), calls=%async_computation.1 | async-start | bytes 1179648 | tf_op jit(solution)/shard_map/all_to_all | solution.py:706
  185.8 26.9 %collective-permute-start.31 = (bf16[2,512,1024]{2,1,0:T(8,128)(2,1)}, bf16[2,512,1024]{2,1,0:T(8,128)(2,1)}, u32[]{:S(2)}, u32[]{:S(2)}) collective-permute-start(bf16[2,512,1024]{2,1,0:T(8,128)(2,1)} %get-tuple-element.271), channel_id=1, source_target_pairs={{0,16},{4,12},{8,24},{12,4},{16,0},{20,28},{24,8},{28,20},{1,17},{... | collective-permute-start | bytes 6291464 | tf_op jit(solution)/shard_map/ppermute | solution.py:38
  211.6 44.3 %collective-permute-start.37 = (bf16[2,128,4096]{2,1,0:T(8,128)(2,1)}, bf16[2,128,4096]{2,1,0:T(8,128)(2,1)}, u32[]{:S(2)}, u32[]{:S(2)}) collective-permute-start(bf16[2,128,4096]{2,1,0:T(8,128)(2,1)} %get-tuple-element.287), channel_id=1, source_target_pairs={{0,16},{4,12},{8,24},{12,4},{16,0},{20,28},{24,8},{28,20},{1,17},{... | collective-permute-start | bytes 6291464 | tf_op jit(solution)/shard_map/ppermute | solution.py:38
  235.3 23.2 %collective-permute-start.36 = (bf16[512,1024]{1,0:T(8,128)(2,1)}, bf16[512,1024]{1,0:T(8,128)(2,1)}, u32[]{:S(2)}, u32[]{:S(2)}) collective-permute-start(bf16[512,1024]{1,0:T(8,128)(2,1)} %fusion.8), channel_id=1, source_target_pairs={{0,8},{4,20},{8,0},{12,28},{16,24},{20,4},{24,16},{28,12},{1,9},{5... | collective-permute-start | bytes 3145736 | tf_op jit(solution)/shard_map/ppermute | solution.py:38
  254.3 49.9 %collective-permute-start.43 = (bf16[2,128,4096]{2,1,0:T(8,128)(2,1)}, bf16[2,128,4096]{2,1,0:T(8,128)(2,1)}, u32[]{:S(2)}, u32[]{:S(2)}) collective-permute-start(bf16[2,128,4096]{2,1,0:T(8,128)(2,1)} %get-tuple-element.317), channel_id=1, source_target_pairs={{0,16},{4,12},{8,24},{12,4},{16,0},{20,28},{24,8},{28,20},{1,17},{... | collective-permute-start | bytes 6291464 | tf_op jit(solution)/shard_map/ppermute | solution.py:38
  258.5 31.8 %collective-permute-start.44 = (bf16[128,4096]{1,0:T(8,128)(2,1)}, bf16[128,4096]{1,0:T(8,128)(2,1)}, u32[]{:S(2)}, u32[]{:S(2)}) collective-permute-start(bf16[128,4096]{1,0:T(8,128)(2,1)} %fusion.7), channel_id=1, source_target_pairs={{0,8},{4,20},{8,0},{12,28},{16,24},{20,4},{24,16},{28,12},{1,9},{5... | collective-permute-start | bytes 3145736 | tf_op jit(solution)/shard_map/ppermute | solution.py:38
  261.8 44.9 %collective-permute-start.42 = (bf16[2,128,1024]{2,1,0:T(8,128)(2,1)}, bf16[2,128,1024]{2,1,0:T(8,128)(2,1)S(1)}, u32[]{:S(2)}, u32[]{:S(2)}) collective-permute-start(bf16[2,128,1024]{2,1,0:T(8,128)(2,1)} %fusion.18), channel_id=1, source_target_pairs={{0,1},{1,0},{2,3},{3,2},{4,5},{5,4},{6,7},{7,6},{8,9},{9,8},{10,11... | collective-permute-start | bytes 1572872 | tf_op jit(solution)/shard_map/ppermute | solution.py:41
  271.8 37.1 %all-to-all-start.2 = ((bf16[32,160,128]{2,1,0:T(8,128)(2,1)}), bf16[32,160,128]{2,1,0:T(8,128)(2,1)}, u32[]{:S(2)}, u32[]{:S(2)}) async-start(bf16[32,160,128]{2,1,0:T(8,128)(2,1)} %fusion.10), calls=%async_computation.2 | async-start | bytes 2621440 | tf_op jit(solution)/shard_map/all_to_all | solution.py:706
  293.1 32.5 %collective-permute-start.47 = (bf16[2,32,4096]{2,1,0:T(8,128)(2,1)}, bf16[2,32,4096]{2,1,0:T(8,128)(2,1)}, u32[]{:S(2)}, u32[]{:S(2)}) collective-permute-start(bf16[2,32,4096]{2,1,0:T(8,128)(2,1)} %fusion.19), channel_id=1, source_target_pairs={{0,1},{1,0},{2,3},{3,2},{4,5},{5,4},{6,7},{7,6},{8,9},{9,8},{10,11... | collective-permute-start | bytes 1572872 | tf_op jit(solution)/shard_map/ppermute | solution.py:41
  307.5 35.3 %collective-permute-start.50 = (bf16[128,1024]{1,0:T(8,128)(2,1)}, bf16[128,1024]{1,0:T(8,128)(2,1)S(1)}, u32[]{:S(2)}, u32[]{:S(2)}) collective-permute-start(bf16[128,1024]{1,0:T(8,128)(2,1)} %fusion.25), channel_id=1, source_target_pairs={{0,2},{1,3},{2,0},{3,1},{4,6},{5,7},{6,4},{7,5},{8,10},{9,11},{10,... | collective-permute-start | bytes 786440 | tf_op jit(solution)/shard_map/ppermute | solution.py:41
  (97 other events, 892.5 us)
where the time goes:
time: 356 us; the launch traced here: 355 us
  waiting for transfers between devices  106 us (30%)
  starting transfers between devices  71.7 us (20%)
  Pallas kernels  67.2 us (19%)
  local copies, waits for them, and re-layouts  53.9 us (15%)
  other arithmetic  34.5 us (10%)
  matrix products  19.2 us (5%)
    ppermute x12, waiting for transfers between devices, over_z(): return lax.ppermute(value, 'fsdp', [(i, i ^ mask) for i in range(self.n_z)])  55.1 us
    ppermute x15, waiting for transfers between devices, crossed(): return lax.ppermute(value, 'dp', pairs)  42.7 us
    pallas_call x6, Pallas kernels, call(): pl.pallas_call(whole_kernel, out_shape=shapes, grid_spec=pltpu.PrefetchSc...  28.5 us
    ppermute x12, starting transfers between devices, over_z(): return lax.ppermute(value, 'fsdp', [(i, i ^ mask) for i in range(self.n_z)])  25.6 us
    unnamed x148, local copies, waits for them, and re-layouts  23.2 us
    ppermute x15, starting transfers between devices, crossed(): return lax.ppermute(value, 'dp', pairs)  21.8 us
    all_to_all x3, starting transfers between devices, swap(): block = lax.all_to_all(block, AXES, split_axis=0, concat_axis=0, tiled=True)  18.1 us
    pallas_call x2, Pallas kernels, norm_back(): pl.pallas_call(kernel, out_shape=[jax.ShapeDtypeStruct(*s) for s in shape...  12.8 us
  transfers between devices with their start and end apart: 54, of which 16 were waited for; matrix products, arithmetic and copies ran while one was open for 23% of the time, Pallas kernels for 18%

commit v1 on v0

--- a/solution.py
+++ b/solution.py
@@ -246,18 +246,13 @@
         self.chunk = lefts[0].shape[1] // grid.n_dp
         self.cols = sum(right.shape[1] for right in rights)
         once = pl.Buffered(1)
-        self.whole = pl.BlockSpec(
-            (self.chunk, self.cols), lambda j, dp: (0, 0), pipeline_mode=once
-        )
         self.rows = [
             pl.BlockSpec(right.shape, lambda j, dp: (0, 0), pipeline_mode=once) for right in rights
         ]
 
-    def shape(self, dtype):
-        return jax.ShapeDtypeStruct((self.chunk, self.cols), dtype)
-
-    def call(self, kernel, other, ins, shapes, specs):
-        tokens, count = self.lefts[0].shape[0], len(self.lefts)
+    def call(self, other, ins, shapes, targets):
+        tokens, count, places = self.lefts[0].shape[0], len(self.lefts), self.places
+        added = len(ins)
 
         def place(j, dp):
             a, b = j // 2, j % 2
@@ -265,64 +260,84 @@
             mask = jnp.where(odd == 1, 2 * a + 4 * b, 4 * a + 2 * b)
             return 0, lax.bitwise_xor(dp[0], mask + other)
 
-        def whole_kernel(dp_ref, *refs):
-            lefts, rights, rest = refs[:count], refs[count : 2 * count], refs[2 * count :]
+        def kernel(dp_ref, *refs):
+            lefts, rights, refs = refs[:count], refs[count : 2 * count], refs[2 * count :]
+            gots, outs = refs[:added], refs[added : added + len(shapes)]
+            blocks, out_sems, *fetched = refs[added + len(shapes) :]
+            step = pl.program_id(0)
+
+            def fetch(k):
+                return pltpu.make_async_copy(gots[k], fetched[0].at[k], fetched[1].at[k])
+
+            def put(k):
+                return pltpu.make_async_copy(blocks.at[k], targets(outs)[k], out_sems.at[k])
+
+            if added:
+
+                @pl.when(step == 0)
+                def _():
+                    for k in range(places):
+                        fetch(k).start()
+
             terms = [contract_rows(a[...], b[...]) for a, b in zip(lefts, rights)]
-            kernel(jnp.concatenate(terms, axis=1) if count > 1 else terms[0], *rest)
-
+            term = jnp.concatenate(terms, axis=1) if count > 1 else terms[0]
+            for k in range(places):
+
+                @pl.when(step == k)
+                def _(k=k):
+                    whole = term
+                    if added:
+                        fetch(k).wait()
+                        whole = whole + fetched[0][k].astype(F32)
+                    blocks[k] = whole.astype(BF16)
+                    put(k).start()
+
+            @pl.when(step == places - 1)
+            def _():
+                for k in range(places):
+                    put(k).wait()
+
+        anywhere = pl.BlockSpec(memory_space=pl.ANY)
+        scratch = [
+            pltpu.VMEM((places, self.chunk, self.cols), BF16),
+            pltpu.SemaphoreType.DMA((places,)),
+        ]
         ins = self.clock.gate(*self.lefts, *self.rights, *ins)
         return pl.pallas_call(
-            whole_kernel,
+            kernel,
             out_shape=shapes,
             grid_spec=pltpu.PrefetchScalarGridSpec(
                 num_scalar_prefetch=1,
-                grid=(self.places,),
+                grid=(places,),
                 in_specs=[
                     *[pl.BlockSpec((tokens, self.chunk), place) for _ in self.lefts],
                     *self.rows,
-                    *[self.whole for _ in ins[2 * count :]],
+                    *[anywhere] * added,
                 ],
-                out_specs=specs,
+                out_specs=[anywhere] * len(shapes),
+                scratch_shapes=scratch * (2 if added else 1),
             ),
-            compiler_params=pltpu.CompilerParams(vmem_limit_bytes=18 << 20),
+            compiler_params=pltpu.CompilerParams(vmem_limit_bytes=20 << 20),
             cost_estimate=pl.CostEstimate(flops=0, bytes_accessed=0, transcendentals=0),
             name="outer",
         )(self.grid.my_dp.reshape(1), *ins)
 
     def across(self):
-        def kernel(term, *outs):
-            term = term.astype(BF16)
-            for k, out in enumerate(outs):
-
-                @pl.when(pl.program_id(0) == k)
-                def _(out=out):
-                    out[...] = term
-
-        shapes = [self.shape(BF16)] * self.places
-        sends = self.call(kernel, 1, (), shapes, [self.whole] * self.places)
+        shapes = [jax.ShapeDtypeStruct((self.chunk, self.cols), BF16)] * self.places
+        sends = self.call(1, (), shapes, lambda outs: outs)
         self.clock.tick(*sends)
         self.got = [self.grid.over_dp(v, 1) for v in sends]
 
     def first(self):
-        grid, places = self.grid, self.places
+        grid = self.grid
         (x,), (y,) = grid.x_masks, grid.y_masks
-
-        def kernel(term, *refs):
-            got, (keep, pass_on, far) = refs[:places], refs[places:]
-            outs = (keep, pass_on, far.at[0], far.at[1])
-            for k in range(places):
-
-                @pl.when(pl.program_id(0) == k)
-                def _(k=k):
-                    outs[k][...] = (term + got[k][...].astype(F32)).astype(outs[k].dtype)
-
-        wide = self.shape(F32)
-        pair = jax.ShapeDtypeStruct((2, *wide.shape), BF16)
-        pair_spec = pl.BlockSpec(
-            pair.shape, lambda j, dp: (0, 0, 0), pipeline_mode=pl.Buffered(1)
-        )
+        one = jax.ShapeDtypeStruct((self.chunk, self.cols), BF16)
+        pair = jax.ShapeDtypeStruct((2, self.chunk, self.cols), BF16)
         keep, pass_on, far = self.call(
-            kernel, 0, self.got, [wide, wide, pair], [self.whole, self.whole, pair_spec]
+            0,
+            self.got,
+            [one, one, pair],
+            lambda outs: (outs[0], outs[1], outs[2].at[0], outs[2].at[1]),
         )
         self.clock.tick(far)
         self.keep, self.pass_on = keep, pass_on
@@ -331,7 +346,7 @@
     def second(self):
         (x,), (y,) = self.grid.x_masks, self.grid.y_masks
         got, pass_on = self.clock.gate(self.got, self.pass_on)
-        send = (pass_on + got[1].astype(F32)).astype(BF16)
+        send = (pass_on.astype(F32) + got[1].astype(F32)).astype(BF16)
         self.clock.tick(send)
         self.aside = got[0]
         self.got = self.grid.crossed(send, x, y)
@@ -343,7 +358,7 @@
     def third(self):
         grid = self.grid
         got, keep = self.clock.gate(self.got, self.keep)
-        lines = total_of(keep, [got, self.aside]).reshape(2, 2, -1, self.cols)
+        lines = total_of(keep.astype(F32), [got, self.aside]).reshape(2, 2, -1, self.cols)
         odd = grid.my_z % 2
         send = lax.dynamic_index_in_dim(lines, 1 - odd, 1, keepdims=False).astype(BF16)
         self.keep = lax.dynamic_index_in_dim(lines, odd, 1, keepdims=False)
@@ -731,14 +746,13 @@
     (attn,) = early.step2()
     attn.step0()
     middle.step1()
-    late.step0()
     small = jnp.broadcast_to(small[None], (devices, *small.shape))
     arrived, small_all = swap(clock.gate(block), small)
     attn.step1()
     attn.step2()
     (up,) = middle.step2()
     up.step0()
-    late.step1()
+    late.step0()
     attn.step3()
     arrived, small_all = clock.gate(arrived, small_all)
     inputs = jnp.dot(from_slots, arrived, preferred_element_type=F32)
@@ -751,22 +765,28 @@
     unit_one, scale_one = standardize(inputs)
     normed_one_b = (unit_one * g1 + s1).astype(BF16)
     clock.tick(normed_one_b)
+    cot_block = contract_rows(to_slots, clock.gate(cotangent).reshape(row_count, width))
+    cot_block = cot_block.astype(BF16)
+    clock.tick(cot_block)
+    arrived_cot = swap(cot_block)
+    late.step1()
     take_both, send_both = clock.gate(take_both, send_both)
     clock.tick(take_both, send_both)
-    (down,) = late.step2()
     up.step1()
     up.step2()
+    (down,) = late.step2()
     down.step0()
     full_qkv, full_out = attn.done((3 * width,))
     mixed = jnp.dot(clock.gate(normed_one_b), full_qkv, preferred_element_type=F32)
     mixed_b = (mixed + jnp.concatenate([bq, jnp.zeros_like(bq), bv], axis=1)).astype(BF16)
     attended_b = attend(first_len, mixed_b)
     clock.tick(attended_b)
+    arrived_cot = clock.gate(arrived_cot)
+    grad_m_b = jnp.dot(from_slots, arrived_cot, preferred_element_type=F32)
+    grad_m_b = grad_m_b.astype(BF16)
+    clock.tick(grad_m_b)
     up.step3()
-    attended_b, cot_rows = clock.gate(attended_b, cotangent)
-    cot_block = contract_rows(to_slots, cot_rows.reshape(row_count, width)).astype(BF16)
-    clock.tick(cot_block)
-    arrived_cot = swap(cot_block)
+    attended_b = clock.gate(attended_b)
     hidden_one = inputs + jnp.dot(attended_b, full_out, preferred_element_type=F32) + bo
     unit_two, scale_two = standardize(hidden_one)
     normed_two_b = (unit_two * g2 + s2).astype(BF16)
@@ -782,10 +802,6 @@
     slope = half_cdf + pre_act * density
     clock.tick(activation_b, slope)
 
-    arrived_cot = clock.gate(arrived_cot)
-    grad_m_b = jnp.dot(from_slots, arrived_cot, preferred_element_type=F32)
-    grad_m_b = grad_m_b.astype(BF16)
-    clock.tick(grad_m_b)
     term_b_down = col_sum(grad_m_b)[None, :]
     for_down = make_scatter(grid, clock, (activation_b, grad_m_b))
     for_down.across()

time: 356 us -> 354 us (level); the launches traced: 355 us -> 348 us
  waiting for transfers between devices: 106 us -> 112 us
  local copies, waits for them, and re-layouts: 53.9 us -> 48.2 us
  starting transfers between devices: 71.7 us -> 66.1 us
    ppermute x15, waiting for transfers between devices: 42.7 us -> 58 us  [crossed(): return lax.ppermute(value, 'dp', pairs)]
    unnamed x148 -> x136, local copies, waits for them, and re-layouts: 23.2 us -> 16.3 us
    ppermute x12, waiting for transfers between devices: 55.1 us -> 49.4 us  [over_z(): return lax.ppermute(value, 'fsdp', [(i, i ^ mask) for i in range(self.n_z)])]
    pallas_call x6, Pallas kernels: 28.5 us -> 24.2 us  [call(): pl.pallas_call(kernel, out_shape=shapes, grid_spec=pltpu.PrefetchScalarGr...]
  transfers between devices with their start and end apart: 54 -> 54, of which waited for: 16 -> 17; matrix products, arithmetic and copies ran while one was open for 23% -> 25% of each run, Pallas kernels for 18% -> 17%
where the time goes in v1:
time: 354 us; the launch traced here: 348 us
  waiting for transfers between devices  112 us (32%)
  starting transfers between devices  66.1 us (19%)
  Pallas kernels  63.8 us (18%)
  local copies, waits for them, and re-layouts  48.2 us (14%)
  other arithmetic  36 us (10%)
  matrix products  19.3 us (5%)
    ppermute x15, waiting for transfers between devices, crossed(): return lax.ppermute(value, 'dp', pairs)  58 us
    ppermute x12, waiting for transfers between devices, over_z(): return lax.ppermute(value, 'fsdp', [(i, i ^ mask) for i in range(self.n_z)])  49.4 us
    pallas_call x6, Pallas kernels, call(): pl.pallas_call(kernel, out_shape=shapes, grid_spec=pltpu.PrefetchScalarGr...  24.2 us
    ppermute x12, starting transfers between devices, over_z(): return lax.ppermute(value, 'fsdp', [(i, i ^ mask) for i in range(self.n_z)])  23.7 us
    ppermute x15, starting transfers between devices, crossed(): return lax.ppermute(value, 'dp', pairs)  20.2 us
    all_to_all x3, starting transfers between devices, swap(): block = lax.all_to_all(block, AXES, split_axis=0, concat_axis=0, tiled=True)  16.9 us
    unnamed x136, local copies, waits for them, and re-layouts  16.3 us
    pallas_call x2, Pallas kernels, norm_back(): pl.pallas_call(kernel, out_shape=[jax.ShapeDtypeStruct(*s) for s in shape...  12.7 us
  transfers between devices with their start and end apart: 54, of which 17 were waited for; matrix products, arithmetic and copies ran while one was open for 25% of the time, Pallas kernels for 17%

profile of v1, /device:TPU:0, one launch (start us, length us, event | category | flops | bytes accessed | tf_op | source)
XLA Modules:
  0.0 347.8 jit_solution(14141038721162004489)
XLA Ops:
  1.7 4.1 %collective-permute-start = (bf16[32,4096]{1,0:T(8,128)(2,1)S(1)}, bf16[32,4096]{1,0:T(8,128)(2,1)S(1)}, u32[]{:S(2)}, u32[]{:S(2)}) collective-permute-start(bf16[32,4096]{1,0:T(8,128)(2,1)S(1)} %pad_maximum_fusion.1), channel_id=1, source_target_pairs={{0,2},{1,3},{2,0},{3,1},{4,6},{5,7},{6,4},{7,5},{8,10},{9,11},{10,... | collective-permute-start | bytes 786440 | tf_op jit(solution)/shard_map/ppermute | solution.py:41
  23.3 13.3 %collective-permute-done.2 = bf16[64,4096]{1,0:T(8,128)(2,1)S(1)} collective-permute-done((bf16[64,4096]{1,0:T(8,128)(2,1)S(1)}, bf16[64,4096]{1,0:T(8,128)(2,1)S(1)}, u32[]{:S(2)}, u32[]{:S(2)}) %collective-permute-start.2) | collective-permute-done | bytes 524320 | tf_op jit(solution)/shard_map/ppermute | solution.py:41
  43.6 6.1 %all-to-all-start = ((bf16[32,88,128]{2,1,0:T(8,128)(2,1)}), bf16[32,88,128]{2,1,0:T(8,128)(2,1)}, u32[]{:S(2)}, u32[]{:S(2)}) async-start(bf16[32,88,128]{2,1,0:T(8,128)(2,1)} %pad_maximum_fusion), calls=%async_computation | async-start | bytes 1441792 | tf_op jit(solution)/shard_map/all_to_all | solution.py:721
  56.3 15.2 %collective-permute-done.4.refs_4_ = bf16[128,4096]{1,0:T(8,128)(2,1)} collective-permute-done((bf16[128,4096]{1,0:T(8,128)(2,1)S(1)}, bf16[128,4096]{1,0:T(8,128)(2,1)}, u32[]{:S(2)}, u32[]{:S(2)}) %collective-permute-start.4) | collective-permute-done | bytes 1048608 | tf_op jit(solution)/shard_map/ppermute | solution.py:38
  88.8 9.0 %collective-permute-done.8 = bf16[128,1024]{1,0:T(8,128)(2,1)S(1)} collective-permute-done((bf16[128,1024]{1,0:T(8,128)(2,1)S(1)}, bf16[128,1024]{1,0:T(8,128)(2,1)S(1)}, u32[]{:S(2)}, u32[]{:S(2)}) %collective-permute-start.8) | collective-permute-done | bytes 262176 | tf_op jit(solution)/shard_map/ppermute | solution.py:41
  97.8 8.2 %collective-permute-done.14.refs_2_ = bf16[128,4096]{1,0:T(8,128)(2,1)} collective-permute-done((bf16[128,4096]{1,0:T(8,128)(2,1)S(1)}, bf16[128,4096]{1,0:T(8,128)(2,1)}, u32[]{:S(2)}, u32[]{:S(2)}) %collective-permute-start.14) | collective-permute-done | bytes 1048608 | tf_op jit(solution)/shard_map/ppermute | solution.py:38
  113.4 4.2 %all-to-all-start.1 = ((bf16[32,72,128]{2,1,0:T(8,128)(2,1)}), bf16[32,72,128]{2,1,0:T(8,128)(2,1)}, u32[]{:S(2)}, u32[]{:S(2)}) async-start(bf16[32,72,128]{2,1,0:T(8,128)(2,1)} %reshape.379), calls=%async_computation.1 | async-start | bytes 1179648 | tf_op jit(solution)/shard_map/all_to_all | solution.py:721
  118.1 5.5 %collective-permute-done.12 = bf16[256,1024]{1,0:T(8,128)(2,1)} collective-permute-done((bf16[256,1024]{1,0:T(8,128)(2,1)S(1)}, bf16[256,1024]{1,0:T(8,128)(2,1)}, u32[]{:S(2)}, u32[]{:S(2)}) %collective-permute-start.12) | collective-permute-done | bytes 524320 | tf_op jit(solution)/shard_map/ppermute | solution.py:41
  131.1 4.2 %assemble.3 = (bf16[1024,3072]{1,0:T(8,128)(2,1)S(1)}, bf16[1024,1024]{1,0:T(8,128)(2,1)S(1)}) custom-call(s32[1]{0:T(128)} %bitcast.19.me_ref, bf16[128,4096]{1,0:T(8,128)(2,1)S(1)} %constant_dynamic-update-slice_fusion.2.refs_0_, bf16[128,4096]{1,0:T(8,128)(2,1)S(1)} %copy-done.31, bf16[128,4096]{1,0:T(8,128)(2,1)S(1)} %copy-done.29, ...), custom_call_target="tpu_custom_call" | custom-call | tf_op jit(solution)/shard_map/assemble/pallas_call | solution.py:172
  157.9 4.4 %fusion.3 = (f32[256,4096]{1,0:T(8,128)S(1)}, bf16[256,4096]{1,0:T(8,128)(2,1)S(1)}) fusion(f32[4096]{0:T(1024)S(1)} %bitcast.179, bf16[256,1024]{1,0:T(8,128)(2,1)S(1)} %get-tuple-element.281.refs_0_, bf16[1024,4096]{1,0:T(8,128)(2,1)S(1)} %assemble.4.weight), kind=kOutput, calls=%fused_computation.5 | convolution fusion | flops 2159017984 | bytes 15220736 | tf_op jit(solution)/shard_map/dot_general | solution.py:798
  165.2 4.8 %collective-permute-done.24.refs_6_ = bf16[512,1024]{1,0:T(8,128)(2,1)S(1)} collective-permute-done((bf16[512,1024]{1,0:T(8,128)(2,1)}, bf16[512,1024]{1,0:T(8,128)(2,1)S(1)}, u32[]{:S(2)}, u32[]{:S(2)}) %collective-permute-start.24) | collective-permute-done | bytes 1048608 | tf_op jit(solution)/shard_map/ppermute | solution.py:38
  178.8 4.3 %outer.7 = (bf16[512,1024]{1,0:T(8,128)(2,1)S(1)}, bf16[512,1024]{1,0:T(8,128)(2,1)S(1)}, bf16[2,512,1024]{2,1,0:T(8,128)(2,1)}) custom-call(s32[1]{0:T(128)} %bitcast.26.dp_ref, bf16[256,4096]{1,0:T(8,128)(2,1)S(1)} %get-tuple-element.322.refs_0_, bf16[256,1024]{1,0:T(8,128)(2,1)S(1)} %get-tuple-element.266.refs_1_.grad.passed, ...), custom_call_target="tpu_custom_call" | custom-call | tf_op jit(solution)/shard_map/outer/pallas_call | solution.py:306
  192.6 7.0 %norm_back.2 = (bf16[256,1024]{1,0:T(8,128)(2,1)S(1)}, f32[8,1024]{1,0:T(8,128)S(1)}, f32[256,1024]{1,0:T(8,128)S(1)}) custom-call(bf16[256,4096]{1,0:T(8,128)(2,1)S(1)} %copy-done.5, bf16[1024,4096]{1,0:T(8,128)(2,1)} %copy-done.3, f32[256,1024]{1,0:T(8,128)S(1)} %copy-done.17, f32[1,1024]{1,0:T(1,128)S(1)} %get-tuple-element.375.gain, ...), custom_call_target="tpu_custom_call" | custom-call | tf_op jit(solution)/shard_map/norm_back/pallas_call | solution.py:622
  200.6 5.1 %outer.9 = (bf16[128,4096]{1,0:T(8,128)(2,1)S(1)}, bf16[128,4096]{1,0:T(8,128)(2,1)S(1)}, bf16[2,128,4096]{2,1,0:T(8,128)(2,1)}) custom-call(s32[1]{0:T(128)} %bitcast.26.dp_ref, bf16[256,1024]{1,0:T(8,128)(2,1)S(1)} %get-tuple-element.281.refs_0_, bf16[256,4096]{1,0:T(8,128)(2,1)S(1)} %copy-done.6, bf16[128,4096]{1,0:T(8,128)(2,1)} %collective-permute-done.32.refs_2_, ...), custom_call_target="tpu_custom_call" | custom-call | tf_op jit(solution)/shard_map/outer/pallas_call | solution.py:306
  213.0 9.8 %attend_back.1 = (bf16[256,3072]{1,0:T(8,128)(2,1)S(1)}, f32[1,3072]{1,0:T(1,128)S(1)}) custom-call(s32[1]{0:T(128)} %dynamic_slice.54.first_ref, bf16[256,3072]{1,0:T(8,128)(2,1)S(1)} %fusion.4.query.key.value, bf16[256,3072]{1,0:T(8,128)(2,1)S(1)} %fusion.4.query.key.value, bf16[256,3072]{1,0:T(8,128)(2,1)S(1)} %fusion.4.query.key.value, ...), custom_call_target="tpu_custom_call" | custom-call | tf_op jit(solution)/shard_map/attend_back/pallas_call | solution.py:532
  234.4 5.7 %norm_back.3 = (bf16[256,1024]{1,0:T(8,128)(2,1)S(1)}, f32[8,1024]{1,0:T(8,128)S(1)}) custom-call(bf16[256,3072]{1,0:T(8,128)(2,1)S(1)} %get-tuple-element.311.refs_2_.grad, bf16[1024,3072]{1,0:T(8,128)(2,1)} %copy-done.12, f32[256,1024]{1,0:T(8,128)S(1)} %copy-done.16, f32[1,1024]{1,0:T(1,128)S(1)} %get-tuple-element.374.gain, f32[256,1]{1,0:T(8,128)S(1)} %copy.56.scale, ...), custom_call_target="tpu_custom_call" | custom-call | tf_op jit(solution)/shard_map/norm_back/pallas_call | solution.py:622
  240.3 4.6 %outer.11 = (bf16[128,4096]{1,0:T(8,128)(2,1)S(1)}, bf16[128,4096]{1,0:T(8,128)(2,1)S(1)}, bf16[2,128,4096]{2,1,0:T(8,128)(2,1)}) custom-call(s32[1]{0:T(128)} %bitcast.26.dp_ref, bf16[256,1024]{1,0:T(8,128)(2,1)S(1)} %copy-done.15, bf16[256,1024]{1,0:T(8,128)(2,1)S(1)} %copy-done.11, bf16[256,3072]{1,0:T(8,128)(2,1)S(1)} %get-tuple-element.311.refs_2_.grad, ...), custom_call_target="tpu_custom_call" | custom-call | tf_op jit(solution)/shard_map/outer/pallas_call | solution.py:306
  264.6 6.7 %all-to-all-start.2 = ((bf16[32,160,128]{2,1,0:T(8,128)(2,1)}), bf16[32,160,128]{2,1,0:T(8,128)(2,1)}, u32[]{:S(2)}, u32[]{:S(2)}) async-start(bf16[32,160,128]{2,1,0:T(8,128)(2,1)} %fusion.10), calls=%async_computation.2 | async-start | bytes 2621440 | tf_op jit(solution)/shard_map/all_to_all | solution.py:721
  271.4 5.8 %collective-permute-done.44 = bf16[128,4096]{1,0:T(8,128)(2,1)} collective-permute-done((bf16[128,4096]{1,0:T(8,128)(2,1)}, bf16[128,4096]{1,0:T(8,128)(2,1)}, u32[]{:S(2)}, u32[]{:S(2)}) %collective-permute-start.44) | collective-permute-done | bytes 1048608 | tf_op jit(solution)/shard_map/ppermute | solution.py:38
  280.1 16.1 %collective-permute-done.43 = bf16[2,128,4096]{2,1,0:T(8,128)(2,1)} collective-permute-done((bf16[2,128,4096]{2,1,0:T(8,128)(2,1)}, bf16[2,128,4096]{2,1,0:T(8,128)(2,1)}, u32[]{:S(2)}, u32[]{:S(2)}) %collective-permute-start.43) | collective-permute-done | bytes 2097184 | tf_op jit(solution)/shard_map/ppermute | solution.py:38
  309.9 4.2 %collective-permute-done.45 = bf16[128,4096]{1,0:T(8,128)(2,1)} collective-permute-done((bf16[128,4096]{1,0:T(8,128)(2,1)}, bf16[128,4096]{1,0:T(8,128)(2,1)}, u32[]{:S(2)}, u32[]{:S(2)}) %collective-permute-start.45) | collective-permute-done | bytes 1048608 | tf_op jit(solution)/shard_map/ppermute | solution.py:38
  317.5 3.9 %collective-permute-start.49 = (bf16[32,4096]{1,0:T(8,128)(2,1)S(1)}, bf16[32,4096]{1,0:T(8,128)(2,1)S(1)}, u32[]{:S(2)}, u32[]{:S(2)}) collective-permute-start(bf16[32,4096]{1,0:T(8,128)(2,1)S(1)} %fusion.26), channel_id=1, source_target_pairs={{0,2},{1,3},{2,0},{3,1},{4,6},{5,7},{6,4},{7,5},{8,10},{9,11},{10,... | collective-permute-start | bytes 786440 | tf_op jit(solution)/shard_map/ppermute | solution.py:41
  321.5 10.7 %collective-permute-done.46 = bf16[2,32,4096]{2,1,0:T(8,128)(2,1)S(1)} collective-permute-done((bf16[2,32,4096]{2,1,0:T(8,128)(2,1)S(1)}, bf16[2,32,4096]{2,1,0:T(8,128)(2,1)S(1)}, u32[]{:S(2)}, u32[]{:S(2)}) %collective-permute-start.46) | collective-permute-done | bytes 524320 | tf_op jit(solution)/shard_map/ppermute | solution.py:41
  338.6 7.4 %collective-permute-done.48 = bf16[32,4096]{1,0:T(8,128)(2,1)S(1)} collective-permute-done((bf16[32,4096]{1,0:T(8,128)(2,1)S(1)}, bf16[32,4096]{1,0:T(8,128)(2,1)S(1)}, u32[]{:S(2)}, u32[]{:S(2)}) %collective-permute-start.48) | collective-permute-done | bytes 262176 | tf_op jit(solution)/shard_map/ppermute | solution.py:41
  (352 shorter events, 175.1 us)
Async XLA Ops:
  43.6 30.0 %all-to-all-start = ((bf16[32,88,128]{2,1,0:T(8,128)(2,1)}), bf16[32,88,128]{2,1,0:T(8,128)(2,1)}, u32[]{:S(2)}, u32[]{:S(2)}) async-start(bf16[32,88,128]{2,1,0:T(8,128)(2,1)} %pad_maximum_fusion), calls=%async_computation | async-start | bytes 1441792 | tf_op jit(solution)/shard_map/all_to_all | solution.py:721
  49.6 21.9 %collective-permute-start.4 = (bf16[128,4096]{1,0:T(8,128)(2,1)S(1)}, bf16[128,4096]{1,0:T(8,128)(2,1)}, u32[]{:S(2)}, u32[]{:S(2)}) collective-permute-start(bf16[128,4096]{1,0:T(8,128)(2,1)S(1)} %constant_dynamic-update-slice_fusion.2.refs_0_), channel_id=1, source_target_pairs={{0,16},{4,12},{8,24},{12,4},{16,0},{20,28},{24,8},{28,20},{1,17},{... | collective-permute-start | bytes 3145736 | tf_op jit(solution)/shard_map/ppermute | solution.py:38
  51.5 20.0 %collective-permute-start.7 = (bf16[128,4096]{1,0:T(8,128)(2,1)S(1)}, bf16[128,4096]{1,0:T(8,128)(2,1)S(1)}, u32[]{:S(2)}, u32[]{:S(2)}) collective-permute-start(bf16[128,4096]{1,0:T(8,128)(2,1)S(1)} %collective-permute-done.5.refs_2_), channel_id=1, source_target_pairs={{0,4},{4,0},{8,12},{12,8},{16,20},{20,16},{24,28},{28,24},{1,5},{5... | collective-permute-start | bytes 3145736 | tf_op jit(solution)/shard_map/ppermute | solution.py:34
  52.5 26.0 %collective-permute-start.3 = (bf16[64,4096]{1,0:T(8,128)(2,1)}, bf16[64,4096]{1,0:T(8,128)(2,1)}, u32[]{:S(2)}, u32[]{:S(2)}) collective-permute-start(bf16[64,4096]{1,0:T(8,128)(2,1)} %constant_dynamic-update-slice_fusion.4), channel_id=1, source_target_pairs={{0,1},{1,0},{2,3},{3,2},{4,5},{5,4},{6,7},{7,6},{8,9},{9,8},{10,11... | collective-permute-start | bytes 1572872 | tf_op jit(solution)/shard_map/ppermute | solution.py:41
  55.0 28.0 %collective-permute-start.9 = (bf16[128,4096]{1,0:T(8,128)(2,1)S(1)}, bf16[128,4096]{1,0:T(8,128)(2,1)}, u32[]{:S(2)}, u32[]{:S(2)}) collective-permute-start(bf16[128,4096]{1,0:T(8,128)(2,1)S(1)} %collective-permute-done.5.refs_2_), channel_id=1, source_target_pairs={{0,16},{4,12},{8,24},{12,4},{16,0},{20,28},{24,8},{28,20},{1,17},{... | collective-permute-start | bytes 3145736 | tf_op jit(solution)/shard_map/ppermute | solution.py:38
  80.7 25.3 %collective-permute-start.14 = (bf16[128,4096]{1,0:T(8,128)(2,1)S(1)}, bf16[128,4096]{1,0:T(8,128)(2,1)}, u32[]{:S(2)}, u32[]{:S(2)}) collective-permute-start(bf16[128,4096]{1,0:T(8,128)(2,1)S(1)} %constant_dynamic-update-slice_fusion.6.refs_0_), channel_id=1, source_target_pairs={{0,8},{4,20},{8,0},{12,28},{16,24},{20,4},{24,16},{28,12},{1,9},{5... | collective-permute-start | bytes 3145736 | tf_op jit(solution)/shard_map/ppermute | solution.py:38
  82.2 23.9 %collective-permute-start.15 = (bf16[128,4096]{1,0:T(8,128)(2,1)S(1)}, bf16[128,4096]{1,0:T(8,128)(2,1)S(1)}, u32[]{:S(2)}, u32[]{:S(2)}) collective-permute-start(bf16[128,4096]{1,0:T(8,128)(2,1)S(1)} %constant_dynamic-update-slice_fusion.6.refs_0_), channel_id=1, source_target_pairs={{0,4},{4,0},{8,12},{12,8},{16,20},{20,16},{24,28},{28,24},{1,5},{5... | collective-permute-start | bytes 3145736 | tf_op jit(solution)/shard_map/ppermute | solution.py:34
  82.2 35.5 %collective-permute-start.13 = (bf16[128,4096]{1,0:T(8,128)(2,1)S(1)}, bf16[128,4096]{1,0:T(8,128)(2,1)}, u32[]{:S(2)}, u32[]{:S(2)}) collective-permute-start(bf16[128,4096]{1,0:T(8,128)(2,1)S(1)} %constant_dynamic-update-slice_fusion.6.refs_0_), channel_id=1, source_target_pairs={{0,16},{4,12},{8,24},{12,4},{16,0},{20,28},{24,8},{28,20},{1,17},{... | collective-permute-start | bytes 3145736 | tf_op jit(solution)/shard_map/ppermute | solution.py:38
  107.1 22.4 %collective-permute-start.11 = (bf16[128,4096]{1,0:T(8,128)(2,1)}, bf16[128,4096]{1,0:T(8,128)(2,1)}, u32[]{:S(2)}, u32[]{:S(2)}) collective-permute-start(bf16[128,4096]{1,0:T(8,128)(2,1)} %collective-permute-done.9.refs_6_), channel_id=1, source_target_pairs={{0,4},{4,0},{8,12},{12,8},{16,20},{20,16},{24,28},{28,24},{1,5},{5... | collective-permute-start | bytes 3145736 | tf_op jit(solution)/shard_map/ppermute | solution.py:34
  111.2 35.2 %collective-permute-start.19 = (bf16[128,4096]{1,0:T(8,128)(2,1)}, bf16[128,4096]{1,0:T(8,128)(2,1)}, u32[]{:S(2)}, u32[]{:S(2)}) collective-permute-start(bf16[128,4096]{1,0:T(8,128)(2,1)} %collective-permute-done.14.refs_2_), channel_id=1, source_target_pairs={{0,16},{4,12},{8,24},{12,4},{16,0},{20,28},{24,8},{28,20},{1,17},{... | collective-permute-start | bytes 3145736 | tf_op jit(solution)/shard_map/ppermute | solution.py:38
  113.4 29.1 %all-to-all-start.1 = ((bf16[32,72,128]{2,1,0:T(8,128)(2,1)}), bf16[32,72,128]{2,1,0:T(8,128)(2,1)}, u32[]{:S(2)}, u32[]{:S(2)}) async-start(bf16[32,72,128]{2,1,0:T(8,128)(2,1)} %reshape.379), calls=%async_computation.1 | async-start | bytes 1179648 | tf_op jit(solution)/shard_map/all_to_all | solution.py:721
  117.7 28.7 %collective-permute-start.20 = (bf16[128,4096]{1,0:T(8,128)(2,1)}, bf16[128,4096]{1,0:T(8,128)(2,1)}, u32[]{:S(2)}, u32[]{:S(2)}) collective-permute-start(bf16[128,4096]{1,0:T(8,128)(2,1)} %collective-permute-done.13.refs_4_), channel_id=1, source_target_pairs={{0,4},{4,0},{8,12},{12,8},{16,20},{20,16},{24,28},{28,24},{1,5},{5... | collective-permute-start | bytes 3145736 | tf_op jit(solution)/shard_map/ppermute | solution.py:34
  126.3 28.2 %collective-permute-start.17 = (bf16[512,1024]{1,0:T(8,128)(2,1)}, bf16[512,1024]{1,0:T(8,128)(2,1)}, u32[]{:S(2)}, u32[]{:S(2)}) collective-permute-start(bf16[512,1024]{1,0:T(8,128)(2,1)} %constant_dynamic-update-slice_fusion.10.refs_0_), channel_id=1, source_target_pairs={{0,8},{4,20},{8,0},{12,28},{16,24},{20,4},{24,16},{28,12},{1,9},{5... | collective-permute-start | bytes 3145736 | tf_op jit(solution)/shard_map/ppermute | solution.py:38
  129.5 25.1 %collective-permute-start.18 = (bf16[512,1024]{1,0:T(8,128)(2,1)}, bf16[512,1024]{1,0:T(8,128)(2,1)}, u32[]{:S(2)}, u32[]{:S(2)}) collective-permute-start(bf16[512,1024]{1,0:T(8,128)(2,1)} %constant_dynamic-update-slice_fusion.10.refs_0_), channel_id=1, source_target_pairs={{0,4},{4,0},{8,12},{12,8},{16,20},{20,16},{24,28},{28,24},{1,5},{5... | collective-permute-start | bytes 3145736 | tf_op jit(solution)/shard_map/ppermute | solution.py:34
  129.5 27.3 %collective-permute-start.22 = (bf16[512,1024]{1,0:T(8,128)(2,1)}, bf16[512,1024]{1,0:T(8,128)(2,1)}, u32[]{:S(2)}, u32[]{:S(2)}) collective-permute-start(bf16[512,1024]{1,0:T(8,128)(2,1)} %constant_dynamic-update-slice_fusion.10.refs_0_), channel_id=1, source_target_pairs={{0,16},{4,12},{8,24},{12,4},{16,0},{20,28},{24,8},{28,20},{1,17},{... | collective-permute-start | bytes 3145736 | tf_op jit(solution)/shard_map/ppermute | solution.py:38
  183.1 26.4 %collective-permute-start.31 = (bf16[2,512,1024]{2,1,0:T(8,128)(2,1)}, bf16[2,512,1024]{2,1,0:T(8,128)(2,1)}, u32[]{:S(2)}, u32[]{:S(2)}) collective-permute-start(bf16[2,512,1024]{2,1,0:T(8,128)(2,1)} %get-tuple-element.271), channel_id=1, source_target_pairs={{0,16},{4,12},{8,24},{12,4},{16,0},{20,28},{24,8},{28,20},{1,17},{... | collective-permute-start | bytes 6291464 | tf_op jit(solution)/shard_map/ppermute | solution.py:38
  205.7 41.2 %collective-permute-start.37 = (bf16[2,128,4096]{2,1,0:T(8,128)(2,1)}, bf16[2,128,4096]{2,1,0:T(8,128)(2,1)}, u32[]{:S(2)}, u32[]{:S(2)}) collective-permute-start(bf16[2,128,4096]{2,1,0:T(8,128)(2,1)} %get-tuple-element.287), channel_id=1, source_target_pairs={{0,16},{4,12},{8,24},{12,4},{16,0},{20,28},{24,8},{28,20},{1,17},{... | collective-permute-start | bytes 6291464 | tf_op jit(solution)/shard_map/ppermute | solution.py:38
  231.1 20.3 %collective-permute-start.36 = (bf16[512,1024]{1,0:T(8,128)(2,1)}, bf16[512,1024]{1,0:T(8,128)(2,1)}, u32[]{:S(2)}, u32[]{:S(2)}) collective-permute-start(bf16[512,1024]{1,0:T(8,128)(2,1)} %fusion.8), channel_id=1, source_target_pairs={{0,8},{4,20},{8,0},{12,28},{16,24},{20,4},{24,16},{28,12},{1,9},{5... | collective-permute-start | bytes 3145736 | tf_op jit(solution)/shard_map/ppermute | solution.py:38
  246.9 49.3 %collective-permute-start.43 = (bf16[2,128,4096]{2,1,0:T(8,128)(2,1)}, bf16[2,128,4096]{2,1,0:T(8,128)(2,1)}, u32[]{:S(2)}, u32[]{:S(2)}) collective-permute-start(bf16[2,128,4096]{2,1,0:T(8,128)(2,1)} %get-tuple-element.317), channel_id=1, source_target_pairs={{0,16},{4,12},{8,24},{12,4},{16,0},{20,28},{24,8},{28,20},{1,17},{... | collective-permute-start | bytes 6291464 | tf_op jit(solution)/shard_map/ppermute | solution.py:38
  249.5 27.6 %collective-permute-start.44 = (bf16[128,4096]{1,0:T(8,128)(2,1)}, bf16[128,4096]{1,0:T(8,128)(2,1)}, u32[]{:S(2)}, u32[]{:S(2)}) collective-permute-start(bf16[128,4096]{1,0:T(8,128)(2,1)} %fusion.7), channel_id=1, source_target_pairs={{0,8},{4,20},{8,0},{12,28},{16,24},{20,4},{24,16},{28,12},{1,9},{5... | collective-permute-start | bytes 3145736 | tf_op jit(solution)/shard_map/ppermute | solution.py:38
  254.5 44.1 %collective-permute-start.42 = (bf16[2,128,1024]{2,1,0:T(8,128)(2,1)}, bf16[2,128,1024]{2,1,0:T(8,128)(2,1)}, u32[]{:S(2)}, u32[]{:S(2)}) collective-permute-start(bf16[2,128,1024]{2,1,0:T(8,128)(2,1)} %fusion.18), channel_id=1, source_target_pairs={{0,1},{1,0},{2,3},{3,2},{4,5},{5,4},{6,7},{7,6},{8,9},{9,8},{10,11... | collective-permute-start | bytes 1572872 | tf_op jit(solution)/shard_map/ppermute | solution.py:41
  264.6 40.4 %all-to-all-start.2 = ((bf16[32,160,128]{2,1,0:T(8,128)(2,1)}), bf16[32,160,128]{2,1,0:T(8,128)(2,1)}, u32[]{:S(2)}, u32[]{:S(2)}) async-start(bf16[32,160,128]{2,1,0:T(8,128)(2,1)} %fusion.10), calls=%async_computation.2 | async-start | bytes 2621440 | tf_op jit(solution)/shard_map/all_to_all | solution.py:721
  280.0 36.3 %collective-permute-start.47 = (bf16[2,32,4096]{2,1,0:T(8,128)(2,1)}, bf16[2,32,4096]{2,1,0:T(8,128)(2,1)}, u32[]{:S(2)}, u32[]{:S(2)}) collective-permute-start(bf16[2,32,4096]{2,1,0:T(8,128)(2,1)} %fusion.19), channel_id=1, source_target_pairs={{0,1},{1,0},{2,3},{3,2},{4,5},{5,4},{6,7},{7,6},{8,9},{9,8},{10,11... | collective-permute-start | bytes 1572872 | tf_op jit(solution)/shard_map/ppermute | solution.py:41
  300.5 35.3 %collective-permute-start.50 = (bf16[128,1024]{1,0:T(8,128)(2,1)}, bf16[128,1024]{1,0:T(8,128)(2,1)S(1)}, u32[]{:S(2)}, u32[]{:S(2)}) collective-permute-start(bf16[128,1024]{1,0:T(8,128)(2,1)} %fusion.25), channel_id=1, source_target_pairs={{0,2},{1,3},{2,0},{3,1},{4,6},{5,7},{6,4},{7,5},{8,10},{9,11},{10,... | collective-permute-start | bytes 786440 | tf_op jit(solution)/shard_map/ppermute | solution.py:41
  (91 other events, 882.3 us)

commit v2 on v1

--- a/solution.py
+++ b/solution.py
@@ -582,19 +582,29 @@
     )(grad_b, weight, slope)
 
 
+def in_hbm(array):
+    return pltpu.with_memory_space_constraint(array, pltpu.HBM)
+
+
 def norm_back(grad_b, weight, unit, gain, scale, passed, keep_wide):
     rows, depth = grad_b.shape
     width = weight.shape[0]
     tile = 1024
     steps = depth // tile
 
-    def kernel(grad, weight, unit, gain, scale, passed, *refs):
-        outs, total = refs[:-1], refs[-1]
+    def kernel(grad, weight, unit_at, gain, scale, passed_at, *refs):
+        outs, (total, unit, passed, sems) = refs[:-4], refs[-4:]
         step = pl.program_id(0)
+        fetches = [
+            pltpu.make_async_copy(unit_at, unit, sems.at[0]),
+            pltpu.make_async_copy(passed_at, passed, sems.at[1]),
+        ]
         part = back_dot(grad[...], weight[...])
 
         @pl.when(step == 0)
         def _():
+            for fetch in fetches:
+                fetch.start()
             total[...] = part
 
         @pl.when(step > 0)
@@ -603,22 +613,32 @@
 
         @pl.when(step == steps - 1)
         def _():
+            for fetch in fetches:
+                fetch.wait()
             whole, u = total[...], unit[...]
             normed = whole * gain[...]
+            outs[1][0:1] = jnp.sum(whole * u, axis=0, keepdims=True)
+            outs[1][1:2] = jnp.sum(whole, axis=0, keepdims=True)
             out = passed[...].astype(F32) + standardize_back(normed, u, scale[...])
+            if keep_wide:
+                total[...] = out
+                store = pltpu.make_async_copy(total, outs[2], sems.at[2])
+                store.start()
             out_b = out.astype(BF16)
             outs[0][...] = out_b
-            outs[1][0:1] = jnp.sum(whole * u, axis=0, keepdims=True)
-            outs[1][1:2] = jnp.sum(whole, axis=0, keepdims=True)
             outs[1][2:3] = jnp.sum(out_b.astype(F32), axis=0, keepdims=True)
             if keep_wide:
-                outs[2][...] = out
+                store.wait()
 
     def once(shape):
         return pl.BlockSpec(shape, lambda j: (0, 0), pipeline_mode=pl.Buffered(1))
 
+    anywhere = pl.BlockSpec(memory_space=pl.ANY)
     shapes = [((rows, width), BF16), ((8, width), F32)]
-    shapes += [((rows, width), F32)] if keep_wide else []
+    out_specs = [once(shape) for shape, _ in shapes]
+    if keep_wide:
+        shapes.append(((rows, width), F32))
+        out_specs.append(anywhere)
     return pl.pallas_call(
         kernel,
         out_shape=[jax.ShapeDtypeStruct(*s) for s in shapes],
@@ -626,17 +646,22 @@
         in_specs=[
             pl.BlockSpec((rows, tile), lambda j: (0, j)),
             pl.BlockSpec((width, tile), lambda j: (0, j)),
-            once((rows, width)),
+            anywhere,
             once((1, width)),
             once((rows, 1)),
-            once((rows, width)),
+            anywhere,
         ],
-        out_specs=[once(shape) for shape, _ in shapes],
-        scratch_shapes=[pltpu.VMEM((rows, width), F32)],
+        out_specs=out_specs,
+        scratch_shapes=[
+            pltpu.VMEM((rows, width), F32),
+            pltpu.VMEM((rows, width), unit.dtype),
+            pltpu.VMEM((rows, width), passed.dtype),
+            pltpu.SemaphoreType.DMA((3,)),
+        ],
         compiler_params=pltpu.CompilerParams(vmem_limit_bytes=16 << 20),
         cost_estimate=pl.CostEstimate(flops=0, bytes_accessed=0, transcendentals=0),
         name="norm_back",
-    )(grad_b, pltpu.with_memory_space_constraint(weight, pltpu.HBM), unit, gain, scale, passed)
+    )(grad_b, in_hbm(weight), in_hbm(unit), gain, scale, in_hbm(passed))
 
 
 def standardize(values):
@@ -818,7 +843,6 @@
     )
     clock.tick(grad_branch_b)
     for_up.first()
-    for_down.second()
     grad_att_b = back_dot(clock.gate(grad_branch_b), full_out).astype(BF16)
     clock.tick(grad_att_b)
     grad_mixed_b, term_mixed = attend_back(first_len, mixed_b, clock.gate(grad_att_b))
@@ -826,7 +850,9 @@
     for_attn = make_scatter(
         grid, clock, (normed_one_b, grad_mixed_b), (attended_b, grad_branch_b)
     )
+    for_down.land()
     for_attn.across()
+    for_down.second()
 
     grad_inputs_b, sums_one = norm_back(
         clock.gate(grad_mixed_b), full_qkv, unit_one, g1, scale_one, grad_hidden, False

time: 354 us -> 348 us (0.983)
  waiting for transfers between devices: 112 us -> 103 us
  starting transfers between devices: 66.1 us -> 73.8 us
  local copies, waits for them, and re-layouts: 48.2 us -> 44.5 us
    ppermute x15, waiting for transfers between devices: 58 us -> 52.9 us  [crossed(): return lax.ppermute(value, 'dp', pairs)]
    ppermute x12, starting transfers between devices: 23.7 us -> 27.8 us  [over_z(): return lax.ppermute(value, 'fsdp', [(i, i ^ mask) for i in range(self.n_z)])]
    unnamed x136 -> x132, local copies, waits for them, and re-layouts: 16.3 us -> 14.3 us
  transfers between devices with their start and end apart: 54 -> 54, of which waited for: 17 -> 16; matrix products, arithmetic and copies ran while one was open for 25% -> 25% of each run, Pallas kernels for 17% -> 17%
where the time goes in v2:
time: 348 us; the launch traced here: 342 us
  waiting for transfers between devices  103 us (30%)
  starting transfers between devices  73.8 us (21%)
  Pallas kernels  64.2 us (18%)
  local copies, waits for them, and re-layouts  44.5 us (13%)
  other arithmetic  36.2 us (10%)
  matrix products  18.3 us (5%)
    ppermute x15, waiting for transfers between devices, crossed(): return lax.ppermute(value, 'dp', pairs)  52.9 us
    ppermute x12, waiting for transfers between devices, over_z(): return lax.ppermute(value, 'fsdp', [(i, i ^ mask) for i in range(self.n_z)])  47.8 us
    ppermute x12, starting transfers between devices, over_z(): return lax.ppermute(value, 'fsdp', [(i, i ^ mask) for i in range(self.n_z)])  27.8 us
    pallas_call x6, Pallas kernels, call(): pl.pallas_call(kernel, out_shape=shapes, grid_spec=pltpu.PrefetchScalarGr...  24.3 us
    ppermute x15, starting transfers between devices, crossed(): return lax.ppermute(value, 'dp', pairs)  22.4 us
    all_to_all x3, starting transfers between devices, swap(): block = lax.all_to_all(block, AXES, split_axis=0, concat_axis=0, tiled=True)  18.3 us
    unnamed x132, local copies, waits for them, and re-layouts  14.3 us
    pallas_call x2, Pallas kernels, norm_back(): pl.pallas_call(kernel, out_shape=[jax.ShapeDtypeStruct(*s) for s in shape...  13 us
  transfers between devices with their start and end apart: 54, of which 16 were waited for; matrix products, arithmetic and copies ran while one was open for 25% of the time, Pallas kernels for 17%

profile of v2, /device:TPU:0, one launch (start us, length us, event | category | flops | bytes accessed | tf_op | source)
XLA Modules:
  0.0 342.4 jit_solution(12566729414816921270)
XLA Ops:
  1.7 4.1 %collective-permute-start = (bf16[32,4096]{1,0:T(8,128)(2,1)S(1)}, bf16[32,4096]{1,0:T(8,128)(2,1)S(1)}, u32[]{:S(2)}, u32[]{:S(2)}) collective-permute-start(bf16[32,4096]{1,0:T(8,128)(2,1)S(1)} %pad_maximum_fusion.1), channel_id=1, source_target_pairs={{0,2},{1,3},{2,0},{3,1},{4,6},{5,7},{6,4},{7,5},{8,10},{9,11},{10,... | collective-permute-start | bytes 786440 | tf_op jit(solution)/shard_map/ppermute | solution.py:41
  23.3 13.3 %collective-permute-done.2 = bf16[64,4096]{1,0:T(8,128)(2,1)S(1)} collective-permute-done((bf16[64,4096]{1,0:T(8,128)(2,1)S(1)}, bf16[64,4096]{1,0:T(8,128)(2,1)S(1)}, u32[]{:S(2)}, u32[]{:S(2)}) %collective-permute-start.2) | collective-permute-done | bytes 524320 | tf_op jit(solution)/shard_map/ppermute | solution.py:41
  43.5 6.1 %all-to-all-start = ((bf16[32,88,128]{2,1,0:T(8,128)(2,1)}), bf16[32,88,128]{2,1,0:T(8,128)(2,1)}, u32[]{:S(2)}, u32[]{:S(2)}) async-start(bf16[32,88,128]{2,1,0:T(8,128)(2,1)} %pad_maximum_fusion), calls=%async_computation | async-start | bytes 1441792 | tf_op jit(solution)/shard_map/all_to_all | solution.py:746
  56.3 15.2 %collective-permute-done.4.refs_4_ = bf16[128,4096]{1,0:T(8,128)(2,1)} collective-permute-done((bf16[128,4096]{1,0:T(8,128)(2,1)S(1)}, bf16[128,4096]{1,0:T(8,128)(2,1)}, u32[]{:S(2)}, u32[]{:S(2)}) %collective-permute-start.4) | collective-permute-done | bytes 1048608 | tf_op jit(solution)/shard_map/ppermute | solution.py:38
  88.8 9.0 %collective-permute-done.8 = bf16[128,1024]{1,0:T(8,128)(2,1)S(1)} collective-permute-done((bf16[128,1024]{1,0:T(8,128)(2,1)S(1)}, bf16[128,1024]{1,0:T(8,128)(2,1)S(1)}, u32[]{:S(2)}, u32[]{:S(2)}) %collective-permute-start.8) | collective-permute-done | bytes 262176 | tf_op jit(solution)/shard_map/ppermute | solution.py:41
  97.8 8.2 %collective-permute-done.14.refs_2_ = bf16[128,4096]{1,0:T(8,128)(2,1)} collective-permute-done((bf16[128,4096]{1,0:T(8,128)(2,1)S(1)}, bf16[128,4096]{1,0:T(8,128)(2,1)}, u32[]{:S(2)}, u32[]{:S(2)}) %collective-permute-start.14) | collective-permute-done | bytes 1048608 | tf_op jit(solution)/shard_map/ppermute | solution.py:38
  113.4 4.2 %all-to-all-start.1 = ((bf16[32,72,128]{2,1,0:T(8,128)(2,1)}), bf16[32,72,128]{2,1,0:T(8,128)(2,1)}, u32[]{:S(2)}, u32[]{:S(2)}) async-start(bf16[32,72,128]{2,1,0:T(8,128)(2,1)} %reshape.379), calls=%async_computation.1 | async-start | bytes 1179648 | tf_op jit(solution)/shard_map/all_to_all | solution.py:746
  118.1 5.5 %collective-permute-done.12 = bf16[256,1024]{1,0:T(8,128)(2,1)} collective-permute-done((bf16[256,1024]{1,0:T(8,128)(2,1)S(1)}, bf16[256,1024]{1,0:T(8,128)(2,1)}, u32[]{:S(2)}, u32[]{:S(2)}) %collective-permute-start.12) | collective-permute-done | bytes 524320 | tf_op jit(solution)/shard_map/ppermute | solution.py:41
  131.2 4.2 %assemble.3 = (bf16[1024,3072]{1,0:T(8,128)(2,1)S(1)}, bf16[1024,1024]{1,0:T(8,128)(2,1)S(1)}) custom-call(s32[1]{0:T(128)} %bitcast.19.me_ref, bf16[128,4096]{1,0:T(8,128)(2,1)S(1)} %constant_dynamic-update-slice_fusion.2.refs_0_, bf16[128,4096]{1,0:T(8,128)(2,1)S(1)} %copy-done.30, bf16[128,4096]{1,0:T(8,128)(2,1)S(1)} %copy-done.28, ...), custom_call_target="tpu_custom_call" | custom-call | tf_op jit(solution)/shard_map/assemble/pallas_call | solution.py:172
  138.7 3.8 %attend.1.refs_1_ = bf16[256,1024]{1,0:T(8,128)(2,1)S(1)} custom-call(s32[1]{0:T(128)} %dynamic_slice.54.first_ref, bf16[256,3072]{1,0:T(8,128)(2,1)S(1)} %fusion.4.query.key.value, bf16[256,3072]{1,0:T(8,128)(2,1)S(1)} %fusion.4.query.key.value, bf16[256,3072]{1,0:T(8,128)(2,1)S(1)} %fusion.4.query.key.value), custom_call_target="tpu_custom_call" | custom-call | tf_op jit(solution)/shard_map/attend/pallas_call | solution.py:490
  157.9 4.4 %fusion.3 = (f32[256,4096]{1,0:T(8,128)S(1)}, bf16[256,4096]{1,0:T(8,128)(2,1)S(1)}) fusion(f32[4096]{0:T(1024)S(1)} %bitcast.179, bf16[256,1024]{1,0:T(8,128)(2,1)S(1)} %get-tuple-element.281.refs_0_, bf16[1024,4096]{1,0:T(8,128)(2,1)S(1)} %assemble.4.weight), kind=kOutput, calls=%fused_computation.5 | convolution fusion | flops 2159017984 | bytes 15220736 | tf_op jit(solution)/shard_map/dot_general | solution.py:823
  165.3 4.8 %collective-permute-done.24.refs_6_ = bf16[512,1024]{1,0:T(8,128)(2,1)S(1)} collective-permute-done((bf16[512,1024]{1,0:T(8,128)(2,1)}, bf16[512,1024]{1,0:T(8,128)(2,1)S(1)}, u32[]{:S(2)}, u32[]{:S(2)}) %collective-permute-start.24) | collective-permute-done | bytes 1048608 | tf_op jit(solution)/shard_map/ppermute | solution.py:38
  178.8 4.4 %outer.7 = (bf16[512,1024]{1,0:T(8,128)(2,1)S(1)}, bf16[512,1024]{1,0:T(8,128)(2,1)S(1)}, bf16[2,512,1024]{2,1,0:T(8,128)(2,1)}) custom-call(s32[1]{0:T(128)} %bitcast.26.dp_ref, bf16[256,4096]{1,0:T(8,128)(2,1)S(1)} %get-tuple-element.324.refs_0_, bf16[256,1024]{1,0:T(8,128)(2,1)S(1)} %get-tuple-element.267.refs_1_.grad.passed_at, ...), custom_call_target="tpu_custom_call" | custom-call | tf_op jit(solution)/shard_map/outer/pallas_call | solution.py:306
  191.4 7.2 %norm_back.2 = (bf16[256,1024]{1,0:T(8,128)(2,1)S(1)}, f32[8,1024]{1,0:T(8,128)S(1)}, f32[256,1024]{1,0:T(8,128)S(1)}) custom-call(bf16[256,4096]{1,0:T(8,128)(2,1)S(1)} %copy-done.5, bf16[1024,4096]{1,0:T(8,128)(2,1)} %copy-done.3, f32[256,1024]{1,0:T(8,128)} %get-tuple-element.362.unit_at, f32[1,1024]{1,0:T(1,128)S(1)} %get-tuple-element.377.gain, ...), custom_call_target="tpu_custom_call" | custom-call | tf_op jit(solution)/shard_map/norm_back/pallas_call | solution.py:642
  199.7 5.1 %outer.9 = (bf16[128,4096]{1,0:T(8,128)(2,1)S(1)}, bf16[128,4096]{1,0:T(8,128)(2,1)S(1)}, bf16[2,128,4096]{2,1,0:T(8,128)(2,1)}) custom-call(s32[1]{0:T(128)} %bitcast.26.dp_ref, bf16[256,1024]{1,0:T(8,128)(2,1)S(1)} %get-tuple-element.281.refs_0_, bf16[256,4096]{1,0:T(8,128)(2,1)S(1)} %copy-done.6, bf16[128,4096]{1,0:T(8,128)(2,1)} %collective-permute-done.31.refs_2_, ...), custom_call_target="tpu_custom_call" | custom-call | tf_op jit(solution)/shard_map/outer/pallas_call | solution.py:306
  205.8 9.8 %attend_back.1 = (bf16[256,3072]{1,0:T(8,128)(2,1)S(1)}, f32[1,3072]{1,0:T(1,128)S(1)}) custom-call(s32[1]{0:T(128)} %dynamic_slice.54.first_ref, bf16[256,3072]{1,0:T(8,128)(2,1)S(1)} %fusion.4.query.key.value, bf16[256,3072]{1,0:T(8,128)(2,1)S(1)} %fusion.4.query.key.value, bf16[256,3072]{1,0:T(8,128)(2,1)S(1)} %fusion.4.query.key.value, ...), custom_call_target="tpu_custom_call" | custom-call | tf_op jit(solution)/shard_map/attend_back/pallas_call | solution.py:532
  225.4 5.9 %norm_back.3 = (bf16[256,1024]{1,0:T(8,128)(2,1)S(1)}, f32[8,1024]{1,0:T(8,128)S(1)}) custom-call(bf16[256,3072]{1,0:T(8,128)(2,1)S(1)} %get-tuple-element.313.refs_2_.grad, bf16[1024,3072]{1,0:T(8,128)(2,1)} %copy-done.13, f32[256,1024]{1,0:T(8,128)} %get-tuple-element.364.unit_at, f32[1,1024]{1,0:T(1,128)S(1)} %get-tuple-element.376.gain, ...), custom_call_target="tpu_custom_call" | custom-call | tf_op jit(solution)/shard_map/norm_back/pallas_call | solution.py:642
  231.4 4.6 %outer.11 = (bf16[128,4096]{1,0:T(8,128)(2,1)S(1)}, bf16[128,4096]{1,0:T(8,128)(2,1)S(1)}, bf16[2,128,4096]{2,1,0:T(8,128)(2,1)}) custom-call(s32[1]{0:T(128)} %bitcast.26.dp_ref, bf16[256,1024]{1,0:T(8,128)(2,1)S(1)} %copy-done.16, bf16[256,1024]{1,0:T(8,128)(2,1)S(1)} %copy-done.12, bf16[256,3072]{1,0:T(8,128)(2,1)S(1)} %get-tuple-element.313.refs_2_.grad, ...), custom_call_target="tpu_custom_call" | custom-call | tf_op jit(solution)/shard_map/outer/pallas_call | solution.py:306
  257.3 8.1 %all-to-all-start.2 = ((bf16[32,160,128]{2,1,0:T(8,128)(2,1)}), bf16[32,160,128]{2,1,0:T(8,128)(2,1)}, u32[]{:S(2)}, u32[]{:S(2)}) async-start(bf16[32,160,128]{2,1,0:T(8,128)(2,1)} %fusion.10), calls=%async_computation.2 | async-start | bytes 2621440 | tf_op jit(solution)/shard_map/all_to_all | solution.py:746
  270.8 15.6 %collective-permute-done.43 = bf16[2,128,4096]{2,1,0:T(8,128)(2,1)} collective-permute-done((bf16[2,128,4096]{2,1,0:T(8,128)(2,1)}, bf16[2,128,4096]{2,1,0:T(8,128)(2,1)}, u32[]{:S(2)}, u32[]{:S(2)}) %collective-permute-start.43) | collective-permute-done | bytes 2097184 | tf_op jit(solution)/shard_map/ppermute | solution.py:38
  308.9 7.1 %collective-permute-start.49 = (bf16[32,4096]{1,0:T(8,128)(2,1)S(1)}, bf16[32,4096]{1,0:T(8,128)(2,1)S(1)}, u32[]{:S(2)}, u32[]{:S(2)}) collective-permute-start(bf16[32,4096]{1,0:T(8,128)(2,1)S(1)} %fusion.26), channel_id=1, source_target_pairs={{0,2},{1,3},{2,0},{3,1},{4,6},{5,7},{6,4},{7,5},{8,10},{9,11},{10,... | collective-permute-start | bytes 786440 | tf_op jit(solution)/shard_map/ppermute | solution.py:41
  316.1 9.2 %collective-permute-done.46 = bf16[2,32,4096]{2,1,0:T(8,128)(2,1)S(1)} collective-permute-done((bf16[2,32,4096]{2,1,0:T(8,128)(2,1)S(1)}, bf16[2,32,4096]{2,1,0:T(8,128)(2,1)S(1)}, u32[]{:S(2)}, u32[]{:S(2)}) %collective-permute-start.46) | collective-permute-done | bytes 524320 | tf_op jit(solution)/shard_map/ppermute | solution.py:41
  325.5 3.9 %collective-permute-start.48 = (bf16[32,4096]{1,0:T(8,128)(2,1)S(1)}, bf16[32,4096]{1,0:T(8,128)(2,1)S(1)}, u32[]{:S(2)}, u32[]{:S(2)}) collective-permute-start(bf16[32,4096]{1,0:T(8,128)(2,1)S(1)} %fusion.27), channel_id=1, source_target_pairs={{0,2},{1,3},{2,0},{3,1},{4,6},{5,7},{6,4},{7,5},{8,10},{9,11},{10,... | collective-permute-start | bytes 786440 | tf_op jit(solution)/shard_map/ppermute | solution.py:41
  333.1 7.4 %collective-permute-done.48 = bf16[32,4096]{1,0:T(8,128)(2,1)S(1)} collective-permute-done((bf16[32,4096]{1,0:T(8,128)(2,1)S(1)}, bf16[32,4096]{1,0:T(8,128)(2,1)S(1)}, u32[]{:S(2)}, u32[]{:S(2)}) %collective-permute-start.48) | collective-permute-done | bytes 262176 | tf_op jit(solution)/shard_map/ppermute | solution.py:41
  (348 shorter events, 169.0 us)
Async XLA Ops:
  43.5 30.0 %all-to-all-start = ((bf16[32,88,128]{2,1,0:T(8,128)(2,1)}), bf16[32,88,128]{2,1,0:T(8,128)(2,1)}, u32[]{:S(2)}, u32[]{:S(2)}) async-start(bf16[32,88,128]{2,1,0:T(8,128)(2,1)} %pad_maximum_fusion), calls=%async_computation | async-start | bytes 1441792 | tf_op jit(solution)/shard_map/all_to_all | solution.py:746
  49.6 21.9 %collective-permute-start.4 = (bf16[128,4096]{1,0:T(8,128)(2,1)S(1)}, bf16[128,4096]{1,0:T(8,128)(2,1)}, u32[]{:S(2)}, u32[]{:S(2)}) collective-permute-start(bf16[128,4096]{1,0:T(8,128)(2,1)S(1)} %constant_dynamic-update-slice_fusion.2.refs_0_), channel_id=1, source_target_pairs={{0,16},{4,12},{8,24},{12,4},{16,0},{20,28},{24,8},{28,20},{1,17},{... | collective-permute-start | bytes 3145736 | tf_op jit(solution)/shard_map/ppermute | solution.py:38
  52.5 26.0 %collective-permute-start.3 = (bf16[64,4096]{1,0:T(8,128)(2,1)}, bf16[64,4096]{1,0:T(8,128)(2,1)}, u32[]{:S(2)}, u32[]{:S(2)}) collective-permute-start(bf16[64,4096]{1,0:T(8,128)(2,1)} %constant_dynamic-update-slice_fusion.4), channel_id=1, source_target_pairs={{0,1},{1,0},{2,3},{3,2},{4,5},{5,4},{6,7},{7,6},{8,9},{9,8},{10,11... | collective-permute-start | bytes 1572872 | tf_op jit(solution)/shard_map/ppermute | solution.py:41
  55.0 28.0 %collective-permute-start.9 = (bf16[128,4096]{1,0:T(8,128)(2,1)S(1)}, bf16[128,4096]{1,0:T(8,128)(2,1)}, u32[]{:S(2)}, u32[]{:S(2)}) collective-permute-start(bf16[128,4096]{1,0:T(8,128)(2,1)S(1)} %collective-permute-done.5.refs_2_), channel_id=1, source_target_pairs={{0,16},{4,12},{8,24},{12,4},{16,0},{20,28},{24,8},{28,20},{1,17},{... | collective-permute-start | bytes 3145736 | tf_op jit(solution)/shard_map/ppermute | solution.py:38
  80.7 25.3 %collective-permute-start.14 = (bf16[128,4096]{1,0:T(8,128)(2,1)S(1)}, bf16[128,4096]{1,0:T(8,128)(2,1)}, u32[]{:S(2)}, u32[]{:S(2)}) collective-permute-start(bf16[128,4096]{1,0:T(8,128)(2,1)S(1)} %constant_dynamic-update-slice_fusion.6.refs_0_), channel_id=1, source_target_pairs={{0,8},{4,20},{8,0},{12,28},{16,24},{20,4},{24,16},{28,12},{1,9},{5... | collective-permute-start | bytes 3145736 | tf_op jit(solution)/shard_map/ppermute | solution.py:38
  82.2 23.9 %collective-permute-start.15 = (bf16[128,4096]{1,0:T(8,128)(2,1)S(1)}, bf16[128,4096]{1,0:T(8,128)(2,1)S(1)}, u32[]{:S(2)}, u32[]{:S(2)}) collective-permute-start(bf16[128,4096]{1,0:T(8,128)(2,1)S(1)} %constant_dynamic-update-slice_fusion.6.refs_0_), channel_id=1, source_target_pairs={{0,4},{4,0},{8,12},{12,8},{16,20},{20,16},{24,28},{28,24},{1,5},{5... | collective-permute-start | bytes 3145736 | tf_op jit(solution)/shard_map/ppermute | solution.py:34
  82.2 35.5 %collective-permute-start.13 = (bf16[128,4096]{1,0:T(8,128)(2,1)S(1)}, bf16[128,4096]{1,0:T(8,128)(2,1)}, u32[]{:S(2)}, u32[]{:S(2)}) collective-permute-start(bf16[128,4096]{1,0:T(8,128)(2,1)S(1)} %constant_dynamic-update-slice_fusion.6.refs_0_), channel_id=1, source_target_pairs={{0,16},{4,12},{8,24},{12,4},{16,0},{20,28},{24,8},{28,20},{1,17},{... | collective-permute-start | bytes 3145736 | tf_op jit(solution)/shard_map/ppermute | solution.py:38
  107.1 22.4 %collective-permute-start.11 = (bf16[128,4096]{1,0:T(8,128)(2,1)}, bf16[128,4096]{1,0:T(8,128)(2,1)}, u32[]{:S(2)}, u32[]{:S(2)}) collective-permute-start(bf16[128,4096]{1,0:T(8,128)(2,1)} %collective-permute-done.9.refs_6_), channel_id=1, source_target_pairs={{0,4},{4,0},{8,12},{12,8},{16,20},{20,16},{24,28},{28,24},{1,5},{5... | collective-permute-start | bytes 3145736 | tf_op jit(solution)/shard_map/ppermute | solution.py:34
  111.2 35.2 %collective-permute-start.19 = (bf16[128,4096]{1,0:T(8,128)(2,1)}, bf16[128,4096]{1,0:T(8,128)(2,1)}, u32[]{:S(2)}, u32[]{:S(2)}) collective-permute-start(bf16[128,4096]{1,0:T(8,128)(2,1)} %collective-permute-done.14.refs_2_), channel_id=1, source_target_pairs={{0,16},{4,12},{8,24},{12,4},{16,0},{20,28},{24,8},{28,20},{1,17},{... | collective-permute-start | bytes 3145736 | tf_op jit(solution)/shard_map/ppermute | solution.py:38
  113.4 29.1 %all-to-all-start.1 = ((bf16[32,72,128]{2,1,0:T(8,128)(2,1)}), bf16[32,72,128]{2,1,0:T(8,128)(2,1)}, u32[]{:S(2)}, u32[]{:S(2)}) async-start(bf16[32,72,128]{2,1,0:T(8,128)(2,1)} %reshape.379), calls=%async_computation.1 | async-start | bytes 1179648 | tf_op jit(solution)/shard_map/all_to_all | solution.py:746
  117.7 28.7 %collective-permute-start.20 = (bf16[128,4096]{1,0:T(8,128)(2,1)}, bf16[128,4096]{1,0:T(8,128)(2,1)}, u32[]{:S(2)}, u32[]{:S(2)}) collective-permute-start(bf16[128,4096]{1,0:T(8,128)(2,1)} %collective-permute-done.13.refs_4_), channel_id=1, source_target_pairs={{0,4},{4,0},{8,12},{12,8},{16,20},{20,16},{24,28},{28,24},{1,5},{5... | collective-permute-start | bytes 3145736 | tf_op jit(solution)/shard_map/ppermute | solution.py:34
  126.4 28.2 %collective-permute-start.17 = (bf16[512,1024]{1,0:T(8,128)(2,1)}, bf16[512,1024]{1,0:T(8,128)(2,1)}, u32[]{:S(2)}, u32[]{:S(2)}) collective-permute-start(bf16[512,1024]{1,0:T(8,128)(2,1)} %constant_dynamic-update-slice_fusion.10.refs_0_), channel_id=1, source_target_pairs={{0,8},{4,20},{8,0},{12,28},{16,24},{20,4},{24,16},{28,12},{1,9},{5... | collective-permute-start | bytes 3145736 | tf_op jit(solution)/shard_map/ppermute | solution.py:38
  129.5 25.1 %collective-permute-start.18 = (bf16[512,1024]{1,0:T(8,128)(2,1)}, bf16[512,1024]{1,0:T(8,128)(2,1)}, u32[]{:S(2)}, u32[]{:S(2)}) collective-permute-start(bf16[512,1024]{1,0:T(8,128)(2,1)} %constant_dynamic-update-slice_fusion.10.refs_0_), channel_id=1, source_target_pairs={{0,4},{4,0},{8,12},{12,8},{16,20},{20,16},{24,28},{28,24},{1,5},{5... | collective-permute-start | bytes 3145736 | tf_op jit(solution)/shard_map/ppermute | solution.py:34
  129.5 27.3 %collective-permute-start.22 = (bf16[512,1024]{1,0:T(8,128)(2,1)}, bf16[512,1024]{1,0:T(8,128)(2,1)}, u32[]{:S(2)}, u32[]{:S(2)}) collective-permute-start(bf16[512,1024]{1,0:T(8,128)(2,1)} %constant_dynamic-update-slice_fusion.10.refs_0_), channel_id=1, source_target_pairs={{0,16},{4,12},{8,24},{12,4},{16,0},{20,28},{24,8},{28,20},{1,17},{... | collective-permute-start | bytes 3145736 | tf_op jit(solution)/shard_map/ppermute | solution.py:38
  183.2 32.5 %collective-permute-start.35 = (bf16[2,512,1024]{2,1,0:T(8,128)(2,1)}, bf16[2,512,1024]{2,1,0:T(8,128)(2,1)}, u32[]{:S(2)}, u32[]{:S(2)}) collective-permute-start(bf16[2,512,1024]{2,1,0:T(8,128)(2,1)} %get-tuple-element.272), channel_id=1, source_target_pairs={{0,16},{4,12},{8,24},{12,4},{16,0},{20,28},{24,8},{28,20},{1,17},{... | collective-permute-start | bytes 6291464 | tf_op jit(solution)/shard_map/ppermute | solution.py:38
  204.8 33.4 %collective-permute-start.37 = (bf16[2,128,4096]{2,1,0:T(8,128)(2,1)}, bf16[2,128,4096]{2,1,0:T(8,128)(2,1)}, u32[]{:S(2)}, u32[]{:S(2)}) collective-permute-start(bf16[2,128,4096]{2,1,0:T(8,128)(2,1)} %get-tuple-element.287), channel_id=1, source_target_pairs={{0,16},{4,12},{8,24},{12,4},{16,0},{20,28},{24,8},{28,20},{1,17},{... | collective-permute-start | bytes 6291464 | tf_op jit(solution)/shard_map/ppermute | solution.py:38
  223.3 22.0 %collective-permute-start.36 = (bf16[512,1024]{1,0:T(8,128)(2,1)}, bf16[512,1024]{1,0:T(8,128)(2,1)}, u32[]{:S(2)}, u32[]{:S(2)}) collective-permute-start(bf16[512,1024]{1,0:T(8,128)(2,1)} %fusion.8), channel_id=1, source_target_pairs={{0,8},{4,20},{8,0},{12,28},{16,24},{20,4},{24,16},{28,12},{1,9},{5... | collective-permute-start | bytes 3145736 | tf_op jit(solution)/shard_map/ppermute | solution.py:38
  238.0 48.4 %collective-permute-start.43 = (bf16[2,128,4096]{2,1,0:T(8,128)(2,1)}, bf16[2,128,4096]{2,1,0:T(8,128)(2,1)}, u32[]{:S(2)}, u32[]{:S(2)}) collective-permute-start(bf16[2,128,4096]{2,1,0:T(8,128)(2,1)} %get-tuple-element.319), channel_id=1, source_target_pairs={{0,16},{4,12},{8,24},{12,4},{16,0},{20,28},{24,8},{28,20},{1,17},{... | collective-permute-start | bytes 6291464 | tf_op jit(solution)/shard_map/ppermute | solution.py:38
  240.8 27.1 %collective-permute-start.44 = (bf16[128,4096]{1,0:T(8,128)(2,1)}, bf16[128,4096]{1,0:T(8,128)(2,1)}, u32[]{:S(2)}, u32[]{:S(2)}) collective-permute-start(bf16[128,4096]{1,0:T(8,128)(2,1)} %fusion.7), channel_id=1, source_target_pairs={{0,8},{4,20},{8,0},{12,28},{16,24},{20,4},{24,16},{28,12},{1,9},{5... | collective-permute-start | bytes 3145736 | tf_op jit(solution)/shard_map/ppermute | solution.py:38
  249.8 41.3 %collective-permute-start.42 = (bf16[2,128,1024]{2,1,0:T(8,128)(2,1)}, bf16[2,128,1024]{2,1,0:T(8,128)(2,1)}, u32[]{:S(2)}, u32[]{:S(2)}) collective-permute-start(bf16[2,128,1024]{2,1,0:T(8,128)(2,1)} %fusion.18), channel_id=1, source_target_pairs={{0,1},{1,0},{2,3},{3,2},{4,5},{5,4},{6,7},{7,6},{8,9},{9,8},{10,11... | collective-permute-start | bytes 1572872 | tf_op jit(solution)/shard_map/ppermute | solution.py:41
  257.3 39.7 %all-to-all-start.2 = ((bf16[32,160,128]{2,1,0:T(8,128)(2,1)}), bf16[32,160,128]{2,1,0:T(8,128)(2,1)}, u32[]{:S(2)}, u32[]{:S(2)}) async-start(bf16[32,160,128]{2,1,0:T(8,128)(2,1)} %fusion.10), calls=%async_computation.2 | async-start | bytes 2621440 | tf_op jit(solution)/shard_map/all_to_all | solution.py:746
  270.7 36.9 %collective-permute-start.47 = (bf16[2,32,4096]{2,1,0:T(8,128)(2,1)}, bf16[2,32,4096]{2,1,0:T(8,128)(2,1)}, u32[]{:S(2)}, u32[]{:S(2)}) collective-permute-start(bf16[2,32,4096]{2,1,0:T(8,128)(2,1)} %fusion.19), channel_id=1, source_target_pairs={{0,1},{1,0},{2,3},{3,2},{4,5},{5,4},{6,7},{7,6},{8,9},{9,8},{10,11... | collective-permute-start | bytes 1572872 | tf_op jit(solution)/shard_map/ppermute | solution.py:41
  293.1 37.3 %collective-permute-start.50 = (bf16[128,1024]{1,0:T(8,128)(2,1)}, bf16[128,1024]{1,0:T(8,128)(2,1)S(1)}, u32[]{:S(2)}, u32[]{:S(2)}) collective-permute-start(bf16[128,1024]{1,0:T(8,128)(2,1)} %fusion.25), channel_id=1, source_target_pairs={{0,2},{1,3},{2,0},{3,1},{4,6},{5,7},{6,4},{7,5},{8,10},{9,11},{10,... | collective-permute-start | bytes 786440 | tf_op jit(solution)/shard_map/ppermute | solution.py:41
  308.9 22.4 %collective-permute-start.49 = (bf16[32,4096]{1,0:T(8,128)(2,1)S(1)}, bf16[32,4096]{1,0:T(8,128)(2,1)S(1)}, u32[]{:S(2)}, u32[]{:S(2)}) collective-permute-start(bf16[32,4096]{1,0:T(8,128)(2,1)S(1)} %fusion.26), channel_id=1, source_target_pairs={{0,2},{1,3},{2,0},{3,1},{4,6},{5,7},{6,4},{7,5},{8,10},{9,11},{10,... | collective-permute-start | bytes 786440 | tf_op jit(solution)/shard_map/ppermute | solution.py:41
  (89 other events, 912.4 us)

commit v3 on v2

--- a/solution.py
+++ b/solution.py
@@ -139,7 +139,6 @@
         owners = grid.n_dp * grid.n_z
         edges = [0, *cuts, self.cols]
         spans = list(zip(edges[:-1], edges[1:]))
-        copies = owners * count * len(spans)
 
         def kernel(me_ref, *refs):
             sources = refs[: len(pieces)]
@@ -147,25 +146,22 @@
             sems = refs[-1]
             me = me_ref[0]
             odd = (me // grid.n_z) % 2 == 1
-            started = []
             for source, (_, even_mask, odd_mask) in zip(sources, pieces):
                 mask = jnp.where(odd, jnp.int32(odd_mask), jnp.int32(even_mask))
                 for at, z in enumerate(z_marks):
                     owner = lax.bitwise_xor(me, mask * grid.n_z + z)
                     for k in range(count):
                         to = pl.multiple_of((owner * count + k) * block, block)
-                        for result, (lo, hi) in zip(results, spans):
-                            copy = pltpu.make_async_copy(
+                        for n, (result, (lo, hi)) in enumerate(zip(results, spans)):
+                            pltpu.make_async_copy(
                                 source.at[
                                     pl.ds(at * block, block), pl.ds(k * self.cols + lo, hi - lo)
                                 ],
                                 result.at[pl.ds(to, block)],
-                                sems.at[len(started)],
-                            )
-                            copy.start()
-                            started.append(copy)
-            for copy in started:
-                copy.wait()
+                                sems.at[n],
+                            ).start()
+            for n, result in enumerate(results):
+                pltpu.make_async_copy(result, result, sems.at[n]).wait()
 
         arrays = self.clock.gate(*[v for v, _, _ in pieces])
         rows = owners * count * block
@@ -177,7 +173,7 @@
                 grid=(),
                 in_specs=[pl.BlockSpec(memory_space=pl.ANY)] * len(pieces),
                 out_specs=[pl.BlockSpec(memory_space=pltpu.VMEM)] * len(spans),
-                scratch_shapes=[pltpu.SemaphoreType.DMA((copies,))],
+                scratch_shapes=[pltpu.SemaphoreType.DMA((len(spans),))],
             ),
             compiler_params=pltpu.CompilerParams(vmem_limit_bytes=10 << 20),
             cost_estimate=pl.CostEstimate(flops=0, bytes_accessed=0, transcendentals=0),
@@ -281,15 +277,20 @@
 
             terms = [contract_rows(a[...], b[...]) for a, b in zip(lefts, rights)]
             term = jnp.concatenate(terms, axis=1) if count > 1 else terms[0]
+            whole = term
+            if added:
+                for k in range(places):
+
+                    @pl.when(step == k)
+                    def _(k=k):
+                        fetch(k).wait()
+
+                whole = term + fetched[0][step].astype(F32)
+            blocks[step] = whole.astype(BF16)
             for k in range(places):
 
                 @pl.when(step == k)
                 def _(k=k):
-                    whole = term
-                    if added:
-                        fetch(k).wait()
-                        whole = whole + fetched[0][k].astype(F32)
-                    blocks[k] = whole.astype(BF16)
                     put(k).start()
 
             @pl.when(step == places - 1)

time: 348 us -> 342 us (0.983); the launches traced: 342 us -> 341 us
  transfers between devices with their start and end apart: 54 -> 54, of which waited for: 16 -> 17; matrix products, arithmetic and copies ran while one was open for 25% -> 25% of each run, Pallas kernels for 17% -> 17%
where the time goes in v3:
time: 342 us; the launch traced here: 341 us
  waiting for transfers between devices  105 us (31%)
  starting transfers between devices  73.2 us (21%)
  Pallas kernels  61.3 us (18%)
  local copies, waits for them, and re-layouts  44.5 us (13%)
  other arithmetic  36.2 us (11%)
  matrix products  18.3 us (5%)
    ppermute x15, waiting for transfers between devices, crossed(): return lax.ppermute(value, 'dp', pairs)  54.8 us
    ppermute x12, waiting for transfers between devices, over_z(): return lax.ppermute(value, 'fsdp', [(i, i ^ mask) for i in range(self.n_z)])  48.7 us
    ppermute x12, starting transfers between devices, over_z(): return lax.ppermute(value, 'fsdp', [(i, i ^ mask) for i in range(self.n_z)])  27.9 us
    pallas_call x6, Pallas kernels, call(): pl.pallas_call(kernel, out_shape=shapes, grid_spec=pltpu.PrefetchScalarGr...  22.8 us
    ppermute x15, starting transfers between devices, crossed(): return lax.ppermute(value, 'dp', pairs)  20.8 us
    all_to_all x3, starting transfers between devices, swap(): block = lax.all_to_all(block, AXES, split_axis=0, concat_axis=0, tiled=True)  19.7 us
    unnamed x132, local copies, waits for them, and re-layouts  14.3 us
    pallas_call x2, Pallas kernels, norm_back(): pl.pallas_call(kernel, out_shape=[jax.ShapeDtypeStruct(*s) for s in shape...  12.9 us
  transfers between devices with their start and end apart: 54, of which 17 were waited for; matrix products, arithmetic and copies ran while one was open for 25% of the time, Pallas kernels for 17%

profile of v3, /device:TPU:0, one launch (start us, length us, event | category | flops | bytes accessed | tf_op | source)
XLA Modules:
  0.0 340.9 jit_solution(2982078133465402602)
XLA Ops:
  1.7 4.1 %collective-permute-start = (bf16[32,4096]{1,0:T(8,128)(2,1)S(1)}, bf16[32,4096]{1,0:T(8,128)(2,1)S(1)}, u32[]{:S(2)}, u32[]{:S(2)}) collective-permute-start(bf16[32,4096]{1,0:T(8,128)(2,1)S(1)} %pad_maximum_fusion.1), channel_id=1, source_target_pairs={{0,2},{1,3},{2,0},{3,1},{4,6},{5,7},{6,4},{7,5},{8,10},{9,11},{10,... | collective-permute-start | bytes 786440 | tf_op jit(solution)/shard_map/ppermute | solution.py:41
  23.3 13.3 %collective-permute-done.2 = bf16[64,4096]{1,0:T(8,128)(2,1)S(1)} collective-permute-done((bf16[64,4096]{1,0:T(8,128)(2,1)S(1)}, bf16[64,4096]{1,0:T(8,128)(2,1)S(1)}, u32[]{:S(2)}, u32[]{:S(2)}) %collective-permute-start.2) | collective-permute-done | bytes 524320 | tf_op jit(solution)/shard_map/ppermute | solution.py:41
  43.5 6.1 %all-to-all-start = ((bf16[32,88,128]{2,1,0:T(8,128)(2,1)}), bf16[32,88,128]{2,1,0:T(8,128)(2,1)}, u32[]{:S(2)}, u32[]{:S(2)}) async-start(bf16[32,88,128]{2,1,0:T(8,128)(2,1)} %pad_maximum_fusion), calls=%async_computation | async-start | bytes 1441792 | tf_op jit(solution)/shard_map/all_to_all | solution.py:747
  56.3 15.2 %collective-permute-done.4.refs_4_ = bf16[128,4096]{1,0:T(8,128)(2,1)} collective-permute-done((bf16[128,4096]{1,0:T(8,128)(2,1)S(1)}, bf16[128,4096]{1,0:T(8,128)(2,1)}, u32[]{:S(2)}, u32[]{:S(2)}) %collective-permute-start.4) | collective-permute-done | bytes 1048608 | tf_op jit(solution)/shard_map/ppermute | solution.py:38
  88.8 9.0 %collective-permute-done.8 = bf16[128,1024]{1,0:T(8,128)(2,1)S(1)} collective-permute-done((bf16[128,1024]{1,0:T(8,128)(2,1)S(1)}, bf16[128,1024]{1,0:T(8,128)(2,1)S(1)}, u32[]{:S(2)}, u32[]{:S(2)}) %collective-permute-start.8) | collective-permute-done | bytes 262176 | tf_op jit(solution)/shard_map/ppermute | solution.py:41
  97.8 8.2 %collective-permute-done.14.refs_2_ = bf16[128,4096]{1,0:T(8,128)(2,1)} collective-permute-done((bf16[128,4096]{1,0:T(8,128)(2,1)S(1)}, bf16[128,4096]{1,0:T(8,128)(2,1)}, u32[]{:S(2)}, u32[]{:S(2)}) %collective-permute-start.14) | collective-permute-done | bytes 1048608 | tf_op jit(solution)/shard_map/ppermute | solution.py:38
  113.4 4.2 %all-to-all-start.1 = ((bf16[32,72,128]{2,1,0:T(8,128)(2,1)}), bf16[32,72,128]{2,1,0:T(8,128)(2,1)}, u32[]{:S(2)}, u32[]{:S(2)}) async-start(bf16[32,72,128]{2,1,0:T(8,128)(2,1)} %reshape.379), calls=%async_computation.1 | async-start | bytes 1179648 | tf_op jit(solution)/shard_map/all_to_all | solution.py:747
  117.8 6.1 %collective-permute-done.12 = bf16[256,1024]{1,0:T(8,128)(2,1)} collective-permute-done((bf16[256,1024]{1,0:T(8,128)(2,1)S(1)}, bf16[256,1024]{1,0:T(8,128)(2,1)}, u32[]{:S(2)}, u32[]{:S(2)}) %collective-permute-start.12) | collective-permute-done | bytes 524320 | tf_op jit(solution)/shard_map/ppermute | solution.py:41
  131.2 3.6 %assemble.3 = (bf16[1024,3072]{1,0:T(8,128)(2,1)S(1)}, bf16[1024,1024]{1,0:T(8,128)(2,1)S(1)}) custom-call(s32[1]{0:T(128)} %bitcast.19.me_ref, bf16[128,4096]{1,0:T(8,128)(2,1)S(1)} %constant_dynamic-update-slice_fusion.2.refs_0_, bf16[128,4096]{1,0:T(8,128)(2,1)S(1)} %copy-done.30, bf16[128,4096]{1,0:T(8,128)(2,1)S(1)} %copy-done.28, ...), custom_call_target="tpu_custom_call" | custom-call | tf_op jit(solution)/shard_map/assemble/pallas_call | solution.py:168
  138.1 3.8 %attend.1.refs_1_ = bf16[256,1024]{1,0:T(8,128)(2,1)S(1)} custom-call(s32[1]{0:T(128)} %dynamic_slice.54.first_ref, bf16[256,3072]{1,0:T(8,128)(2,1)S(1)} %fusion.4.query.key.value, bf16[256,3072]{1,0:T(8,128)(2,1)S(1)} %fusion.4.query.key.value, bf16[256,3072]{1,0:T(8,128)(2,1)S(1)} %fusion.4.query.key.value), custom_call_target="tpu_custom_call" | custom-call | tf_op jit(solution)/shard_map/attend/pallas_call | solution.py:491
  157.1 4.4 %fusion.3 = (f32[256,4096]{1,0:T(8,128)S(1)}, bf16[256,4096]{1,0:T(8,128)(2,1)S(1)}) fusion(f32[4096]{0:T(1024)S(1)} %bitcast.179, bf16[256,1024]{1,0:T(8,128)(2,1)S(1)} %get-tuple-element.281.refs_0_, bf16[1024,4096]{1,0:T(8,128)(2,1)S(1)} %assemble.4.weight), kind=kOutput, calls=%fused_computation.5 | convolution fusion | flops 2159017984 | bytes 15220736 | tf_op jit(solution)/shard_map/dot_general | solution.py:824
  164.0 5.8 %collective-permute-done.24.refs_6_ = bf16[512,1024]{1,0:T(8,128)(2,1)S(1)} collective-permute-done((bf16[512,1024]{1,0:T(8,128)(2,1)}, bf16[512,1024]{1,0:T(8,128)(2,1)S(1)}, u32[]{:S(2)}, u32[]{:S(2)}) %collective-permute-start.24) | collective-permute-done | bytes 1048608 | tf_op jit(solution)/shard_map/ppermute | solution.py:38
  178.5 3.8 %outer.7 = (bf16[512,1024]{1,0:T(8,128)(2,1)S(1)}, bf16[512,1024]{1,0:T(8,128)(2,1)S(1)}, bf16[2,512,1024]{2,1,0:T(8,128)(2,1)}) custom-call(s32[1]{0:T(128)} %bitcast.26.dp_ref, bf16[256,4096]{1,0:T(8,128)(2,1)S(1)} %get-tuple-element.324.refs_0_, bf16[256,1024]{1,0:T(8,128)(2,1)S(1)} %get-tuple-element.267.refs_1_.grad.passed_at, ...), custom_call_target="tpu_custom_call" | custom-call | tf_op jit(solution)/shard_map/outer/pallas_call | solution.py:307
  190.4 7.0 %norm_back.2 = (bf16[256,1024]{1,0:T(8,128)(2,1)S(1)}, f32[8,1024]{1,0:T(8,128)S(1)}, f32[256,1024]{1,0:T(8,128)S(1)}) custom-call(bf16[256,4096]{1,0:T(8,128)(2,1)S(1)} %copy-done.5, bf16[1024,4096]{1,0:T(8,128)(2,1)} %copy-done.3, f32[256,1024]{1,0:T(8,128)} %get-tuple-element.362.unit_at, f32[1,1024]{1,0:T(1,128)S(1)} %get-tuple-element.377.gain, ...), custom_call_target="tpu_custom_call" | custom-call | tf_op jit(solution)/shard_map/norm_back/pallas_call | solution.py:643
  198.4 5.6 %outer.9 = (bf16[128,4096]{1,0:T(8,128)(2,1)S(1)}, bf16[128,4096]{1,0:T(8,128)(2,1)S(1)}, bf16[2,128,4096]{2,1,0:T(8,128)(2,1)}) custom-call(s32[1]{0:T(128)} %bitcast.26.dp_ref, bf16[256,1024]{1,0:T(8,128)(2,1)S(1)} %get-tuple-element.281.refs_0_, bf16[256,4096]{1,0:T(8,128)(2,1)S(1)} %copy-done.6, bf16[128,4096]{1,0:T(8,128)(2,1)} %collective-permute-done.31.refs_2_, ...), custom_call_target="tpu_custom_call" | custom-call | tf_op jit(solution)/shard_map/outer/pallas_call | solution.py:307
  205.0 9.8 %attend_back.1 = (bf16[256,3072]{1,0:T(8,128)(2,1)S(1)}, f32[1,3072]{1,0:T(1,128)S(1)}) custom-call(s32[1]{0:T(128)} %dynamic_slice.54.first_ref, bf16[256,3072]{1,0:T(8,128)(2,1)S(1)} %fusion.4.query.key.value, bf16[256,3072]{1,0:T(8,128)(2,1)S(1)} %fusion.4.query.key.value, bf16[256,3072]{1,0:T(8,128)(2,1)S(1)} %fusion.4.query.key.value, ...), custom_call_target="tpu_custom_call" | custom-call | tf_op jit(solution)/shard_map/attend_back/pallas_call | solution.py:533
  223.6 5.9 %norm_back.3 = (bf16[256,1024]{1,0:T(8,128)(2,1)S(1)}, f32[8,1024]{1,0:T(8,128)S(1)}) custom-call(bf16[256,3072]{1,0:T(8,128)(2,1)S(1)} %get-tuple-element.313.refs_2_.grad, bf16[1024,3072]{1,0:T(8,128)(2,1)} %copy-done.13, f32[256,1024]{1,0:T(8,128)} %get-tuple-element.364.unit_at, f32[1,1024]{1,0:T(1,128)S(1)} %get-tuple-element.376.gain, ...), custom_call_target="tpu_custom_call" | custom-call | tf_op jit(solution)/shard_map/norm_back/pallas_call | solution.py:643
  229.6 4.4 %outer.11 = (bf16[128,4096]{1,0:T(8,128)(2,1)S(1)}, bf16[128,4096]{1,0:T(8,128)(2,1)S(1)}, bf16[2,128,4096]{2,1,0:T(8,128)(2,1)}) custom-call(s32[1]{0:T(128)} %bitcast.26.dp_ref, bf16[256,1024]{1,0:T(8,128)(2,1)S(1)} %copy-done.16, bf16[256,1024]{1,0:T(8,128)(2,1)S(1)} %copy-done.12, bf16[256,3072]{1,0:T(8,128)(2,1)S(1)} %get-tuple-element.313.refs_2_.grad, ...), custom_call_target="tpu_custom_call" | custom-call | tf_op jit(solution)/shard_map/outer/pallas_call | solution.py:307
  256.0 9.5 %all-to-all-start.2 = ((bf16[32,160,128]{2,1,0:T(8,128)(2,1)}), bf16[32,160,128]{2,1,0:T(8,128)(2,1)}, u32[]{:S(2)}, u32[]{:S(2)}) async-start(bf16[32,160,128]{2,1,0:T(8,128)(2,1)} %fusion.10), calls=%async_computation.2 | async-start | bytes 2621440 | tf_op jit(solution)/shard_map/all_to_all | solution.py:747
  269.9 16.4 %collective-permute-done.43 = bf16[2,128,4096]{2,1,0:T(8,128)(2,1)} collective-permute-done((bf16[2,128,4096]{2,1,0:T(8,128)(2,1)}, bf16[2,128,4096]{2,1,0:T(8,128)(2,1)}, u32[]{:S(2)}, u32[]{:S(2)}) %collective-permute-start.43) | collective-permute-done | bytes 2097184 | tf_op jit(solution)/shard_map/ppermute | solution.py:38
  300.6 4.6 %collective-permute-done.45 = bf16[128,4096]{1,0:T(8,128)(2,1)} collective-permute-done((bf16[128,4096]{1,0:T(8,128)(2,1)}, bf16[128,4096]{1,0:T(8,128)(2,1)}, u32[]{:S(2)}, u32[]{:S(2)}) %collective-permute-start.45) | collective-permute-done | bytes 1048608 | tf_op jit(solution)/shard_map/ppermute | solution.py:38
  308.6 6.3 %collective-permute-start.49 = (bf16[32,4096]{1,0:T(8,128)(2,1)S(1)}, bf16[32,4096]{1,0:T(8,128)(2,1)S(1)}, u32[]{:S(2)}, u32[]{:S(2)}) collective-permute-start(bf16[32,4096]{1,0:T(8,128)(2,1)S(1)} %fusion.26), channel_id=1, source_target_pairs={{0,2},{1,3},{2,0},{3,1},{4,6},{5,7},{6,4},{7,5},{8,10},{9,11},{10,... | collective-permute-start | bytes 786440 | tf_op jit(solution)/shard_map/ppermute | solution.py:41
  315.1 9.4 %collective-permute-done.46 = bf16[2,32,4096]{2,1,0:T(8,128)(2,1)S(1)} collective-permute-done((bf16[2,32,4096]{2,1,0:T(8,128)(2,1)S(1)}, bf16[2,32,4096]{2,1,0:T(8,128)(2,1)S(1)}, u32[]{:S(2)}, u32[]{:S(2)}) %collective-permute-start.46) | collective-permute-done | bytes 524320 | tf_op jit(solution)/shard_map/ppermute | solution.py:41
  332.0 7.4 %collective-permute-done.48 = bf16[32,4096]{1,0:T(8,128)(2,1)S(1)} collective-permute-done((bf16[32,4096]{1,0:T(8,128)(2,1)S(1)}, bf16[32,4096]{1,0:T(8,128)(2,1)S(1)}, u32[]{:S(2)}, u32[]{:S(2)}) %collective-permute-start.48) | collective-permute-done | bytes 262176 | tf_op jit(solution)/shard_map/ppermute | solution.py:41
  (348 shorter events, 164.9 us)
Async XLA Ops:
  43.5 30.0 %all-to-all-start = ((bf16[32,88,128]{2,1,0:T(8,128)(2,1)}), bf16[32,88,128]{2,1,0:T(8,128)(2,1)}, u32[]{:S(2)}, u32[]{:S(2)}) async-start(bf16[32,88,128]{2,1,0:T(8,128)(2,1)} %pad_maximum_fusion), calls=%async_computation | async-start | bytes 1441792 | tf_op jit(solution)/shard_map/all_to_all | solution.py:747
  49.6 21.9 %collective-permute-start.4 = (bf16[128,4096]{1,0:T(8,128)(2,1)S(1)}, bf16[128,4096]{1,0:T(8,128)(2,1)}, u32[]{:S(2)}, u32[]{:S(2)}) collective-permute-start(bf16[128,4096]{1,0:T(8,128)(2,1)S(1)} %constant_dynamic-update-slice_fusion.2.refs_0_), channel_id=1, source_target_pairs={{0,16},{4,12},{8,24},{12,4},{16,0},{20,28},{24,8},{28,20},{1,17},{... | collective-permute-start | bytes 3145736 | tf_op jit(solution)/shard_map/ppermute | solution.py:38
  52.5 26.0 %collective-permute-start.3 = (bf16[64,4096]{1,0:T(8,128)(2,1)}, bf16[64,4096]{1,0:T(8,128)(2,1)}, u32[]{:S(2)}, u32[]{:S(2)}) collective-permute-start(bf16[64,4096]{1,0:T(8,128)(2,1)} %constant_dynamic-update-slice_fusion.4), channel_id=1, source_target_pairs={{0,1},{1,0},{2,3},{3,2},{4,5},{5,4},{6,7},{7,6},{8,9},{9,8},{10,11... | collective-permute-start | bytes 1572872 | tf_op jit(solution)/shard_map/ppermute | solution.py:41
  55.0 28.0 %collective-permute-start.9 = (bf16[128,4096]{1,0:T(8,128)(2,1)S(1)}, bf16[128,4096]{1,0:T(8,128)(2,1)}, u32[]{:S(2)}, u32[]{:S(2)}) collective-permute-start(bf16[128,4096]{1,0:T(8,128)(2,1)S(1)} %collective-permute-done.5.refs_2_), channel_id=1, source_target_pairs={{0,16},{4,12},{8,24},{12,4},{16,0},{20,28},{24,8},{28,20},{1,17},{... | collective-permute-start | bytes 3145736 | tf_op jit(solution)/shard_map/ppermute | solution.py:38
  80.7 25.3 %collective-permute-start.14 = (bf16[128,4096]{1,0:T(8,128)(2,1)S(1)}, bf16[128,4096]{1,0:T(8,128)(2,1)}, u32[]{:S(2)}, u32[]{:S(2)}) collective-permute-start(bf16[128,4096]{1,0:T(8,128)(2,1)S(1)} %constant_dynamic-update-slice_fusion.6.refs_0_), channel_id=1, source_target_pairs={{0,8},{4,20},{8,0},{12,28},{16,24},{20,4},{24,16},{28,12},{1,9},{5... | collective-permute-start | bytes 3145736 | tf_op jit(solution)/shard_map/ppermute | solution.py:38
  82.2 23.9 %collective-permute-start.15 = (bf16[128,4096]{1,0:T(8,128)(2,1)S(1)}, bf16[128,4096]{1,0:T(8,128)(2,1)S(1)}, u32[]{:S(2)}, u32[]{:S(2)}) collective-permute-start(bf16[128,4096]{1,0:T(8,128)(2,1)S(1)} %constant_dynamic-update-slice_fusion.6.refs_0_), channel_id=1, source_target_pairs={{0,4},{4,0},{8,12},{12,8},{16,20},{20,16},{24,28},{28,24},{1,5},{5... | collective-permute-start | bytes 3145736 | tf_op jit(solution)/shard_map/ppermute | solution.py:34
  82.2 35.5 %collective-permute-start.13 = (bf16[128,4096]{1,0:T(8,128)(2,1)S(1)}, bf16[128,4096]{1,0:T(8,128)(2,1)}, u32[]{:S(2)}, u32[]{:S(2)}) collective-permute-start(bf16[128,4096]{1,0:T(8,128)(2,1)S(1)} %constant_dynamic-update-slice_fusion.6.refs_0_), channel_id=1, source_target_pairs={{0,16},{4,12},{8,24},{12,4},{16,0},{20,28},{24,8},{28,20},{1,17},{... | collective-permute-start | bytes 3145736 | tf_op jit(solution)/shard_map/ppermute | solution.py:38
  107.1 22.5 %collective-permute-start.11 = (bf16[128,4096]{1,0:T(8,128)(2,1)}, bf16[128,4096]{1,0:T(8,128)(2,1)}, u32[]{:S(2)}, u32[]{:S(2)}) collective-permute-start(bf16[128,4096]{1,0:T(8,128)(2,1)} %collective-permute-done.9.refs_6_), channel_id=1, source_target_pairs={{0,4},{4,0},{8,12},{12,8},{16,20},{20,16},{24,28},{28,24},{1,5},{5... | collective-permute-start | bytes 3145736 | tf_op jit(solution)/shard_map/ppermute | solution.py:34
  111.2 34.7 %collective-permute-start.19 = (bf16[128,4096]{1,0:T(8,128)(2,1)}, bf16[128,4096]{1,0:T(8,128)(2,1)}, u32[]{:S(2)}, u32[]{:S(2)}) collective-permute-start(bf16[128,4096]{1,0:T(8,128)(2,1)} %collective-permute-done.14.refs_2_), channel_id=1, source_target_pairs={{0,16},{4,12},{8,24},{12,4},{16,0},{20,28},{24,8},{28,20},{1,17},{... | collective-permute-start | bytes 3145736 | tf_op jit(solution)/shard_map/ppermute | solution.py:38
  113.4 28.6 %all-to-all-start.1 = ((bf16[32,72,128]{2,1,0:T(8,128)(2,1)}), bf16[32,72,128]{2,1,0:T(8,128)(2,1)}, u32[]{:S(2)}, u32[]{:S(2)}) async-start(bf16[32,72,128]{2,1,0:T(8,128)(2,1)} %reshape.379), calls=%async_computation.1 | async-start | bytes 1179648 | tf_op jit(solution)/shard_map/all_to_all | solution.py:747
  117.7 28.2 %collective-permute-start.20 = (bf16[128,4096]{1,0:T(8,128)(2,1)}, bf16[128,4096]{1,0:T(8,128)(2,1)}, u32[]{:S(2)}, u32[]{:S(2)}) collective-permute-start(bf16[128,4096]{1,0:T(8,128)(2,1)} %collective-permute-done.13.refs_4_), channel_id=1, source_target_pairs={{0,4},{4,0},{8,12},{12,8},{16,20},{20,16},{24,28},{28,24},{1,5},{5... | collective-permute-start | bytes 3145736 | tf_op jit(solution)/shard_map/ppermute | solution.py:34
  126.6 27.2 %collective-permute-start.17 = (bf16[512,1024]{1,0:T(8,128)(2,1)}, bf16[512,1024]{1,0:T(8,128)(2,1)}, u32[]{:S(2)}, u32[]{:S(2)}) collective-permute-start(bf16[512,1024]{1,0:T(8,128)(2,1)} %constant_dynamic-update-slice_fusion.10.refs_0_), channel_id=1, source_target_pairs={{0,8},{4,20},{8,0},{12,28},{16,24},{20,4},{24,16},{28,12},{1,9},{5... | collective-permute-start | bytes 3145736 | tf_op jit(solution)/shard_map/ppermute | solution.py:38
  129.6 24.2 %collective-permute-start.18 = (bf16[512,1024]{1,0:T(8,128)(2,1)}, bf16[512,1024]{1,0:T(8,128)(2,1)}, u32[]{:S(2)}, u32[]{:S(2)}) collective-permute-start(bf16[512,1024]{1,0:T(8,128)(2,1)} %constant_dynamic-update-slice_fusion.10.refs_0_), channel_id=1, source_target_pairs={{0,4},{4,0},{8,12},{12,8},{16,20},{20,16},{24,28},{28,24},{1,5},{5... | collective-permute-start | bytes 3145736 | tf_op jit(solution)/shard_map/ppermute | solution.py:34
  129.6 27.2 %collective-permute-start.22 = (bf16[512,1024]{1,0:T(8,128)(2,1)}, bf16[512,1024]{1,0:T(8,128)(2,1)}, u32[]{:S(2)}, u32[]{:S(2)}) collective-permute-start(bf16[512,1024]{1,0:T(8,128)(2,1)} %constant_dynamic-update-slice_fusion.10.refs_0_), channel_id=1, source_target_pairs={{0,16},{4,12},{8,24},{12,4},{16,0},{20,28},{24,8},{28,20},{1,17},{... | collective-permute-start | bytes 3145736 | tf_op jit(solution)/shard_map/ppermute | solution.py:38
  182.3 32.6 %collective-permute-start.35 = (bf16[2,512,1024]{2,1,0:T(8,128)(2,1)}, bf16[2,512,1024]{2,1,0:T(8,128)(2,1)}, u32[]{:S(2)}, u32[]{:S(2)}) collective-permute-start(bf16[2,512,1024]{2,1,0:T(8,128)(2,1)} %get-tuple-element.272), channel_id=1, source_target_pairs={{0,16},{4,12},{8,24},{12,4},{16,0},{20,28},{24,8},{28,20},{1,17},{... | collective-permute-start | bytes 6291464 | tf_op jit(solution)/shard_map/ppermute | solution.py:38
  204.1 33.1 %collective-permute-start.37 = (bf16[2,128,4096]{2,1,0:T(8,128)(2,1)}, bf16[2,128,4096]{2,1,0:T(8,128)(2,1)}, u32[]{:S(2)}, u32[]{:S(2)}) collective-permute-start(bf16[2,128,4096]{2,1,0:T(8,128)(2,1)} %get-tuple-element.287), channel_id=1, source_target_pairs={{0,16},{4,12},{8,24},{12,4},{16,0},{20,28},{24,8},{28,20},{1,17},{... | collective-permute-start | bytes 6291464 | tf_op jit(solution)/shard_map/ppermute | solution.py:38
  222.1 21.9 %collective-permute-start.36 = (bf16[512,1024]{1,0:T(8,128)(2,1)}, bf16[512,1024]{1,0:T(8,128)(2,1)}, u32[]{:S(2)}, u32[]{:S(2)}) collective-permute-start(bf16[512,1024]{1,0:T(8,128)(2,1)} %fusion.8), channel_id=1, source_target_pairs={{0,8},{4,20},{8,0},{12,28},{16,24},{20,4},{24,16},{28,12},{1,9},{5... | collective-permute-start | bytes 3145736 | tf_op jit(solution)/shard_map/ppermute | solution.py:38
  235.9 50.4 %collective-permute-start.43 = (bf16[2,128,4096]{2,1,0:T(8,128)(2,1)}, bf16[2,128,4096]{2,1,0:T(8,128)(2,1)}, u32[]{:S(2)}, u32[]{:S(2)}) collective-permute-start(bf16[2,128,4096]{2,1,0:T(8,128)(2,1)} %get-tuple-element.319), channel_id=1, source_target_pairs={{0,16},{4,12},{8,24},{12,4},{16,0},{20,28},{24,8},{28,20},{1,17},{... | collective-permute-start | bytes 6291464 | tf_op jit(solution)/shard_map/ppermute | solution.py:38
  239.7 26.7 %collective-permute-start.44 = (bf16[128,4096]{1,0:T(8,128)(2,1)}, bf16[128,4096]{1,0:T(8,128)(2,1)}, u32[]{:S(2)}, u32[]{:S(2)}) collective-permute-start(bf16[128,4096]{1,0:T(8,128)(2,1)} %fusion.7), channel_id=1, source_target_pairs={{0,8},{4,20},{8,0},{12,28},{16,24},{20,4},{24,16},{28,12},{1,9},{5... | collective-permute-start | bytes 3145736 | tf_op jit(solution)/shard_map/ppermute | solution.py:38
  248.4 40.9 %collective-permute-start.42 = (bf16[2,128,1024]{2,1,0:T(8,128)(2,1)}, bf16[2,128,1024]{2,1,0:T(8,128)(2,1)}, u32[]{:S(2)}, u32[]{:S(2)}) collective-permute-start(bf16[2,128,1024]{2,1,0:T(8,128)(2,1)} %fusion.18), channel_id=1, source_target_pairs={{0,1},{1,0},{2,3},{3,2},{4,5},{5,4},{6,7},{7,6},{8,9},{9,8},{10,11... | collective-permute-start | bytes 1572872 | tf_op jit(solution)/shard_map/ppermute | solution.py:41
  256.0 39.7 %all-to-all-start.2 = ((bf16[32,160,128]{2,1,0:T(8,128)(2,1)}), bf16[32,160,128]{2,1,0:T(8,128)(2,1)}, u32[]{:S(2)}, u32[]{:S(2)}) async-start(bf16[32,160,128]{2,1,0:T(8,128)(2,1)} %fusion.10), calls=%async_computation.2 | async-start | bytes 2621440 | tf_op jit(solution)/shard_map/all_to_all | solution.py:747
  269.3 38.1 %collective-permute-start.47 = (bf16[2,32,4096]{2,1,0:T(8,128)(2,1)}, bf16[2,32,4096]{2,1,0:T(8,128)(2,1)}, u32[]{:S(2)}, u32[]{:S(2)}) collective-permute-start(bf16[2,32,4096]{2,1,0:T(8,128)(2,1)} %fusion.19), channel_id=1, source_target_pairs={{0,1},{1,0},{2,3},{3,2},{4,5},{5,4},{6,7},{7,6},{8,9},{9,8},{10,11... | collective-permute-start | bytes 1572872 | tf_op jit(solution)/shard_map/ppermute | solution.py:41
  291.2 38.0 %collective-permute-start.50 = (bf16[128,1024]{1,0:T(8,128)(2,1)}, bf16[128,1024]{1,0:T(8,128)(2,1)S(1)}, u32[]{:S(2)}, u32[]{:S(2)}) collective-permute-start(bf16[128,1024]{1,0:T(8,128)(2,1)} %fusion.25), channel_id=1, source_target_pairs={{0,2},{1,3},{2,0},{3,1},{4,6},{5,7},{6,4},{7,5},{8,10},{9,11},{10,... | collective-permute-start | bytes 786440 | tf_op jit(solution)/shard_map/ppermute | solution.py:41
  308.6 21.5 %collective-permute-start.49 = (bf16[32,4096]{1,0:T(8,128)(2,1)S(1)}, bf16[32,4096]{1,0:T(8,128)(2,1)S(1)}, u32[]{:S(2)}, u32[]{:S(2)}) collective-permute-start(bf16[32,4096]{1,0:T(8,128)(2,1)S(1)} %fusion.26), channel_id=1, source_target_pairs={{0,2},{1,3},{2,0},{3,1},{4,6},{5,7},{6,4},{7,5},{8,10},{9,11},{10,... | collective-permute-start | bytes 786440 | tf_op jit(solution)/shard_map/ppermute | solution.py:41
  (89 other events, 914.0 us)

commit v4 on v3

--- a/solution.py
+++ b/solution.py
@@ -881,10 +881,10 @@
 
     for_up.third()
     for_attn.second()
-    for_down.fourth()
     returned, small_back = clock.gate(returned, small_back)
     clock.tick(returned)
     for_attn.third()
+    for_down.fourth()
     for_up.fourth()
     for_attn.fourth()
     returned = clock.gate(returned)

time: 342 us -> 350 us (1.023)
  waiting for transfers between devices: 105 us -> 120 us
  starting transfers between devices: 73.2 us -> 67.4 us
    ppermute x12, waiting for transfers between devices: 48.7 us -> 58.6 us  [over_z(): return lax.ppermute(value, 'fsdp', [(i, i ^ mask) for i in range(self.n_z)])]
    all_to_all x3, waiting for transfers between devices: 0.01 us -> 6.3 us  [swap(): block = lax.all_to_all(block, AXES, split_axis=0, concat_axis=0, tiled=True)]
    ppermute x12, starting transfers between devices: 27.9 us -> 22 us  [over_z(): return lax.ppermute(value, 'fsdp', [(i, i ^ mask) for i in range(self.n_z)])]
  transfers between devices with their start and end apart: 54 -> 54, of which waited for: 17 -> 18; matrix products, arithmetic and copies ran while one was open for 25% -> 24% of each run, Pallas kernels for 17% -> 16%
where the time goes in v4:
time: 350 us; the launch traced here: 349 us
  waiting for transfers between devices  120 us (34%)
  starting transfers between devices  67.4 us (19%)
  Pallas kernels  61.3 us (18%)
  local copies, waits for them, and re-layouts  43.9 us (13%)
  other arithmetic  36.3 us (10%)
  matrix products  18.3 us (5%)
    ppermute x12, waiting for transfers between devices, over_z(): return lax.ppermute(value, 'fsdp', [(i, i ^ mask) for i in range(self.n_z)])  58.6 us
    ppermute x15, waiting for transfers between devices, crossed(): return lax.ppermute(value, 'dp', pairs)  53 us
    pallas_call x6, Pallas kernels, call(): pl.pallas_call(kernel, out_shape=shapes, grid_spec=pltpu.PrefetchScalarGr...  22.8 us
    ppermute x12, starting transfers between devices, over_z(): return lax.ppermute(value, 'fsdp', [(i, i ^ mask) for i in range(self.n_z)])  22 us
    ppermute x15, starting transfers between devices, crossed(): return lax.ppermute(value, 'dp', pairs)  20.8 us
    all_to_all x3, starting transfers between devices, swap(): block = lax.all_to_all(block, AXES, split_axis=0, concat_axis=0, tiled=True)  19.7 us
    unnamed x132, local copies, waits for them, and re-layouts  14.3 us
    pallas_call x2, Pallas kernels, norm_back(): pl.pallas_call(kernel, out_shape=[jax.ShapeDtypeStruct(*s) for s in shape...  12.9 us
  transfers between devices with their start and end apart: 54, of which 18 were waited for; matrix products, arithmetic and copies ran while one was open for 24% of the time, Pallas kernels for 16%

profile of v4, /device:TPU:0, one launch (start us, length us, event | category | flops | bytes accessed | tf_op | source)
XLA Modules:
  0.0 349.0 jit_solution(985976526272553831)
XLA Ops:
  1.7 4.1 %collective-permute-start = (bf16[32,4096]{1,0:T(8,128)(2,1)S(1)}, bf16[32,4096]{1,0:T(8,128)(2,1)S(1)}, u32[]{:S(2)}, u32[]{:S(2)}) collective-permute-start(bf16[32,4096]{1,0:T(8,128)(2,1)S(1)} %pad_maximum_fusion.1), channel_id=1, source_target_pairs={{0,2},{1,3},{2,0},{3,1},{4,6},{5,7},{6,4},{7,5},{8,10},{9,11},{10,... | collective-permute-start | bytes 786440 | tf_op jit(solution)/shard_map/ppermute | solution.py:41
  23.3 13.3 %collective-permute-done.2 = bf16[64,4096]{1,0:T(8,128)(2,1)S(1)} collective-permute-done((bf16[64,4096]{1,0:T(8,128)(2,1)S(1)}, bf16[64,4096]{1,0:T(8,128)(2,1)S(1)}, u32[]{:S(2)}, u32[]{:S(2)}) %collective-permute-start.2) | collective-permute-done | bytes 524320 | tf_op jit(solution)/shard_map/ppermute | solution.py:41
  43.5 6.1 %all-to-all-start = ((bf16[32,88,128]{2,1,0:T(8,128)(2,1)}), bf16[32,88,128]{2,1,0:T(8,128)(2,1)}, u32[]{:S(2)}, u32[]{:S(2)}) async-start(bf16[32,88,128]{2,1,0:T(8,128)(2,1)} %pad_maximum_fusion), calls=%async_computation | async-start | bytes 1441792 | tf_op jit(solution)/shard_map/all_to_all | solution.py:747
  56.3 15.2 %collective-permute-done.4.refs_4_ = bf16[128,4096]{1,0:T(8,128)(2,1)} collective-permute-done((bf16[128,4096]{1,0:T(8,128)(2,1)S(1)}, bf16[128,4096]{1,0:T(8,128)(2,1)}, u32[]{:S(2)}, u32[]{:S(2)}) %collective-permute-start.4) | collective-permute-done | bytes 1048608 | tf_op jit(solution)/shard_map/ppermute | solution.py:38
  88.8 9.0 %collective-permute-done.8 = bf16[128,1024]{1,0:T(8,128)(2,1)S(1)} collective-permute-done((bf16[128,1024]{1,0:T(8,128)(2,1)S(1)}, bf16[128,1024]{1,0:T(8,128)(2,1)S(1)}, u32[]{:S(2)}, u32[]{:S(2)}) %collective-permute-start.8) | collective-permute-done | bytes 262176 | tf_op jit(solution)/shard_map/ppermute | solution.py:41
  97.8 8.2 %collective-permute-done.14.refs_2_ = bf16[128,4096]{1,0:T(8,128)(2,1)} collective-permute-done((bf16[128,4096]{1,0:T(8,128)(2,1)S(1)}, bf16[128,4096]{1,0:T(8,128)(2,1)}, u32[]{:S(2)}, u32[]{:S(2)}) %collective-permute-start.14) | collective-permute-done | bytes 1048608 | tf_op jit(solution)/shard_map/ppermute | solution.py:38
  113.4 4.2 %all-to-all-start.1 = ((bf16[32,72,128]{2,1,0:T(8,128)(2,1)}), bf16[32,72,128]{2,1,0:T(8,128)(2,1)}, u32[]{:S(2)}, u32[]{:S(2)}) async-start(bf16[32,72,128]{2,1,0:T(8,128)(2,1)} %reshape.379), calls=%async_computation.1 | async-start | bytes 1179648 | tf_op jit(solution)/shard_map/all_to_all | solution.py:747
  117.8 6.1 %collective-permute-done.12 = bf16[256,1024]{1,0:T(8,128)(2,1)} collective-permute-done((bf16[256,1024]{1,0:T(8,128)(2,1)S(1)}, bf16[256,1024]{1,0:T(8,128)(2,1)}, u32[]{:S(2)}, u32[]{:S(2)}) %collective-permute-start.12) | collective-permute-done | bytes 524320 | tf_op jit(solution)/shard_map/ppermute | solution.py:41
  138.1 3.8 %attend.1.refs_1_ = bf16[256,1024]{1,0:T(8,128)(2,1)S(1)} custom-call(s32[1]{0:T(128)} %dynamic_slice.54.first_ref, bf16[256,3072]{1,0:T(8,128)(2,1)S(1)} %fusion.4.query.key.value, bf16[256,3072]{1,0:T(8,128)(2,1)S(1)} %fusion.4.query.key.value, bf16[256,3072]{1,0:T(8,128)(2,1)S(1)} %fusion.4.query.key.value), custom_call_target="tpu_custom_call" | custom-call | tf_op jit(solution)/shard_map/attend/pallas_call | solution.py:491
  157.1 4.4 %fusion.3 = (f32[256,4096]{1,0:T(8,128)S(1)}, bf16[256,4096]{1,0:T(8,128)(2,1)S(1)}) fusion(f32[4096]{0:T(1024)S(1)} %bitcast.179, bf16[256,1024]{1,0:T(8,128)(2,1)S(1)} %get-tuple-element.281.refs_0_, bf16[1024,4096]{1,0:T(8,128)(2,1)S(1)} %assemble.4.weight), kind=kOutput, calls=%fused_computation.5 | convolution fusion | flops 2159017984 | bytes 15220736 | tf_op jit(solution)/shard_map/dot_general | solution.py:824
  164.0 5.8 %collective-permute-done.24.refs_6_ = bf16[512,1024]{1,0:T(8,128)(2,1)S(1)} collective-permute-done((bf16[512,1024]{1,0:T(8,128)(2,1)}, bf16[512,1024]{1,0:T(8,128)(2,1)S(1)}, u32[]{:S(2)}, u32[]{:S(2)}) %collective-permute-start.24) | collective-permute-done | bytes 1048608 | tf_op jit(solution)/shard_map/ppermute | solution.py:38
  178.5 3.8 %outer.7 = (bf16[512,1024]{1,0:T(8,128)(2,1)S(1)}, bf16[512,1024]{1,0:T(8,128)(2,1)S(1)}, bf16[2,512,1024]{2,1,0:T(8,128)(2,1)}) custom-call(s32[1]{0:T(128)} %bitcast.26.dp_ref, bf16[256,4096]{1,0:T(8,128)(2,1)S(1)} %get-tuple-element.324.refs_0_, bf16[256,1024]{1,0:T(8,128)(2,1)S(1)} %get-tuple-element.267.refs_1_.grad.passed_at, ...), custom_call_target="tpu_custom_call" | custom-call | tf_op jit(solution)/shard_map/outer/pallas_call | solution.py:307
  190.4 7.0 %norm_back.2 = (bf16[256,1024]{1,0:T(8,128)(2,1)S(1)}, f32[8,1024]{1,0:T(8,128)S(1)}, f32[256,1024]{1,0:T(8,128)S(1)}) custom-call(bf16[256,4096]{1,0:T(8,128)(2,1)S(1)} %copy-done.5, bf16[1024,4096]{1,0:T(8,128)(2,1)} %copy-done.3, f32[256,1024]{1,0:T(8,128)} %get-tuple-element.362.unit_at, f32[1,1024]{1,0:T(1,128)S(1)} %get-tuple-element.377.gain, ...), custom_call_target="tpu_custom_call" | custom-call | tf_op jit(solution)/shard_map/norm_back/pallas_call | solution.py:643
  198.4 5.6 %outer.9 = (bf16[128,4096]{1,0:T(8,128)(2,1)S(1)}, bf16[128,4096]{1,0:T(8,128)(2,1)S(1)}, bf16[2,128,4096]{2,1,0:T(8,128)(2,1)}) custom-call(s32[1]{0:T(128)} %bitcast.26.dp_ref, bf16[256,1024]{1,0:T(8,128)(2,1)S(1)} %get-tuple-element.281.refs_0_, bf16[256,4096]{1,0:T(8,128)(2,1)S(1)} %copy-done.6, bf16[128,4096]{1,0:T(8,128)(2,1)} %collective-permute-done.31.refs_2_, ...), custom_call_target="tpu_custom_call" | custom-call | tf_op jit(solution)/shard_map/outer/pallas_call | solution.py:307
  205.0 9.8 %attend_back.1 = (bf16[256,3072]{1,0:T(8,128)(2,1)S(1)}, f32[1,3072]{1,0:T(1,128)S(1)}) custom-call(s32[1]{0:T(128)} %dynamic_slice.54.first_ref, bf16[256,3072]{1,0:T(8,128)(2,1)S(1)} %fusion.4.query.key.value, bf16[256,3072]{1,0:T(8,128)(2,1)S(1)} %fusion.4.query.key.value, bf16[256,3072]{1,0:T(8,128)(2,1)S(1)} %fusion.4.query.key.value, ...), custom_call_target="tpu_custom_call" | custom-call | tf_op jit(solution)/shard_map/attend_back/pallas_call | solution.py:533
  223.6 5.9 %norm_back.3 = (bf16[256,1024]{1,0:T(8,128)(2,1)S(1)}, f32[8,1024]{1,0:T(8,128)S(1)}) custom-call(bf16[256,3072]{1,0:T(8,128)(2,1)S(1)} %get-tuple-element.313.refs_2_.grad, bf16[1024,3072]{1,0:T(8,128)(2,1)} %copy-done.13, f32[256,1024]{1,0:T(8,128)} %get-tuple-element.364.unit_at, f32[1,1024]{1,0:T(1,128)S(1)} %get-tuple-element.376.gain, ...), custom_call_target="tpu_custom_call" | custom-call | tf_op jit(solution)/shard_map/norm_back/pallas_call | solution.py:643
  229.6 4.4 %outer.11 = (bf16[128,4096]{1,0:T(8,128)(2,1)S(1)}, bf16[128,4096]{1,0:T(8,128)(2,1)S(1)}, bf16[2,128,4096]{2,1,0:T(8,128)(2,1)}) custom-call(s32[1]{0:T(128)} %bitcast.26.dp_ref, bf16[256,1024]{1,0:T(8,128)(2,1)S(1)} %copy-done.16, bf16[256,1024]{1,0:T(8,128)(2,1)S(1)} %copy-done.12, bf16[256,3072]{1,0:T(8,128)(2,1)S(1)} %get-tuple-element.313.refs_2_.grad, ...), custom_call_target="tpu_custom_call" | custom-call | tf_op jit(solution)/shard_map/outer/pallas_call | solution.py:307
  256.0 9.4 %all-to-all-start.2 = ((bf16[32,160,128]{2,1,0:T(8,128)(2,1)}), bf16[32,160,128]{2,1,0:T(8,128)(2,1)}, u32[]{:S(2)}, u32[]{:S(2)}) async-start(bf16[32,160,128]{2,1,0:T(8,128)(2,1)} %fusion.10), calls=%async_computation.2 | async-start | bytes 2621440 | tf_op jit(solution)/shard_map/all_to_all | solution.py:747
  270.9 15.4 %collective-permute-done.42 = bf16[2,128,4096]{2,1,0:T(8,128)(2,1)} collective-permute-done((bf16[2,128,4096]{2,1,0:T(8,128)(2,1)}, bf16[2,128,4096]{2,1,0:T(8,128)(2,1)}, u32[]{:S(2)}, u32[]{:S(2)}) %collective-permute-start.42) | collective-permute-done | bytes 2097184 | tf_op jit(solution)/shard_map/ppermute | solution.py:38
  289.4 6.3 %all-to-all-done.2 = bf16[32,160,128]{2,1,0:T(8,128)(2,1)} async-done(((bf16[32,160,128]{2,1,0:T(8,128)(2,1)}), bf16[32,160,128]{2,1,0:T(8,128)(2,1)}, u32[]{:S(2)}, u32[]{:S(2)}) %all-to-all-start.2) | async-done | bytes 1310752 | tf_op jit(solution)/shard_map/all_to_all | solution.py:747
  300.5 4.8 %collective-permute-done.44 = bf16[128,4096]{1,0:T(8,128)(2,1)} collective-permute-done((bf16[128,4096]{1,0:T(8,128)(2,1)}, bf16[128,4096]{1,0:T(8,128)(2,1)}, u32[]{:S(2)}, u32[]{:S(2)}) %collective-permute-start.44) | collective-permute-done | bytes 1048608 | tf_op jit(solution)/shard_map/ppermute | solution.py:38
  308.7 6.3 %collective-permute-start.50 = (bf16[128,1024]{1,0:T(8,128)(2,1)S(1)}, bf16[128,1024]{1,0:T(8,128)(2,1)S(1)}, u32[]{:S(2)}, u32[]{:S(2)}) collective-permute-start(bf16[128,1024]{1,0:T(8,128)(2,1)S(1)} %fusion.25), channel_id=1, source_target_pairs={{0,2},{1,3},{2,0},{3,1},{4,6},{5,7},{6,4},{7,5},{8,10},{9,11},{10,... | collective-permute-start | bytes 786440 | tf_op jit(solution)/shard_map/ppermute | solution.py:41
  316.5 10.9 %collective-permute-done.45 = bf16[2,32,4096]{2,1,0:T(8,128)(2,1)S(1)} collective-permute-done((bf16[2,32,4096]{2,1,0:T(8,128)(2,1)S(1)}, bf16[2,32,4096]{2,1,0:T(8,128)(2,1)S(1)}, u32[]{:S(2)}, u32[]{:S(2)}) %collective-permute-start.45) | collective-permute-done | bytes 524320 | tf_op jit(solution)/shard_map/ppermute | solution.py:41
  329.9 14.3 %collective-permute-done.49 = bf16[32,4096]{1,0:T(8,128)(2,1)S(1)} collective-permute-done((bf16[32,4096]{1,0:T(8,128)(2,1)S(1)}, bf16[32,4096]{1,0:T(8,128)(2,1)S(1)}, u32[]{:S(2)}, u32[]{:S(2)}) %collective-permute-start.49) | collective-permute-done | bytes 262176 | tf_op jit(solution)/shard_map/ppermute | solution.py:41
  (348 shorter events, 162.8 us)
Async XLA Ops:
  43.5 30.0 %all-to-all-start = ((bf16[32,88,128]{2,1,0:T(8,128)(2,1)}), bf16[32,88,128]{2,1,0:T(8,128)(2,1)}, u32[]{:S(2)}, u32[]{:S(2)}) async-start(bf16[32,88,128]{2,1,0:T(8,128)(2,1)} %pad_maximum_fusion), calls=%async_computation | async-start | bytes 1441792 | tf_op jit(solution)/shard_map/all_to_all | solution.py:747
  49.6 21.9 %collective-permute-start.4 = (bf16[128,4096]{1,0:T(8,128)(2,1)S(1)}, bf16[128,4096]{1,0:T(8,128)(2,1)}, u32[]{:S(2)}, u32[]{:S(2)}) collective-permute-start(bf16[128,4096]{1,0:T(8,128)(2,1)S(1)} %constant_dynamic-update-slice_fusion.2.refs_0_), channel_id=1, source_target_pairs={{0,16},{4,12},{8,24},{12,4},{16,0},{20,28},{24,8},{28,20},{1,17},{... | collective-permute-start | bytes 3145736 | tf_op jit(solution)/shard_map/ppermute | solution.py:38
  52.5 26.0 %collective-permute-start.3 = (bf16[64,4096]{1,0:T(8,128)(2,1)}, bf16[64,4096]{1,0:T(8,128)(2,1)}, u32[]{:S(2)}, u32[]{:S(2)}) collective-permute-start(bf16[64,4096]{1,0:T(8,128)(2,1)} %constant_dynamic-update-slice_fusion.4), channel_id=1, source_target_pairs={{0,1},{1,0},{2,3},{3,2},{4,5},{5,4},{6,7},{7,6},{8,9},{9,8},{10,11... | collective-permute-start | bytes 1572872 | tf_op jit(solution)/shard_map/ppermute | solution.py:41
  55.0 28.0 %collective-permute-start.9 = (bf16[128,4096]{1,0:T(8,128)(2,1)S(1)}, bf16[128,4096]{1,0:T(8,128)(2,1)}, u32[]{:S(2)}, u32[]{:S(2)}) collective-permute-start(bf16[128,4096]{1,0:T(8,128)(2,1)S(1)} %collective-permute-done.5.refs_2_), channel_id=1, source_target_pairs={{0,16},{4,12},{8,24},{12,4},{16,0},{20,28},{24,8},{28,20},{1,17},{... | collective-permute-start | bytes 3145736 | tf_op jit(solution)/shard_map/ppermute | solution.py:38
  80.7 25.3 %collective-permute-start.14 = (bf16[128,4096]{1,0:T(8,128)(2,1)S(1)}, bf16[128,4096]{1,0:T(8,128)(2,1)}, u32[]{:S(2)}, u32[]{:S(2)}) collective-permute-start(bf16[128,4096]{1,0:T(8,128)(2,1)S(1)} %constant_dynamic-update-slice_fusion.6.refs_0_), channel_id=1, source_target_pairs={{0,8},{4,20},{8,0},{12,28},{16,24},{20,4},{24,16},{28,12},{1,9},{5... | collective-permute-start | bytes 3145736 | tf_op jit(solution)/shard_map/ppermute | solution.py:38
  82.2 23.9 %collective-permute-start.15 = (bf16[128,4096]{1,0:T(8,128)(2,1)S(1)}, bf16[128,4096]{1,0:T(8,128)(2,1)S(1)}, u32[]{:S(2)}, u32[]{:S(2)}) collective-permute-start(bf16[128,4096]{1,0:T(8,128)(2,1)S(1)} %constant_dynamic-update-slice_fusion.6.refs_0_), channel_id=1, source_target_pairs={{0,4},{4,0},{8,12},{12,8},{16,20},{20,16},{24,28},{28,24},{1,5},{5... | collective-permute-start | bytes 3145736 | tf_op jit(solution)/shard_map/ppermute | solution.py:34
  82.2 35.5 %collective-permute-start.13 = (bf16[128,4096]{1,0:T(8,128)(2,1)S(1)}, bf16[128,4096]{1,0:T(8,128)(2,1)}, u32[]{:S(2)}, u32[]{:S(2)}) collective-permute-start(bf16[128,4096]{1,0:T(8,128)(2,1)S(1)} %constant_dynamic-update-slice_fusion.6.refs_0_), channel_id=1, source_target_pairs={{0,16},{4,12},{8,24},{12,4},{16,0},{20,28},{24,8},{28,20},{1,17},{... | collective-permute-start | bytes 3145736 | tf_op jit(solution)/shard_map/ppermute | solution.py:38
  107.1 22.5 %collective-permute-start.11 = (bf16[128,4096]{1,0:T(8,128)(2,1)}, bf16[128,4096]{1,0:T(8,128)(2,1)}, u32[]{:S(2)}, u32[]{:S(2)}) collective-permute-start(bf16[128,4096]{1,0:T(8,128)(2,1)} %collective-permute-done.9.refs_6_), channel_id=1, source_target_pairs={{0,4},{4,0},{8,12},{12,8},{16,20},{20,16},{24,28},{28,24},{1,5},{5... | collective-permute-start | bytes 3145736 | tf_op jit(solution)/shard_map/ppermute | solution.py:34
  111.2 34.7 %collective-permute-start.19 = (bf16[128,4096]{1,0:T(8,128)(2,1)}, bf16[128,4096]{1,0:T(8,128)(2,1)}, u32[]{:S(2)}, u32[]{:S(2)}) collective-permute-start(bf16[128,4096]{1,0:T(8,128)(2,1)} %collective-permute-done.14.refs_2_), channel_id=1, source_target_pairs={{0,16},{4,12},{8,24},{12,4},{16,0},{20,28},{24,8},{28,20},{1,17},{... | collective-permute-start | bytes 3145736 | tf_op jit(solution)/shard_map/ppermute | solution.py:38
  113.4 28.6 %all-to-all-start.1 = ((bf16[32,72,128]{2,1,0:T(8,128)(2,1)}), bf16[32,72,128]{2,1,0:T(8,128)(2,1)}, u32[]{:S(2)}, u32[]{:S(2)}) async-start(bf16[32,72,128]{2,1,0:T(8,128)(2,1)} %reshape.379), calls=%async_computation.1 | async-start | bytes 1179648 | tf_op jit(solution)/shard_map/all_to_all | solution.py:747
  117.7 28.2 %collective-permute-start.20 = (bf16[128,4096]{1,0:T(8,128)(2,1)}, bf16[128,4096]{1,0:T(8,128)(2,1)}, u32[]{:S(2)}, u32[]{:S(2)}) collective-permute-start(bf16[128,4096]{1,0:T(8,128)(2,1)} %collective-permute-done.13.refs_4_), channel_id=1, source_target_pairs={{0,4},{4,0},{8,12},{12,8},{16,20},{20,16},{24,28},{28,24},{1,5},{5... | collective-permute-start | bytes 3145736 | tf_op jit(solution)/shard_map/ppermute | solution.py:34
  126.6 27.2 %collective-permute-start.17 = (bf16[512,1024]{1,0:T(8,128)(2,1)}, bf16[512,1024]{1,0:T(8,128)(2,1)}, u32[]{:S(2)}, u32[]{:S(2)}) collective-permute-start(bf16[512,1024]{1,0:T(8,128)(2,1)} %constant_dynamic-update-slice_fusion.10.refs_0_), channel_id=1, source_target_pairs={{0,8},{4,20},{8,0},{12,28},{16,24},{20,4},{24,16},{28,12},{1,9},{5... | collective-permute-start | bytes 3145736 | tf_op jit(solution)/shard_map/ppermute | solution.py:38
  129.6 24.2 %collective-permute-start.18 = (bf16[512,1024]{1,0:T(8,128)(2,1)}, bf16[512,1024]{1,0:T(8,128)(2,1)}, u32[]{:S(2)}, u32[]{:S(2)}) collective-permute-start(bf16[512,1024]{1,0:T(8,128)(2,1)} %constant_dynamic-update-slice_fusion.10.refs_0_), channel_id=1, source_target_pairs={{0,4},{4,0},{8,12},{12,8},{16,20},{20,16},{24,28},{28,24},{1,5},{5... | collective-permute-start | bytes 3145736 | tf_op jit(solution)/shard_map/ppermute | solution.py:34
  129.6 27.2 %collective-permute-start.22 = (bf16[512,1024]{1,0:T(8,128)(2,1)}, bf16[512,1024]{1,0:T(8,128)(2,1)}, u32[]{:S(2)}, u32[]{:S(2)}) collective-permute-start(bf16[512,1024]{1,0:T(8,128)(2,1)} %constant_dynamic-update-slice_fusion.10.refs_0_), channel_id=1, source_target_pairs={{0,16},{4,12},{8,24},{12,4},{16,0},{20,28},{24,8},{28,20},{1,17},{... | collective-permute-start | bytes 3145736 | tf_op jit(solution)/shard_map/ppermute | solution.py:38
  182.3 32.6 %collective-permute-start.35 = (bf16[2,512,1024]{2,1,0:T(8,128)(2,1)}, bf16[2,512,1024]{2,1,0:T(8,128)(2,1)}, u32[]{:S(2)}, u32[]{:S(2)}) collective-permute-start(bf16[2,512,1024]{2,1,0:T(8,128)(2,1)} %get-tuple-element.272), channel_id=1, source_target_pairs={{0,16},{4,12},{8,24},{12,4},{16,0},{20,28},{24,8},{28,20},{1,17},{... | collective-permute-start | bytes 6291464 | tf_op jit(solution)/shard_map/ppermute | solution.py:38
  204.0 33.1 %collective-permute-start.37 = (bf16[2,128,4096]{2,1,0:T(8,128)(2,1)}, bf16[2,128,4096]{2,1,0:T(8,128)(2,1)}, u32[]{:S(2)}, u32[]{:S(2)}) collective-permute-start(bf16[2,128,4096]{2,1,0:T(8,128)(2,1)} %get-tuple-element.287), channel_id=1, source_target_pairs={{0,16},{4,12},{8,24},{12,4},{16,0},{20,28},{24,8},{28,20},{1,17},{... | collective-permute-start | bytes 6291464 | tf_op jit(solution)/shard_map/ppermute | solution.py:38
  222.0 21.9 %collective-permute-start.36 = (bf16[512,1024]{1,0:T(8,128)(2,1)}, bf16[512,1024]{1,0:T(8,128)(2,1)}, u32[]{:S(2)}, u32[]{:S(2)}) collective-permute-start(bf16[512,1024]{1,0:T(8,128)(2,1)} %fusion.8), channel_id=1, source_target_pairs={{0,8},{4,20},{8,0},{12,28},{16,24},{20,4},{24,16},{28,12},{1,9},{5... | collective-permute-start | bytes 3145736 | tf_op jit(solution)/shard_map/ppermute | solution.py:38
  235.9 50.4 %collective-permute-start.42 = (bf16[2,128,4096]{2,1,0:T(8,128)(2,1)}, bf16[2,128,4096]{2,1,0:T(8,128)(2,1)}, u32[]{:S(2)}, u32[]{:S(2)}) collective-permute-start(bf16[2,128,4096]{2,1,0:T(8,128)(2,1)} %get-tuple-element.319), channel_id=1, source_target_pairs={{0,16},{4,12},{8,24},{12,4},{16,0},{20,28},{24,8},{28,20},{1,17},{... | collective-permute-start | bytes 6291464 | tf_op jit(solution)/shard_map/ppermute | solution.py:38
  239.7 26.8 %collective-permute-start.43 = (bf16[128,4096]{1,0:T(8,128)(2,1)}, bf16[128,4096]{1,0:T(8,128)(2,1)}, u32[]{:S(2)}, u32[]{:S(2)}) collective-permute-start(bf16[128,4096]{1,0:T(8,128)(2,1)} %fusion.7), channel_id=1, source_target_pairs={{0,8},{4,20},{8,0},{12,28},{16,24},{20,4},{24,16},{28,12},{1,9},{5... | collective-permute-start | bytes 3145736 | tf_op jit(solution)/shard_map/ppermute | solution.py:38
  248.4 59.0 %collective-permute-start.47 = (bf16[2,128,1024]{2,1,0:T(8,128)(2,1)}, bf16[2,128,1024]{2,1,0:T(8,128)(2,1)}, u32[]{:S(2)}, u32[]{:S(2)}) collective-permute-start(bf16[2,128,1024]{2,1,0:T(8,128)(2,1)} %fusion.18), channel_id=1, source_target_pairs={{0,1},{1,0},{2,3},{3,2},{4,5},{5,4},{6,7},{7,6},{8,9},{9,8},{10,11... | collective-permute-start | bytes 1572872 | tf_op jit(solution)/shard_map/ppermute | solution.py:41
  256.0 39.7 %all-to-all-start.2 = ((bf16[32,160,128]{2,1,0:T(8,128)(2,1)}), bf16[32,160,128]{2,1,0:T(8,128)(2,1)}, u32[]{:S(2)}, u32[]{:S(2)}) async-start(bf16[32,160,128]{2,1,0:T(8,128)(2,1)} %fusion.10), calls=%async_computation.2 | async-start | bytes 2621440 | tf_op jit(solution)/shard_map/all_to_all | solution.py:747
  269.5 45.6 %collective-permute-start.46 = (bf16[2,32,4096]{2,1,0:T(8,128)(2,1)}, bf16[2,32,4096]{2,1,0:T(8,128)(2,1)}, u32[]{:S(2)}, u32[]{:S(2)}) collective-permute-start(bf16[2,32,4096]{2,1,0:T(8,128)(2,1)} %fusion.19), channel_id=1, source_target_pairs={{0,1},{1,0},{2,3},{3,2},{4,5},{5,4},{6,7},{7,6},{8,9},{9,8},{10,11... | collective-permute-start | bytes 1572872 | tf_op jit(solution)/shard_map/ppermute | solution.py:41
  308.7 20.3 %collective-permute-start.50 = (bf16[128,1024]{1,0:T(8,128)(2,1)S(1)}, bf16[128,1024]{1,0:T(8,128)(2,1)S(1)}, u32[]{:S(2)}, u32[]{:S(2)}) collective-permute-start(bf16[128,1024]{1,0:T(8,128)(2,1)S(1)} %fusion.25), channel_id=1, source_target_pairs={{0,2},{1,3},{2,0},{3,1},{4,6},{5,7},{6,4},{7,5},{8,10},{9,11},{10,... | collective-permute-start | bytes 786440 | tf_op jit(solution)/shard_map/ppermute | solution.py:41
  316.4 27.9 %collective-permute-start.49 = (bf16[32,4096]{1,0:T(8,128)(2,1)S(1)}, bf16[32,4096]{1,0:T(8,128)(2,1)S(1)}, u32[]{:S(2)}, u32[]{:S(2)}) collective-permute-start(bf16[32,4096]{1,0:T(8,128)(2,1)S(1)} %fusion.26), channel_id=1, source_target_pairs={{0,2},{1,3},{2,0},{3,1},{4,6},{5,7},{6,4},{7,5},{8,10},{9,11},{10,... | collective-permute-start | bytes 786440 | tf_op jit(solution)/shard_map/ppermute | solution.py:41
  (89 other events, 933.0 us)
